TPU v7x, 128 devices: a whole 4x4x4 slice. The times are simulated.
128 devices in a mesh: gx: 32 (over z, x, core), gy: 4 (over y).
Axes of the slice: x: 4, y: 4, z: 4, core: 2. Of those that a mesh axis runs over, the one named last changes fastest.
Arguments:
- forcing: float32 [6, 2, 4096, 512], P(None, None, 'gx', 'gy'), may hold values from -3 to 3
- gap_cubed: float32 [4096, 512], P('gx', 'gy'), may hold values from 0.5 to 2
- hole_mask: int32 [4096, 512], P('gx', 'gy'), may hold values 0 or 1
- coarse_bases: float32 [40, 4096, 512], P(None, 'gx', 'gy'), may hold values from -12 to 12
- basis_counts: int32 [32, 4], P('gx', 'gy'), may hold values from 8 to 40, as said below
Outputs:
- solution: float32 [6, 2, 4096, 512], P(None, None, 'gx', 'gy')
Inputs may be any that keep to these rules, and one draw needn't show every extreme that they name: `basis_counts`: each tile uses the first of its 40 stored bases, at least 8 of them; some tile uses all 40 and some tile exactly 8.
All inputs are finite; a program needn't handle non-finite values. No bound on the sum of `hole_mask` on one device may be relied on, other than what follows from the above.
Results may differ from a plain program's by a relative error of at most 0.0003.
Values sent between devices are 32-bit elements; how exact they have to be, the bound alone decides.
A program may use at most 128 MiB of HBM per device.

v0:
```python
import jax
import jax.numpy as jnp
from jax import lax
from jax.sharding import PartitionSpec as P

MARGIN = 16
SWEEPS = 20
CSTEPS = 7
ITERS = 2


squeeze_number = 0.2
vent_gain = 4.0
relaxation = 0.8
guard_value = 1e-12
highest = lax.Precision.HIGHEST


def padded_2(cells, sides, width):
    for axis, dim in sides:
        count = lax.axis_size(axis)
        head = lax.slice_in_dim(cells, 0, width, axis=dim)
        tail = lax.slice_in_dim(cells, cells.shape[dim] - width, cells.shape[dim], axis=dim)
        cells = jnp.concatenate(
            [
                lax.ppermute(tail, axis, [(i, (i + 1) % count) for i in range(count)]),
                cells,
                lax.ppermute(head, axis, [((i + 1) % count, i) for i in range(count)]),
            ],
            axis=dim,
        )
    return cells


def edge_terms(gap_padded):
    centre = gap_padded[1:-1, 1:-1]
    north_edge = 0.5 * (centre + gap_padded[2:, 1:-1])
    south_edge = 0.5 * (centre + gap_padded[:-2, 1:-1])
    east_edge = 0.5 * (centre + gap_padded[1:-1, 2:])
    west_edge = 0.5 * (centre + gap_padded[1:-1, :-2])
    return (north_edge, south_edge, east_edge, west_edge)


def diagonal_of(edge_set, vent_term):
    return edge_set[0] + edge_set[1] + edge_set[2] + edge_set[3] + vent_term


def apply_operator(padded, edge_set, diagonal):
    north_edge, south_edge, east_edge, west_edge = edge_set
    centre = padded[:, :, 1:-1, 1:-1]
    beside_all = (
        north_edge * padded[:, :, 2:, 1:-1]
        + south_edge * padded[:, :, :-2, 1:-1]
        + east_edge * padded[:, :, 1:-1, 2:]
        + west_edge * padded[:, :, 1:-1, :-2]
    )
    turned = jnp.stack([-centre[:, 1], centre[:, 0]], axis=1)
    return diagonal * centre - beside_all + squeeze_number * turned


def local_solve(residual, edge_set, diagonal, inside):
    real_diag = jnp.where(inside > 0, diagonal, 1.0)
    step_scale = relaxation * inside / (real_diag * real_diag + squeeze_number * squeeze_number)

    def sweep(sweep_index, iterate):
        padded = jnp.pad(iterate, ((0, 0), (0, 0), (1, 1), (1, 1)))
        defect = residual - apply_operator(padded, edge_set, diagonal)
        update_real = real_diag * defect[:, 0] + squeeze_number * defect[:, 1]
        update_imag = real_diag * defect[:, 1] - squeeze_number * defect[:, 0]
        return iterate + step_scale * jnp.stack([update_real, update_imag], axis=1)

    return lax.fori_loop(0, SWEEPS, sweep, jnp.zeros_like(residual))


def complex_scale(alpha_real, alpha_imag, vectors):
    return jnp.stack(
        [
            alpha_real * vectors[..., 0] - alpha_imag * vectors[..., 1],
            alpha_real * vectors[..., 1] + alpha_imag * vectors[..., 0],
        ],
        axis=-1,
    )


def plate_columns(width, tile_cols):
    first_col = lax.axis_index("gy") * tile_cols - width
    col_ids = first_col + jnp.arange(tile_cols + 2 * width, dtype=jnp.int32)
    return ((col_ids >= 0) & (col_ids < tile_cols * lax.axis_size("gy"))).astype(jnp.float32)


def body(forcing, gap_cubed, hole_mask, coarse_bases, basis_counts):
    mode_count = forcing.shape[0]
    tile_rows, tile_cols = gap_cubed.shape
    basis_total = coarse_bases.shape[0]
    deep_width = MARGIN + 1
    wide_rows = tile_rows + 2 * MARGIN
    wide_cols = tile_cols + 2 * MARGIN
    vent_term = vent_gain * hole_mask.astype(jnp.float32) * gap_cubed
    start_stack = jnp.concatenate(
        [gap_cubed[None], vent_term[None], forcing.reshape(2 * mode_count, tile_rows, tile_cols)],
        axis=0,
    )
    grown_stack = padded_2(start_stack, (("gx", 1), ("gy", 2)), deep_width)
    grown_stack = grown_stack * plate_columns(deep_width, tile_cols)
    gap_deep = grown_stack[0]
    vent_wide = grown_stack[1, 1:-1, 1:-1]
    force_wide = grown_stack[2:, 1:-1, 1:-1].reshape(mode_count, 2, wide_rows, wide_cols)
    inside = jnp.broadcast_to(plate_columns(MARGIN, tile_cols)[None, :], (wide_rows, wide_cols))
    wide_edges = edge_terms(gap_deep)
    wide_diag = diagonal_of(wide_edges, vent_wide)
    owned_edges = edge_terms(gap_deep[MARGIN:-MARGIN, MARGIN:-MARGIN])
    owned_diag = diagonal_of(owned_edges, vent_term)
    unit_mask = plate_columns(1, tile_cols)
    active = (jnp.arange(basis_total, dtype=jnp.int32) < basis_counts[0, 0]).astype(jnp.float32)
    base_field = coarse_bases * active[:, None, None]
    flat_bases = base_field.reshape(basis_total, tile_rows * tile_cols)

    def restrict(pressure):
        flat_field = pressure.reshape(2 * mode_count, tile_rows * tile_cols)
        product = lax.dot_general(
            flat_bases,
            flat_field,
            (((1,), (1,)), ((), ())),
            precision=highest,
            preferred_element_type=jnp.float32,
        )
        return product.reshape(basis_total, mode_count, 2)

    def prolong(coarse):
        product = lax.dot_general(
            coarse.reshape(basis_total, 2 * mode_count),
            flat_bases,
            (((0,), (0,)), ((), ())),
            precision=highest,
            preferred_element_type=jnp.float32,
        )
        return product.reshape(mode_count, 2, tile_rows, tile_cols)

    solution = jnp.zeros_like(forcing)
    residual_wide = force_wide
    for outer_step in range(ITERS):
        if outer_step > 0:
            padded = padded_2(solution, (("gx", 2), ("gy", 3)), 1) * unit_mask
            owned_resid = forcing - apply_operator(padded, owned_edges, owned_diag)
            residual_wide = padded_2(owned_resid, (("gx", 2), ("gy", 3)), MARGIN)
            residual_wide = residual_wide * plate_columns(MARGIN, tile_cols)
        residual = residual_wide[:, :, MARGIN:-MARGIN, MARGIN:-MARGIN]
        local_part = local_solve(residual_wide, wide_edges, wide_diag, inside)[
            :, :, MARGIN:-MARGIN, MARGIN:-MARGIN
        ]
        search = restrict(residual)
        coarse = jnp.zeros_like(search)
        for coarse_step in range(CSTEPS):
            coarse_padded = padded_2(prolong(search), (("gx", 2), ("gy", 3)), 1) * unit_mask
            images = restrict(apply_operator(coarse_padded, owned_edges, owned_diag))
            num_real = jnp.sum(
                images[..., 0] * search[..., 0] + images[..., 1] * search[..., 1], axis=0
            )
            num_imag = jnp.sum(
                images[..., 0] * search[..., 1] - images[..., 1] * search[..., 0], axis=0
            )
            squares = jnp.sum(images * images, axis=(0, 2))
            num_real, num_imag, squares = lax.psum((num_real, num_imag, squares), ("gx", "gy"))
            denominator = squares + guard_value
            alpha_real = num_real / denominator
            alpha_imag = num_imag / denominator
            coarse = coarse + complex_scale(alpha_real, alpha_imag, search)
            search = search - complex_scale(alpha_real, alpha_imag, images)
        solution = solution + local_part + prolong(coarse)
    return solution


def solution(mesh):
    placed = (
        P(None, None, "gx", "gy"),
        P("gx", "gy"),
        P("gx", "gy"),
        P(None, "gx", "gy"),
        P("gx", "gy"),
    )
    return jax.shard_map(
        body, mesh=mesh, in_specs=placed, out_specs=P(None, None, "gx", "gy"), check_vma=False
    )
```

profile of v0, /device:TPU:16, one launch (start us, length us, event | category | flops | bytes accessed | tf_op | source)
XLA Modules:
  0.0 1812.8 jit_solution(3201429061828324834)
XLA Ops:
  2.7 5.7 collective-permute-start.1
  36.0 3.4 fusion.10
  42.6 5.1 collective-permute-start.5
  64.5 4.0 multiply_reduce_fusion.13
  68.7 64.7 %all-reduce.15 = (f32[6]{0:T(128)S(1)}, f32[6]{0:T(128)S(1)}, f32[6]{0:T(128)S(1)}) all-reduce(f32[6]{0:T(128)S(1)} %get-tuple-element.400, f32[6]{0:T(128)S(1)} %get-tuple-element.728, f32[6]{0:T(128)S(1)} %get-tuple-element.399), channel_id=1, replica_groups=mesh['gx'=32,'gy'=4] {'gx','gy'}, use_global_device_ids=true, to_apply=%region_7.8 | all-reduce | flops 18 | bytes 144 | tf_op jit(solution)/shard_map/psum | solution.py:163
  136.7 5.2 collective-permute-start.9
  158.4 4.0 multiply_reduce_fusion.12
  162.6 66.1 %all-reduce.14 = (f32[6]{0:T(128)S(1)}, f32[6]{0:T(128)S(1)}, f32[6]{0:T(128)S(1)}) all-reduce(f32[6]{0:T(128)S(1)} %get-tuple-element.398, f32[6]{0:T(128)S(1)} %get-tuple-element.730, f32[6]{0:T(128)S(1)} %get-tuple-element.397), channel_id=1, replica_groups=mesh['gx'=32,'gy'=4] {'gx','gy'}, use_global_device_ids=true, to_apply=%region_13.14 | all-reduce | flops 18 | bytes 144 | tf_op jit(solution)/shard_map/psum | solution.py:163
  232.4 5.1 collective-permute-start.13
  253.6 4.0 multiply_reduce_fusion.11
  257.8 66.6 %all-reduce.13 = (f32[6]{0:T(128)S(1)}, f32[6]{0:T(128)S(1)}, f32[6]{0:T(128)S(1)}) all-reduce(f32[6]{0:T(128)S(1)} %get-tuple-element.396, f32[6]{0:T(128)S(1)} %get-tuple-element.732, f32[6]{0:T(128)S(1)} %get-tuple-element.395), channel_id=1, replica_groups=mesh['gx'=32,'gy'=4] {'gx','gy'}, use_global_device_ids=true, to_apply=%region_19.20 | all-reduce | flops 18 | bytes 144 | tf_op jit(solution)/shard_map/psum | solution.py:163
  328.3 5.1 collective-permute-start.17
  349.7 4.0 multiply_reduce_fusion.10
  353.9 66.4 %all-reduce.12 = (f32[6]{0:T(128)S(1)}, f32[6]{0:T(128)S(1)}, f32[6]{0:T(128)S(1)}) all-reduce(f32[6]{0:T(128)S(1)} %get-tuple-element.394, f32[6]{0:T(128)S(1)} %get-tuple-element.734, f32[6]{0:T(128)S(1)} %get-tuple-element.393), channel_id=1, replica_groups=mesh['gx'=32,'gy'=4] {'gx','gy'}, use_global_device_ids=true, to_apply=%region_25.26 | all-reduce | flops 18 | bytes 144 | tf_op jit(solution)/shard_map/psum | solution.py:163
  425.2 5.1 collective-permute-start.21
  448.1 4.0 multiply_reduce_fusion.9
  452.3 66.3 %all-reduce.11 = (f32[6]{0:T(128)S(1)}, f32[6]{0:T(128)S(1)}, f32[6]{0:T(128)S(1)}) all-reduce(f32[6]{0:T(128)S(1)} %get-tuple-element.392, f32[6]{0:T(128)S(1)} %get-tuple-element.736, f32[6]{0:T(128)S(1)} %get-tuple-element.391), channel_id=1, replica_groups=mesh['gx'=32,'gy'=4] {'gx','gy'}, use_global_device_ids=true, to_apply=%region_31.32 | all-reduce | flops 18 | bytes 144 | tf_op jit(solution)/shard_map/psum | solution.py:163
  523.3 5.2 collective-permute-start.25
  548.6 4.0 multiply_reduce_fusion.8
  552.8 65.7 %all-reduce.10 = (f32[6]{0:T(128)S(1)}, f32[6]{0:T(128)S(1)}, f32[6]{0:T(128)S(1)}) all-reduce(f32[6]{0:T(128)S(1)} %get-tuple-element.390, f32[6]{0:T(128)S(1)} %get-tuple-element.738, f32[6]{0:T(128)S(1)} %get-tuple-element.389), channel_id=1, replica_groups=mesh['gx'=32,'gy'=4] {'gx','gy'}, use_global_device_ids=true, to_apply=%region_37.38 | all-reduce | flops 18 | bytes 144 | tf_op jit(solution)/shard_map/psum | solution.py:163
  622.6 4.8 collective-permute-start.29
  637.7 161.1 %while.26 = (s32[]{:T(128)}, f32[6,2,160,160]{3,2,1,0:T(8,128)}, f32[160,160]{1,0:T(8,128)S(1)}, f32[160,160]{1,0:T(8,128)S(1)}, f32[160,160]{1,0:T(8,128)S(1)},...) while((s32[]{:T(128)}, f32[6,2,160,160]{3,2,1,0:T(8,128)}, ...), condition=%wide.region_1.2_spmd.clone, body=%wide.region_0.1_spmd.clone.sunk | while | flops 6604803 | bytes 22425812 | solution.py:72
  798.8 4.2 copy.295
  809.6 4.6 multiply_reduce_fusion.7
  814.9 66.2 %all-reduce.9 = (f32[6]{0:T(128)}, f32[6]{0:T(128)}, f32[6]{0:T(128)}) all-reduce(f32[6]{0:T(128)} %get-tuple-element.388, f32[6]{0:T(128)} %get-tuple-element.740, f32[6]{0:T(128)} %get-tuple-element.387), channel_id=1, replica_groups=mesh['gx'=32,'gy'=4] {'gx','gy'}, use_global_device_ids=true, to_apply=%region_43.44 | all-reduce | flops 18 | bytes 144 | tf_op jit(solution)/shard_map/psum | solution.py:163
  882.7 4.9 fusion.58
  887.7 5.1 collective-permute-start.33
  912.7 5.1 collective-permute-start.37
  926.2 3.4 collective-permute-start.38
  945.8 3.4 fusion.8
  952.4 5.1 collective-permute-start.41
  976.4 4.6 multiply_reduce_fusion.6
  981.7 64.6 %all-reduce.8 = (f32[6]{0:T(128)S(1)}, f32[6]{0:T(128)S(1)}, f32[6]{0:T(128)S(1)}) all-reduce(f32[6]{0:T(128)} %get-tuple-element.386, f32[6]{0:T(128)} %get-tuple-element.742, f32[6]{0:T(128)} %get-tuple-element.385), channel_id=1, replica_groups=mesh['gx'=32,'gy'=4] {'gx','gy'}, use_global_device_ids=true, to_apply=%region_51.52 | all-reduce | flops 18 | bytes 144 | tf_op jit(solution)/shard_map/psum | solution.py:163
  1050.1 5.2 collective-permute-start.45
  1073.9 4.6 multiply_reduce_fusion.5
  1078.6 66.3 %all-reduce.7 = (f32[6]{0:T(128)S(1)}, f32[6]{0:T(128)S(1)}, f32[6]{0:T(128)}) all-reduce(f32[6]{0:T(128)S(1)} %get-tuple-element.384, f32[6]{0:T(128)} %get-tuple-element.744, f32[6]{0:T(128)S(1)} %get-tuple-element.383), channel_id=1, replica_groups=mesh['gx'=32,'gy'=4] {'gx','gy'}, use_global_device_ids=true, to_apply=%region_57.58 | all-reduce | flops 18 | bytes 144 | tf_op jit(solution)/shard_map/psum | solution.py:163
  1149.6 5.1 collective-permute-start.49
  1173.1 4.6 multiply_reduce_fusion.4
  1177.8 66.7 %all-reduce.6 = (f32[6]{0:T(128)S(1)}, f32[6]{0:T(128)S(1)}, f32[6]{0:T(128)}) all-reduce(f32[6]{0:T(128)S(1)} %get-tuple-element.382, f32[6]{0:T(128)} %get-tuple-element.746, f32[6]{0:T(128)S(1)} %get-tuple-element.381), channel_id=1, replica_groups=mesh['gx'=32,'gy'=4] {'gx','gy'}, use_global_device_ids=true, to_apply=%region_63.64 | all-reduce | flops 18 | bytes 144 | tf_op jit(solution)/shard_map/psum | solution.py:163
  1249.0 5.1 collective-permute-start.53
  1272.7 4.6 multiply_reduce_fusion.3
  1277.4 66.3 %all-reduce.5 = (f32[6]{0:T(128)S(1)}, f32[6]{0:T(128)S(1)}, f32[6]{0:T(128)}) all-reduce(f32[6]{0:T(128)S(1)} %get-tuple-element.380, f32[6]{0:T(128)} %get-tuple-element.748, f32[6]{0:T(128)S(1)} %get-tuple-element.379), channel_id=1, replica_groups=mesh['gx'=32,'gy'=4] {'gx','gy'}, use_global_device_ids=true, to_apply=%region_69.70 | all-reduce | flops 18 | bytes 144 | tf_op jit(solution)/shard_map/psum | solution.py:163
  1348.2 5.1 collective-permute-start.57
  1372.1 4.6 multiply_reduce_fusion.2
  1376.8 66.3 %all-reduce.4 = (f32[6]{0:T(128)S(1)}, f32[6]{0:T(128)S(1)}, f32[6]{0:T(128)}) all-reduce(f32[6]{0:T(128)S(1)} %get-tuple-element.378, f32[6]{0:T(128)} %get-tuple-element.750, f32[6]{0:T(128)S(1)} %get-tuple-element.377), channel_id=1, replica_groups=mesh['gx'=32,'gy'=4] {'gx','gy'}, use_global_device_ids=true, to_apply=%region_75.76 | all-reduce | flops 18 | bytes 144 | tf_op jit(solution)/shard_map/psum | solution.py:163
  1447.5 5.2 collective-permute-start.61
  1471.2 4.6 multiply_reduce_fusion.1
  1475.9 66.3 %all-reduce.3 = (f32[6]{0:T(128)S(1)}, f32[6]{0:T(128)S(1)}, f32[6]{0:T(128)}) all-reduce(f32[6]{0:T(128)S(1)} %get-tuple-element.376, f32[6]{0:T(128)} %get-tuple-element.752, f32[6]{0:T(128)S(1)} %get-tuple-element.375), channel_id=1, replica_groups=mesh['gx'=32,'gy'=4] {'gx','gy'}, use_global_device_ids=true, to_apply=%region_81.82 | all-reduce | flops 18 | bytes 144 | tf_op jit(solution)/shard_map/psum | solution.py:163
  1547.6 5.1 collective-permute-start.65
  1552.7 3.8 copy.366
  1564.5 161.5 %while.27 = (s32[]{:T(128)}, f32[6,2,160,160]{3,2,1,0:T(8,128)}, f32[160,160]{1,0:T(8,128)S(1)}, f32[160,160]{1,0:T(8,128)S(1)}, f32[160,160]{1,0:T(8,128)S(1)},...) while((s32[]{:T(128)}, f32[6,2,160,160]{3,2,1,0:T(8,128)}, ...), condition=%wide.region_45.46_spmd.clone, body=%wide.region_44.45_spmd.clone.sunk | while | flops 6604803 | bytes 22425812 | solution.py:72
  1574.7 3.2 fusion.488
  1582.9 3.2 fusion.488
  1591.1 3.2 fusion.488
  1599.3 3.2 fusion.488
  1607.6 3.2 fusion.488
  1615.8 3.2 fusion.488
  1665.2 3.2 fusion.488
  1706.3 3.2 fusion.488
  1722.7 3.2 fusion.488
  1726.0 4.2 copy.367
  1738.3 4.0 multiply_reduce_fusion
  1742.4 63.5 %all-reduce.2 = (f32[6]{0:T(128)S(1)}, f32[6]{0:T(128)S(1)}, f32[6]{0:T(128)S(1)}) all-reduce(f32[6]{0:T(128)S(1)} %get-tuple-element.374, f32[6]{0:T(128)S(1)} %get-tuple-element.754, f32[6]{0:T(128)S(1)} %get-tuple-element.373), channel_id=1, replica_groups=mesh['gx'=32,'gy'=4] {'gx','gy'}, use_global_device_ids=true, to_apply=%region_87.88 | all-reduce | flops 18 | bytes 144 | tf_op jit(solution)/shard_map/psum | solution.py:163
  1806.2 5.3 fusion.59
  (1032 shorter events, 676.8 us)
Async XLA Ops:
  2.7 9.1 collective-permute-start
  2.7 9.1 collective-permute-start.1
  17.3 6.9 collective-permute-start.2
  21.2 7.4 collective-permute-start.3
  42.5 6.5 collective-permute-start.4
  42.6 6.4 collective-permute-start.5
  52.6 4.8 collective-permute-start.6
  136.6 6.5 collective-permute-start.8
  136.7 6.6 collective-permute-start.9
  231.9 6.9 collective-permute-start.12
  232.4 6.4 collective-permute-start.13
  244.5 4.3 collective-permute-start.15
  328.2 6.5 collective-permute-start.16
  328.3 6.4 collective-permute-start.17
  338.2 4.0 collective-permute-start.18
  340.5 4.5 collective-permute-start.19
  425.2 6.4 collective-permute-start.20
  425.2 6.4 collective-permute-start.21
  436.4 4.8 collective-permute-start.22
  439.0 4.3 collective-permute-start.23
  523.3 6.4 collective-permute-start.24
  523.3 6.6 collective-permute-start.25
  534.6 6.8 collective-permute-start.26
  538.2 4.9 collective-permute-start.27
  622.3 6.5 collective-permute-start.28
  622.6 6.2 collective-permute-start.29
  632.3 170.7 %collective-permute-start.30 = (f32[6,2,130,1]{2,1,3,0:T(2,128)S(1)}, f32[6,2,130,1]{2,1,3,0:T(2,128)S(1)}, u32[]{:S(2)}, u32[]{:S(2)}) collective-permute-start(f32[6,2,130,1]{2,1,3,0:T(2,128)S(1)} %copy.349), channel_id=1, source_target_pairs={{0,1},{1,2},{2,3},{3,0},{4,5},{5,6},{6,7},{7,4},{8,9},{9,10},{10,1... | collective-permute-start | bytes 18728 | tf_op jit(solution)/shard_map/ppermute | solution.py:26
  637.2 167.5 %collective-permute-start.31 = (f32[6,2,130,1]{2,1,3,0:T(2,128)S(1)}, f32[6,2,130,1]{2,1,3,0:T(2,128)S(1)}, u32[]{:S(2)}, u32[]{:S(2)}) collective-permute-start(f32[6,2,130,1]{2,1,3,0:T(2,128)S(1)} %copy.350), channel_id=1, source_target_pairs={{1,0},{2,1},{3,2},{0,3},{5,4},{6,5},{7,6},{4,7},{9,8},{10,9},{11,1... | collective-permute-start | bytes 18728 | tf_op jit(solution)/shard_map/ppermute | solution.py:28
  887.6 6.5 collective-permute-start.32
  887.7 6.4 collective-permute-start.33
  897.6 4.4 collective-permute-start.34
  901.2 4.0 collective-permute-start.35
  912.6 7.8 collective-permute-start.36
  912.7 7.7 collective-permute-start.37
  926.2 6.9 collective-permute-start.38
  932.1 6.0 collective-permute-start.39
  952.3 6.5 collective-permute-start.40
  952.4 6.4 collective-permute-start.41
  962.9 4.7 collective-permute-start.42
  966.9 4.0 collective-permute-start.43
  1050.1 6.5 collective-permute-start.44
  1050.1 6.6 collective-permute-start.45
  1060.9 4.4 collective-permute-start.46
  1064.3 4.0 collective-permute-start.47
  1149.3 6.7 collective-permute-start.48
  1149.6 6.4 collective-permute-start.49
  1160.2 4.4 collective-permute-start.50
  1163.5 4.0 collective-permute-start.51
  1248.9 6.5 collective-permute-start.52
  1249.0 6.4 collective-permute-start.53
  1259.6 4.5 collective-permute-start.54
  1262.9 4.2 collective-permute-start.55
  1348.1 6.5 collective-permute-start.56
  1348.2 6.4 collective-permute-start.57
  1358.8 4.7 collective-permute-start.58
  1362.5 4.0 collective-permute-start.59
  1447.4 6.5 collective-permute-start.60
  1447.5 6.6 collective-permute-start.61
  1458.2 4.4 collective-permute-start.62
  1461.6 4.0 collective-permute-start.63
  1547.6 8.9 collective-permute-start.64
  1547.6 8.9 collective-permute-start.65
  1559.9 170.3 %collective-permute-start.66 = (f32[6,2,130,1]{2,1,3,0:T(2,128)S(1)}, f32[6,2,130,1]{2,1,3,0:T(2,128)}, u32[]{:S(2)}, u32[]{:S(2)}) collective-permute-start(f32[6,2,130,1]{2,1,3,0:T(2,128)S(1)} %copy.422), channel_id=1, source_target_pairs={{0,1},{1,2},{2,3},{3,0},{4,5},{5,6},{6,7},{7,4},{8,9},{9,10},{10,1... | collective-permute-start | bytes 18728 | tf_op jit(solution)/shard_map/ppermute | solution.py:26
  1563.3 169.3 %collective-permute-start.67 = (f32[6,2,130,1]{2,1,3,0:T(2,128)}, f32[6,2,130,1]{2,1,3,0:T(2,128)}, u32[]{:S(2)}, u32[]{:S(2)}) collective-permute-start(f32[6,2,130,1]{2,1,3,0:T(2,128)} %copy.423), channel_id=1, source_target_pairs={{1,0},{2,1},{3,2},{0,3},{5,4},{6,5},{7,6},{4,7},{9,8},{10,9},{11,1... | collective-permute-start | bytes 18728 | tf_op jit(solution)/shard_map/ppermute | solution.py:28
  (213 other events, 3401.4 us)
where the time goes:
time: 1830 us; the launch traced here: 1810 us
  blocking collectives  922 us (50%)
  other arithmetic  348 us (19%)
  local copies, waits for them, and re-layouts  251 us (14%)
  starting transfers between devices  129 us (7%)
  matrix products  120 us (7%)
  waiting for transfers between devices  38.2 us (2%)
    psum x14, blocking collectives, body(): lax.psum((num_real, num_imag, squares), ('gx', 'gy'))  922 us
    add x40, other arithmetic, sweep(): return iterate + step_scale * jnp.stack([update_real, update_imag], axis=1)  126 us
    ppermute x34, starting transfers between devices, padded_2(): lax.ppermute(head, axis, [((i + 1) % count, i) for i in range(count)])  104 us
    dot_general x16, matrix products, restrict(): lax.dot_general(flat_bases, flat_field, (((1,), (1,)), ((), ())), precisi...  67 us
    while x40, other arithmetic  64.4 us
    slice x50, local copies, waits for them, and re-layouts, padded_2(): lax.slice_in_dim(cells, cells.shape[dim] - width, cells.shape[dim], axis=...  63.8 us
    sub x40, other arithmetic, sweep(): defect = residual - apply_operator(padded, edge_set, diagonal)  59.6 us
    while x240, local copies, waits for them, and re-layouts  55.3 us
  transfers between devices with their start and end apart: 68, of which 36 were waited for; matrix products, arithmetic and copies ran while one was open for 20% of the time, Pallas kernels for 0%

commit v1 on v0

--- a/solution.py
+++ b/solution.py
@@ -30,6 +30,19 @@
             axis=dim,
         )
     return cells
+
+
+def tree_sum(values, axes):
+    for axis in axes:
+        count = lax.axis_size(axis)
+        if count & (count - 1):
+            values = lax.psum(values, axis)
+            continue
+        stride = 1
+        while stride < count:
+            values = values + lax.ppermute(values, axis, [(i, i ^ stride) for i in range(count)])
+            stride *= 2
+    return values
 
 
 def edge_terms(gap_padded):
@@ -160,7 +173,8 @@
                 images[..., 0] * search[..., 1] - images[..., 1] * search[..., 0], axis=0
             )
             squares = jnp.sum(images * images, axis=(0, 2))
-            num_real, num_imag, squares = lax.psum((num_real, num_imag, squares), ("gx", "gy"))
+            packed = tree_sum(jnp.concatenate([num_real, num_imag, squares]), ("gy", "gx"))
+            num_real, num_imag, squares = jnp.split(packed, 3)
             denominator = squares + guard_value
             alpha_real = num_real / denominator
             alpha_imag = num_imag / denominator

time: 1830 us -> 1260 us (0.69)
  blocking collectives: 922 us -> 0 us
  waiting for transfers between devices: 38.2 us -> 369 us
  starting transfers between devices: 129 us -> 167 us
    psum x14 -> x0, blocking collectives: 922 us -> none  [body(): lax.psum((num_real, num_imag, squares), ('gx', 'gy'))]
    ppermute x0 -> x98, waiting for transfers between devices: none -> 319 us  [tree_sum(): lax.ppermute(values, axis, [(i, i ^ stride) for i in range(count)])]
    ppermute x0 -> x98, starting transfers between devices: none -> 40.6 us  [tree_sum(): lax.ppermute(values, axis, [(i, i ^ stride) for i in range(count)])]
  transfers between devices with their start and end apart: 68 -> 166, of which waited for: 36 -> 136; matrix products, arithmetic and copies ran while one was open for 20% -> 28% of each run, Pallas kernels for 0% -> 0%
where the time goes in v1:
time: 1260 us; the launch traced here: 1250 us
  waiting for transfers between devices  369 us (29%)
  other arithmetic  344 us (27%)
  local copies, waits for them, and re-layouts  246 us (20%)
  starting transfers between devices  167 us (13%)
  matrix products  116 us (9%)
    ppermute x98, waiting for transfers between devices, tree_sum(): lax.ppermute(values, axis, [(i, i ^ stride) for i in range(count)])  319 us
    add x40, other arithmetic, sweep(): return iterate + step_scale * jnp.stack([update_real, update_imag], axis=1)  127 us
    ppermute x34, starting transfers between devices, padded_2(): lax.ppermute(head, axis, [((i + 1) % count, i) for i in range(count)])  98.3 us
    while x40, other arithmetic  64.4 us
    slice x50, local copies, waits for them, and re-layouts, padded_2(): lax.slice_in_dim(cells, cells.shape[dim] - width, cells.shape[dim], axis=...  64.1 us
    dot_general x16, matrix products, restrict(): lax.dot_general(flat_bases, flat_field, (((1,), (1,)), ((), ())), precisi...  63.3 us
    sub x40, other arithmetic, sweep(): defect = residual - apply_operator(padded, edge_set, diagonal)  59.6 us
    while x240, local copies, waits for them, and re-layouts  55.3 us
  transfers between devices with their start and end apart: 166, of which 136 were waited for; matrix products, arithmetic and copies ran while one was open for 28% of the time, Pallas kernels for 0%

profile of v1, /device:TPU:16, one launch (start us, length us, event | category | flops | bytes accessed | tf_op | source)
XLA Modules:
  0.0 1247.3 jit_solution(9169495784697380146)
XLA Ops:
  2.7 5.7 collective-permute-start.1
  42.6 5.1 collective-permute-start.5
  82.4 5.1 collective-permute-done.12
  99.6 5.1 collective-permute-start.16
  130.2 4.3 collective-permute-done.20
  139.3 5.1 collective-permute-done.23
  156.7 5.1 collective-permute-start.27
  187.1 5.1 collective-permute-done.31
  196.9 5.1 collective-permute-done.34
  205.6 5.1 collective-permute-done.36
  214.0 5.1 collective-permute-start.38
  243.9 4.8 collective-permute-done.42
  253.5 5.1 collective-permute-done.45
  262.1 5.1 collective-permute-done.47
  270.5 5.4 collective-permute-start.49
  301.4 4.0 collective-permute-done.53
  310.2 5.1 collective-permute-done.56
  319.0 5.1 collective-permute-done.58
  328.0 5.1 collective-permute-start.60
  358.7 4.2 collective-permute-done.64
  367.7 5.1 collective-permute-done.67
  376.3 5.1 collective-permute-done.69
  386.2 5.1 collective-permute-start.71
  418.6 4.5 collective-permute-done.75
  428.6 4.4 collective-permute-done.78
  433.0 161.5 %while.26 = (s32[]{:T(128)}, f32[6,2,160,160]{3,2,1,0:T(8,128)}, f32[160,160]{1,0:T(8,128)S(1)}, f32[160,160]{1,0:T(8,128)S(1)}, f32[160,160]{1,0:T(8,128)S(1)},...) while((s32[]{:T(128)}, f32[6,2,160,160]{3,2,1,0:T(8,128)}, ...), condition=%wide.region_1.2_spmd.clone, body=%wide.region_0.1_spmd.clone.sunk | while | flops 6604803 | bytes 22425812 | solution.py:85
  595.1 4.2 copy.295
  600.0 4.9 fusion.58
  605.0 5.1 collective-permute-start.82
  628.5 5.2 collective-permute-start.86
  667.2 5.5 collective-permute-start.90
  691.5 4.0 multiply_reduce_fusion.6
  699.8 4.7 collective-permute-done.94
  709.2 5.1 collective-permute-done.97
  718.1 5.1 collective-permute-done.99
  727.1 5.1 collective-permute-start.101
  750.9 4.0 multiply_reduce_fusion.5
  768.8 5.1 collective-permute-done.108
  777.5 5.1 collective-permute-done.110
  786.5 5.1 collective-permute-start.112
  811.0 4.0 multiply_reduce_fusion.4
  820.0 4.0 collective-permute-done.116
  828.8 5.1 collective-permute-done.119
  837.5 5.1 collective-permute-done.121
  846.5 5.2 collective-permute-start.123
  879.8 4.3 collective-permute-done.127
  888.8 5.1 collective-permute-done.130
  897.7 5.1 collective-permute-done.132
  906.7 5.1 collective-permute-start.134
  930.8 4.0 multiply_reduce_fusion.2
  939.9 4.3 collective-permute-done.138
  949.0 5.1 collective-permute-done.141
  957.6 5.1 collective-permute-done.143
  966.7 5.1 collective-permute-start.145
  991.0 4.0 multiply_reduce_fusion.1
  999.6 4.3 collective-permute-done.149
  1008.7 5.1 collective-permute-done.152
  1017.4 5.1 collective-permute-done.154
  1026.4 5.2 collective-permute-start.156
  1050.2 4.0 multiply_reduce_fusion
  1058.8 4.3 collective-permute-done.160
  1073.2 161.4 %while.27 = (s32[]{:T(128)}, f32[6,2,160,160]{3,2,1,0:T(8,128)}, f32[160,160]{1,0:T(8,128)S(1)}, f32[160,160]{1,0:T(8,128)S(1)}, f32[160,160]{1,0:T(8,128)S(1)},...) while((s32[]{:T(128)}, f32[6,2,160,160]{3,2,1,0:T(8,128)}, ...), condition=%wide.region_24.25_spmd.clone, body=%wide.region_23.24_spmd.clone.sunk | while | flops 6604803 | bytes 22425812 | solution.py:85
  1236.2 4.2 copy.367
  1240.7 5.3 fusion.59
  (1306 shorter events, 942.7 us)
Async XLA Ops:
  2.7 9.1 collective-permute-start
  2.7 9.1 collective-permute-start.1
  17.4 6.9 collective-permute-start.2
  21.3 7.4 collective-permute-start.3
  42.6 6.5 collective-permute-start.4
  42.6 6.4 collective-permute-start.5
  72.5 5.1 collective-permute-start.9
  82.4 5.1 collective-permute-start.12
  91.0 5.1 collective-permute-start.14
  99.4 6.7 collective-permute-start.15
  99.6 6.4 collective-permute-start.16
  129.4 5.1 collective-permute-start.20
  139.3 5.1 collective-permute-start.23
  147.9 5.5 collective-permute-start.25
  156.6 6.5 collective-permute-start.26
  156.7 6.4 collective-permute-start.27
  186.9 5.3 collective-permute-start.31
  205.6 5.1 collective-permute-start.36
  213.9 6.5 collective-permute-start.37
  214.0 6.4 collective-permute-start.38
  243.6 5.1 collective-permute-start.42
  270.5 6.5 collective-permute-start.48
  270.5 6.8 collective-permute-start.49
  300.4 5.1 collective-permute-start.53
  318.8 5.2 collective-permute-start.58
  327.9 6.5 collective-permute-start.59
  328.0 6.4 collective-permute-start.60
  357.6 5.3 collective-permute-start.64
  386.2 6.4 collective-permute-start.70
  386.2 6.4 collective-permute-start.71
  418.1 5.1 collective-permute-start.75
  433.0 161.5 %collective-permute-start.79 = (f32[18]{0:T(128)S(1)}, f32[18]{0:T(128)S(1)}, u32[]{:S(2)}, u32[]{:S(2)}) collective-permute-start(f32[18]{0:T(128)S(1)} %add.1054), channel_id=1, source_target_pairs={{0,32},{4,36},{8,40},{12,44},{16,48},{20,52},{24,56},{28,60},{32,0... | collective-permute-start | bytes 224 | tf_op jit(solution)/shard_map/ppermute | solution.py:43
  594.5 5.2 collective-permute-start.80
  604.9 6.5 collective-permute-start.81
  605.0 6.4 collective-permute-start.82
  628.4 7.8 collective-permute-start.85
  628.5 7.8 collective-permute-start.86
  642.0 6.0 collective-permute-start.87
  646.9 6.0 collective-permute-start.88
  667.2 6.5 collective-permute-start.89
  667.2 6.9 collective-permute-start.90
  699.4 5.1 collective-permute-start.94
  717.9 5.2 collective-permute-start.99
  727.0 6.5 collective-permute-start.100
  727.1 6.4 collective-permute-start.101
  758.8 5.3 collective-permute-start.105
  786.4 6.5 collective-permute-start.111
  786.5 6.4 collective-permute-start.112
  819.0 5.1 collective-permute-start.116
  846.4 6.5 collective-permute-start.122
  846.5 6.6 collective-permute-start.123
  879.0 5.1 collective-permute-start.127
  897.5 5.3 collective-permute-start.132
  906.6 6.5 collective-permute-start.133
  906.7 6.4 collective-permute-start.134
  938.8 5.5 collective-permute-start.138
  966.6 6.5 collective-permute-start.144
  966.7 6.4 collective-permute-start.145
  998.9 5.1 collective-permute-start.149
  1026.3 6.5 collective-permute-start.155
  1026.4 6.6 collective-permute-start.156
  1058.1 5.1 collective-permute-start.160
  1073.0 161.7 %collective-permute-start.164 = (f32[18]{0:T(128)S(1)}, f32[18]{0:T(128)S(1)}, u32[]{:S(2)}, u32[]{:S(2)}) collective-permute-start(f32[18]{0:T(128)S(1)} %add.1171), channel_id=1, source_target_pairs={{0,32},{4,36},{8,40},{12,44},{16,48},{20,52},{24,56},{28,60},{32,0... | collective-permute-start | bytes 224 | tf_op jit(solution)/shard_map/ppermute | solution.py:43
  1234.7 5.7 collective-permute-start.165
  (301 other events, 2271.6 us)

commit v2 on v1

--- a/solution.py
+++ b/solution.py
@@ -149,6 +149,63 @@
         )
         return product.reshape(mode_count, 2, tile_rows, tile_cols)
 
+    def pair(left, right):
+        return lax.dot_general(
+            left, right, (((1,), (1,)), ((), ())), precision=highest, preferred_element_type=jnp.float32
+        )
+
+    gx_count = lax.axis_size("gx")
+    gy_count = lax.axis_size("gy")
+    gy_index = lax.axis_index("gy")
+    north_edge, south_edge, east_edge, west_edge = owned_edges
+    from_next_x = lax.ppermute(base_field[:, 0, :], "gx", [((i + 1) % gx_count, i) for i in range(gx_count)])
+    from_prev_x = lax.ppermute(base_field[:, -1, :], "gx", [(i, (i + 1) % gx_count) for i in range(gx_count)])
+    from_next_y = lax.ppermute(base_field[:, :, 0], "gy", [((i + 1) % gy_count, i) for i in range(gy_count)])
+    from_prev_y = lax.ppermute(base_field[:, :, -1], "gy", [(i, (i + 1) % gy_count) for i in range(gy_count)])
+    has_next_y = (gy_index < gy_count - 1).astype(jnp.float32)
+    has_prev_y = (gy_index > 0).astype(jnp.float32)
+    base_padded = jnp.pad(base_field, ((0, 0), (1, 1), (1, 1)))
+    base_image = owned_diag * base_field - (
+        north_edge * base_padded[:, 2:, 1:-1]
+        + south_edge * base_padded[:, :-2, 1:-1]
+        + east_edge * base_padded[:, 1:-1, 2:]
+        + west_edge * base_padded[:, 1:-1, :-2]
+    )
+    self_block = pair(flat_bases, base_image.reshape(basis_total, tile_rows * tile_cols))
+    gram_block = pair(flat_bases, flat_bases)
+    next_x_block = -pair(base_field[:, -1, :] * north_edge[-1], from_next_x)
+    prev_x_block = -pair(base_field[:, 0, :] * south_edge[0], from_prev_x)
+    next_y_block = -pair(base_field[:, :, -1] * east_edge[:, -1], from_next_y) * has_next_y
+    prev_y_block = -pair(base_field[:, :, 0] * west_edge[:, 0], from_prev_y) * has_prev_y
+    block_row = jnp.concatenate(
+        [self_block, next_x_block, prev_x_block, next_y_block, prev_y_block, squeeze_number * gram_block],
+        axis=1,
+    )
+    all_blocks = lax.all_gather(block_row, ("gx", "gy")).reshape(gx_count, gy_count, basis_total, 6 * basis_total)
+
+    def coarse_image(search):
+        turned = jnp.stack([-search[..., 1], search[..., 0]], axis=-1)
+        stacked = jnp.concatenate(
+            [
+                search,
+                jnp.roll(search, -1, axis=0),
+                jnp.roll(search, 1, axis=0),
+                jnp.roll(search, -1, axis=1),
+                jnp.roll(search, 1, axis=1),
+                turned,
+            ],
+            axis=2,
+        )
+        product = lax.dot_general(
+            all_blocks,
+            stacked.reshape(gx_count, gy_count, 6 * basis_total, 2 * mode_count),
+            (((3,), (2,)), ((0, 1), (0, 1))),
+            precision=highest,
+            preferred_element_type=jnp.float32,
+        )
+        return product.reshape(search.shape)
+
+    gx_index = lax.axis_index("gx")
     solution = jnp.zeros_like(forcing)
     residual_wide = force_wide
     for outer_step in range(ITERS):
@@ -161,26 +218,26 @@
         local_part = local_solve(residual_wide, wide_edges, wide_diag, inside)[
             :, :, MARGIN:-MARGIN, MARGIN:-MARGIN
         ]
-        search = restrict(residual)
+        search = lax.all_gather(restrict(residual), ("gx", "gy")).reshape(
+            gx_count, gy_count, basis_total, mode_count, 2
+        )
         coarse = jnp.zeros_like(search)
         for coarse_step in range(CSTEPS):
-            coarse_padded = padded_2(prolong(search), (("gx", 2), ("gy", 3)), 1) * unit_mask
-            images = restrict(apply_operator(coarse_padded, owned_edges, owned_diag))
+            images = coarse_image(search)
             num_real = jnp.sum(
-                images[..., 0] * search[..., 0] + images[..., 1] * search[..., 1], axis=0
+                images[..., 0] * search[..., 0] + images[..., 1] * search[..., 1], axis=(0, 1, 2)
             )
             num_imag = jnp.sum(
-                images[..., 0] * search[..., 1] - images[..., 1] * search[..., 0], axis=0
+                images[..., 0] * search[..., 1] - images[..., 1] * search[..., 0], axis=(0, 1, 2)
             )
-            squares = jnp.sum(images * images, axis=(0, 2))
-            packed = tree_sum(jnp.concatenate([num_real, num_imag, squares]), ("gy", "gx"))
-            num_real, num_imag, squares = jnp.split(packed, 3)
+            squares = jnp.sum(images * images, axis=(0, 1, 2, 4))
             denominator = squares + guard_value
             alpha_real = num_real / denominator
             alpha_imag = num_imag / denominator
             coarse = coarse + complex_scale(alpha_real, alpha_imag, search)
             search = search - complex_scale(alpha_real, alpha_imag, images)
-        solution = solution + local_part + prolong(coarse)
+        own_coarse = coarse[gx_index, gy_index]
+        solution = solution + local_part + prolong(own_coarse)
     return solution
 
 

time: 1260 us -> 918 us (0.73)
  waiting for transfers between devices: 369 us -> 12.4 us
  blocking collectives: 0 us -> 150 us
  other arithmetic: 344 us -> 200 us
  starting transfers between devices: 167 us -> 30.9 us
  local copies, waits for them, and re-layouts: 246 us -> 353 us
  matrix products: 116 us -> 139 us
  between operations: 2.83 us -> 16.9 us
    ppermute x98 -> x4, waiting for transfers between devices: 319 us -> 0.01 us  [the longest x1 0.01 us: body(): lax.ppermute(base_field[:, -1, :], 'gx', [(i, (i + 1) % gx_count) for i i...]
    all_gather x0 -> x2, blocking collectives: none -> 150 us  [body(): lax.all_gather(restrict(residual), ('gx', 'gy'))]
    concatenate x0 -> x89, local copies, waits for them, and re-layouts: none -> 141 us  [the longest x24 79.4 us: coarse_image(): jnp.concatenate([search, jnp.roll(search, -1, axis=0), jnp.roll(search, 1...]
    dot_general x0 -> x20, matrix products: none -> 124 us  [the longest x14 112 us: coarse_image(): lax.dot_general(all_blocks, stacked.reshape(gx_count, gy_count, 6 * basis...]
    add x40, other arithmetic: 127 us -> 26.8 us  [sweep(): return iterate + step_scale * jnp.stack([update_real, update_imag], axis=1)]
    ppermute x34 -> x6, starting transfers between devices: 98.3 us -> 18.3 us  [padded_2(): lax.ppermute(head, axis, [((i + 1) % count, i) for i in range(count)])]
    slice x0 -> x82, local copies, waits for them, and re-layouts: none -> 66.3 us  [the longest x32 27.5 us: coarse_image(): jnp.roll(search, 1, axis=0)]
    while x40, other arithmetic: 64.4 us -> 6.52 us
  transfers between devices with their start and end apart: 166 -> 17, of which waited for: 136 -> 7; matrix products, arithmetic and copies ran while one was open for 28% -> 18% of each run, Pallas kernels for 0% -> 0%
where the time goes in v2:
time: 918 us; the launch traced here: 905 us
  local copies, waits for them, and re-layouts  353 us (38%)
  other arithmetic  200 us (22%)
  blocking collectives  150 us (16%)
  matrix products  139 us (15%)
  starting transfers between devices  30.9 us (3%)
  between operations  16.9 us (2%)
  waiting for transfers between devices  12.4 us (1%)
    all_gather x2, blocking collectives, body(): lax.all_gather(restrict(residual), ('gx', 'gy'))  150 us
    dot_general x14, matrix products, coarse_image(): lax.dot_general(all_blocks, stacked.reshape(gx_count, gy_count, 6 * basis...  112 us
    concatenate x24, local copies, waits for them, and re-layouts, coarse_image(): jnp.concatenate([search, jnp.roll(search, -1, axis=0), jnp.roll(search, 1...  79.4 us
    sub x40, other arithmetic, sweep(): defect = residual - apply_operator(padded, edge_set, diagonal)  59.6 us
    while x80, local copies, waits for them, and re-layouts  55.7 us
    slice x32, local copies, waits for them, and re-layouts, coarse_image(): jnp.roll(search, 1, axis=0)  27.5 us
    add x40, other arithmetic, sweep(): return iterate + step_scale * jnp.stack([update_real, update_imag], axis=1)  26.8 us
    sub x14, other arithmetic, complex_scale(): alpha_real * vectors[..., 0] - alpha_imag * vectors[..., 1]  20.3 us
  transfers between devices with their start and end apart: 17, of which 7 were waited for; matrix products, arithmetic and copies ran while one was open for 18% of the time, Pallas kernels for 0%

profile of v2, /device:TPU:16, one launch (start us, length us, event | category | flops | bytes accessed | tf_op | source)
XLA Modules:
  0.0 904.5 jit_solution(2233387813146662917)
XLA Ops:
  8.5 5.7 collective-permute-start.1
  14.9 3.3 copy_multiply_fusion
  18.2 3.1 fusion.144
  21.3 2.5 copy.867
  25.1 2.5 copy.868
  29.8 5.4 fusion.64
  37.1 2.7 copy.861
  43.9 2.8 collective-permute-done.2
  46.6 5.2 collective-permute-start.4
  55.7 2.9 maximum_multiply_fusion.5
  58.9 3.3 fusion.61
  69.9 83.0 %while.26 = (s32[]{:T(128)}, f32[6,2,160,160]{3,2,1,0:T(8,128)S(1)}, f32[160,160]{1,0:T(8,128)S(1)}, f32[160,160]{1,0:T(8,128)S(1)}, f32[160,160]{1,0:T(8,128)S(...) while((s32[]{:T(128)}, ...), condition=%wide.region_1.2_spmd.clone, body=%wide.region_0.1_spmd.clone.sunk | while | flops 6604803 | bytes 21606556 | solution.py:85
  155.1 4.1 fusion.67
  159.4 74.9 %all-gather.1 = f32[5120,6,2]{1,2,0:T(2,128)} all-gather(f32[40,6,2]{1,2,0:T(2,128)S(1)} %copy.870), channel_id=3, replica_groups=mesh['gx'=32,'gy'=4] {'gx','gy'}, dimensions={0}, use_global_device_ids=true | all-gather | bytes 247680 | tf_op jit(solution)/shard_map/all_gather | solution.py:221
  234.3 6.6 copy.871
  241.0 7.2 copy.1055
  255.6 4.5 fusion.143
  260.1 5.6 copy.872
  267.5 6.6 copy.877
  285.0 2.7 copy.865
  289.3 5.4 concatenate.424
  294.7 7.9 multiply_reduce_fusion.13
  314.1 3.8 concatenate.434
  317.9 7.6 multiply_reduce_fusion.12
  337.8 3.6 concatenate.444
  341.5 7.6 multiply_reduce_fusion.11
  361.4 3.6 concatenate.454
  365.1 7.8 multiply_reduce_fusion.10
  385.2 3.6 concatenate.464
  388.8 7.6 multiply_reduce_fusion.9
  408.8 3.6 concatenate.474
  412.4 7.6 multiply_reduce_fusion.8
  432.3 3.6 concatenate.484
  436.0 7.8 multiply_reduce_fusion.7
  448.4 5.5 fusion.54
  453.9 5.1 collective-permute-start.9
  475.2 5.2 collective-permute-start.13
  480.4 2.5 collective-permute-done.12
  486.9 3.3 collective-permute-start.14
  493.4 2.4 copy.962
  497.3 2.5 copy.963
  499.9 2.9 maximum_multiply_fusion.4
  506.7 75.2 %all-gather.2 = f32[5120,6,2]{1,2,0:T(2,128)} all-gather(f32[40,6,2]{1,2,0:T(2,128)S(1)} %copy.966), channel_id=4, replica_groups=mesh['gx'=32,'gy'=4] {'gx','gy'}, dimensions={0}, use_global_device_ids=true | all-gather | bytes 247680 | tf_op jit(solution)/shard_map/all_gather | solution.py:221
  581.9 6.1 copy.1064
  591.5 4.4 fusion.141
  596.7 6.6 copy.967
  610.2 6.6 copy.973
  621.2 6.6 copy.968
  639.1 5.7 concatenate.501
  644.8 7.9 multiply_reduce_fusion.6
  664.2 5.0 concatenate.511
  669.2 8.4 multiply_reduce_fusion.5
  689.0 5.0 concatenate.521
  694.1 8.4 multiply_reduce_fusion.4
  713.9 5.2 concatenate.531
  719.1 8.4 multiply_reduce_fusion.3
  738.9 5.0 concatenate.541
  744.0 8.4 multiply_reduce_fusion.2
  763.8 5.0 concatenate.551
  768.8 8.4 multiply_reduce_fusion.1
  791.7 4.9 concatenate.561
  796.6 8.4 multiply_reduce_fusion
  808.1 83.0 %while.27 = (s32[]{:T(128)}, f32[6,2,160,160]{3,2,1,0:T(8,128)S(1)}, f32[160,160]{1,0:T(8,128)S(1)}, f32[160,160]{1,0:T(8,128)S(1)}, f32[160,160]{1,0:T(8,128)S(...) while((s32[]{:T(128)}, ...), condition=%wide.region_31.32_spmd.clone, body=%wide.region_30.31_spmd.clone.sunk | while | flops 6604803 | bytes 21606556 | solution.py:85
  893.1 3.3 fusion.55
  (887 shorter events, 419.9 us)
Async XLA Ops:
  6.5 288.2 %all-gather.5.cloned.1.call-start = ((), (), s32[]{:S(2)}) async-start(), calls=%async_computation | async-start | bytes 5283840 | tf_op jit(solution)/shard_map/all_gather | solution.py:184
  8.4 26.8 %collective-permute-start = (f32[14,17,128]{2,1,0:T(8,128)S(1)}, f32[14,17,128]{2,1,0:T(8,128)S(1)}, u32[]{:S(2)}, u32[]{:S(2)}) collective-permute-start(f32[14,17,128]{2,1,0:T(8,128)S(1)} %get-tuple-element.494), channel_id=1, source_target_pairs={{0,4},{4,8},{8,12},{12,16},{16,20},{20,24},{24,28},{28,32},{32,36}... | collective-permute-start | bytes 365576 | tf_op jit(solution)/shard_map/ppermute | solution.py:26
  8.5 26.7 %collective-permute-start.1 = (f32[14,17,128]{2,1,0:T(8,128)S(1)}, f32[14,17,128]{2,1,0:T(8,128)S(1)}, u32[]{:S(2)}, u32[]{:S(2)}) collective-permute-start(f32[14,17,128]{2,1,0:T(8,128)S(1)} %get-tuple-element.495), channel_id=1, source_target_pairs={{4,0},{8,4},{12,8},{16,12},{20,16},{24,20},{28,24},{32,28},{36,32}... | collective-permute-start | bytes 365576 | tf_op jit(solution)/shard_map/ppermute | solution.py:28
  14.9 3.3 copy-start.78
  18.2 3.1 copy-start.1
  23.8 40.4 %collective-permute-start.7 = (f32[40,128]{1,0:T(8,128)S(1)}, f32[40,128]{1,0:T(8,128)}, u32[]{:S(2)}, u32[]{:S(2)}) collective-permute-start(f32[40,128]{1,0:T(8,128)S(1)} %bitcast.361), channel_id=1, source_target_pairs={{0,1},{1,2},{2,3},{3,0},{4,5},{5,6},{6,7},{7,4},{8,9},{9,10},{10,1... | collective-permute-start | bytes 61448 | tf_op jit(solution)/shard_map/ppermute | solution.py:164
  27.6 39.4 %collective-permute-start.6 = (f32[40,128]{1,0:T(8,128)S(1)}, f32[40,128]{1,0:T(8,128)}, u32[]{:S(2)}, u32[]{:S(2)}) collective-permute-start(f32[40,128]{1,0:T(8,128)S(1)} %bitcast.362), channel_id=1, source_target_pairs={{1,0},{2,1},{3,2},{0,3},{5,4},{6,5},{7,6},{4,7},{9,8},{10,9},{11,1... | collective-permute-start | bytes 61448 | tf_op jit(solution)/shard_map/ppermute | solution.py:163
  29.8 5.5 copy-start.26
  29.8 5.5 copy-start.55
  29.8 32.4 %collective-permute-start.5 = (f32[40,128]{1,0:T(8,128)}, f32[40,128]{1,0:T(8,128)}, u32[]{:S(2)}, u32[]{:S(2)}) collective-permute-start(f32[40,128]{1,0:T(8,128)} %get-tuple-element.480), channel_id=1, source_target_pairs={{0,4},{4,8},{8,12},{12,16},{16,20},{20,24},{24,28},{28,32},{32,36}... | collective-permute-start | bytes 61448 | tf_op jit(solution)/shard_map/ppermute | solution.py:162
  37.1 4.0 copy-start.48
  39.9 6.8 collective-permute-start.2
  42.5 10.8 %collective-permute-start.3 = (f32[14,162,17]{1,0,2:T(8,128)}, f32[14,162,17]{1,0,2:T(8,128)}, u32[]{:S(2)}, u32[]{:S(2)}) collective-permute-start(f32[14,162,17]{1,0,2:T(8,128)} %copy.862), channel_id=1, source_target_pairs={{1,0},{2,1},{3,2},{0,3},{5,4},{6,5},{7,6},{4,7},{9,8},{10,9},{11,1... | collective-permute-start | bytes 462680 | tf_op jit(solution)/shard_map/ppermute | solution.py:28
  46.6 16.5 %collective-permute-start.4 = (f32[40,128]{1,0:T(8,128)}, f32[40,128]{1,0:T(8,128)}, u32[]{:S(2)}, u32[]{:S(2)}) collective-permute-start(f32[40,128]{1,0:T(8,128)} %get-tuple-element.481), channel_id=1, source_target_pairs={{4,0},{8,4},{12,8},{16,12},{20,16},{24,20},{28,24},{32,28},{36,32}... | collective-permute-start | bytes 61448 | tf_op jit(solution)/shard_map/ppermute | solution.py:161
  55.7 2.9 copy-start.73
  55.7 3.1 copy-start.2
  58.6 6.6 copy-start.28
  58.8 3.4 copy-start.67
  58.8 3.4 copy-start.69
  58.8 3.4 copy-start.71
  58.8 5.2 copy-start.63
  58.8 5.2 copy-start.65
  64.1 3.9 copy-start.77
  153.0 6.2 copy-start.8
  153.0 6.2 copy-start.10
  153.0 6.2 copy-start.12
  153.0 6.2 copy-start.14
  153.0 6.2 copy-start.16
  153.0 6.2 copy-start.18
  153.0 6.2 copy-start.20
  241.0 14.6 %slice-start = ((s8[5242880]{0:T(1024)(128)(4,1)}), s8[1048576]{0:T(1024)(128)(4,1)S(1)}, s32[]{:S(2)}) async-start(s8[5242880]{0:T(1024)(128)(4,1)} %bitcast.259), calls=%async_computation.1 | async-start | bytes 2097152
  250.0 5.7 slice-start.1
  274.1 5.5 copy-start.6
  285.0 2.7 copy-start.52
  285.0 2.7 copy-start.53
  285.0 2.7 copy-start.74
  285.0 2.7 copy-start.75
  314.1 3.8 copy-start.33
  444.3 3.1 copy-start.56
  444.3 3.1 copy-start.57
  444.3 3.1 copy-start.58
  444.3 3.1 copy-start.59
  453.8 16.8 %copy-start.22 = (f32[6,2,128,128]{3,0,2,1:T(8,128)}, f32[6,2,128,128]{3,0,2,1:T(8,128)S(1)}, u32[]{:S(2)}) copy-start(f32[6,2,128,128]{3,0,2,1:T(8,128)S(1)} %fusion.54) | copy-start | bytes 2359300
  453.8 6.5 collective-permute-start.8
  453.9 6.4 collective-permute-start.9
  463.5 3.7 collective-permute-start.10
  464.5 4.5 collective-permute-start.11
  475.1 7.8 collective-permute-start.12
  475.2 7.7 collective-permute-start.13
  485.0 5.1 copy-start.47
  486.9 6.5 collective-permute-start.14
  491.3 6.0 collective-permute-start.15
  499.9 4.5 copy-start.3
  588.1 3.5 copy-start
  603.4 2.9 copy-start.54
  603.4 2.9 copy-start.62
  634.4 4.7 copy-start.29
  634.4 3.5 copy-start.51
  634.4 3.5 copy-start.76
  664.2 5.0 copy-start.39
  689.0 5.1 copy-start.41
  713.9 5.2 copy-start.43
  738.9 5.0 copy-start.45
  763.7 5.1 copy-start.31
  (74 other events, 109.2 us)
Sparse Core Ops, SparseCore 0:
  68.8 64.3 all-gather.4

commit v3 on v2

--- a/solution.py
+++ b/solution.py
@@ -41,6 +41,23 @@
         stride = 1
         while stride < count:
             values = values + lax.ppermute(values, axis, [(i, i ^ stride) for i in range(count)])
+            stride *= 2
+    return values
+
+
+def tree_gather(values, axes):
+    for axis in axes:
+        count = lax.axis_size(axis)
+        if count & (count - 1):
+            values = lax.all_gather(values, axis)
+            continue
+        index = lax.axis_index(axis)
+        values = values[None]
+        stride = 1
+        while stride < count:
+            other = lax.ppermute(values, axis, [(i, i ^ stride) for i in range(count)])
+            upper = (index // stride) % 2 == 1
+            values = jnp.where(upper, jnp.concatenate([other, values]), jnp.concatenate([values, other]))
             stride *= 2
     return values
 
@@ -177,35 +194,31 @@
     prev_x_block = -pair(base_field[:, 0, :] * south_edge[0], from_prev_x)
     next_y_block = -pair(base_field[:, :, -1] * east_edge[:, -1], from_next_y) * has_next_y
     prev_y_block = -pair(base_field[:, :, 0] * west_edge[:, 0], from_prev_y) * has_prev_y
-    block_row = jnp.concatenate(
-        [self_block, next_x_block, prev_x_block, next_y_block, prev_y_block, squeeze_number * gram_block],
-        axis=1,
-    )
-    all_blocks = lax.all_gather(block_row, ("gx", "gy")).reshape(gx_count, gy_count, basis_total, 6 * basis_total)
+    block_set = jnp.stack(
+        [self_block, next_x_block, prev_x_block, next_y_block, prev_y_block, squeeze_number * gram_block]
+    )
+    tile_total = gx_count * gy_count
+    all_blocks = jnp.moveaxis(lax.all_gather(block_set, ("gx", "gy")), 0, -1)
 
     def coarse_image(search):
-        turned = jnp.stack([-search[..., 1], search[..., 0]], axis=-1)
-        stacked = jnp.concatenate(
-            [
-                search,
-                jnp.roll(search, -1, axis=0),
-                jnp.roll(search, 1, axis=0),
-                jnp.roll(search, -1, axis=1),
-                jnp.roll(search, 1, axis=1),
-                turned,
-            ],
-            axis=2,
-        )
-        product = lax.dot_general(
-            all_blocks,
-            stacked.reshape(gx_count, gy_count, 6 * basis_total, 2 * mode_count),
-            (((3,), (2,)), ((0, 1), (0, 1))),
-            precision=highest,
-            preferred_element_type=jnp.float32,
-        )
-        return product.reshape(search.shape)
+        halves = search.reshape(basis_total, mode_count, 2, tile_total)
+        turned = jnp.stack([-halves[:, :, 1], halves[:, :, 0]], axis=2).reshape(search.shape)
+        shifted = (
+            search,
+            jnp.roll(search, -gy_count, axis=-1),
+            jnp.roll(search, gy_count, axis=-1),
+            jnp.roll(search, -1, axis=-1),
+            jnp.roll(search, 1, axis=-1),
+            turned,
+        )
+        total = None
+        for block, vectors in zip(all_blocks, shifted):
+            term = jnp.sum(block[:, :, None, :] * vectors[None, :, :, :], axis=1)
+            total = term if total is None else total + term
+        return total
 
     gx_index = lax.axis_index("gx")
+    tile_index = gx_index * gy_count + gy_index
     solution = jnp.zeros_like(forcing)
     residual_wide = force_wide
     for outer_step in range(ITERS):
@@ -218,25 +231,41 @@
         local_part = local_solve(residual_wide, wide_edges, wide_diag, inside)[
             :, :, MARGIN:-MARGIN, MARGIN:-MARGIN
         ]
-        search = lax.all_gather(restrict(residual), ("gx", "gy")).reshape(
-            gx_count, gy_count, basis_total, mode_count, 2
-        )
+        gathered = tree_gather(restrict(residual).reshape(-1), ("gy", "gx"))
+        search = gathered.reshape(tile_total, -1).T.reshape(basis_total, 2 * mode_count, tile_total)
         coarse = jnp.zeros_like(search)
         for coarse_step in range(CSTEPS):
             images = coarse_image(search)
+            image_halves = images.reshape(basis_total, mode_count, 2, tile_total)
+            search_halves = search.reshape(basis_total, mode_count, 2, tile_total)
             num_real = jnp.sum(
-                images[..., 0] * search[..., 0] + images[..., 1] * search[..., 1], axis=(0, 1, 2)
+                image_halves[:, :, 0] * search_halves[:, :, 0] + image_halves[:, :, 1] * search_halves[:, :, 1],
+                axis=(0, 2),
             )
             num_imag = jnp.sum(
-                images[..., 0] * search[..., 1] - images[..., 1] * search[..., 0], axis=(0, 1, 2)
+                image_halves[:, :, 0] * search_halves[:, :, 1] - image_halves[:, :, 1] * search_halves[:, :, 0],
+                axis=(0, 2),
             )
-            squares = jnp.sum(images * images, axis=(0, 1, 2, 4))
+            squares = jnp.sum(image_halves * image_halves, axis=(0, 2, 3))
             denominator = squares + guard_value
-            alpha_real = num_real / denominator
-            alpha_imag = num_imag / denominator
-            coarse = coarse + complex_scale(alpha_real, alpha_imag, search)
-            search = search - complex_scale(alpha_real, alpha_imag, images)
-        own_coarse = coarse[gx_index, gy_index]
+            alpha_real = (num_real / denominator)[None, :, None]
+            alpha_imag = (num_imag / denominator)[None, :, None]
+            coarse_halves = coarse.reshape(search_halves.shape)
+            coarse = jnp.stack(
+                [
+                    coarse_halves[:, :, 0] + alpha_real * search_halves[:, :, 0] - alpha_imag * search_halves[:, :, 1],
+                    coarse_halves[:, :, 1] + alpha_real * search_halves[:, :, 1] + alpha_imag * search_halves[:, :, 0],
+                ],
+                axis=2,
+            ).reshape(search.shape)
+            search = jnp.stack(
+                [
+                    search_halves[:, :, 0] - (alpha_real * image_halves[:, :, 0] - alpha_imag * image_halves[:, :, 1]),
+                    search_halves[:, :, 1] - (alpha_real * image_halves[:, :, 1] + alpha_imag * image_halves[:, :, 0]),
+                ],
+                axis=2,
+            ).reshape(search.shape)
+        own_coarse = lax.dynamic_index_in_dim(coarse, tile_index, axis=2, keepdims=False)
         solution = solution + local_part + prolong(own_coarse)
     return solution
 

time: 918 us -> 701 us (0.76)
  other arithmetic: 200 us -> 381 us
  local copies, waits for them, and re-layouts: 353 us -> 176 us
  blocking collectives: 150 us -> 0 us
  matrix products: 139 us -> 32.2 us
  waiting for transfers between devices: 12.4 us -> 50.1 us
    reduce_sum x28 -> x125, other arithmetic: 13.1 us -> 211 us  [the longest x83 177 us: coarse_image(): term = jnp.sum(block[:, :, None, :] * vectors[None, :, :, :], axis=1)]
    all_gather x2 -> x0, blocking collectives: 150 us -> none  [body(): lax.all_gather(restrict(residual), ('gx', 'gy'))]
    concatenate x89 -> x8, local copies, waits for them, and re-layouts: 141 us -> 3.43 us  [the longest x2 0.86 us: coarse_image(): jnp.roll(search, gy_count, axis=-1)]
    dot_general x14 -> x0, matrix products: 112 us -> none  [coarse_image(): lax.dot_general(all_blocks, stacked.reshape(gx_count, gy_count, 6 * basis...]
    slice x78 -> x59, local copies, waits for them, and re-layouts: 58.1 us -> 7.82 us  [the longest x28 3.66 us: coarse_image(): jnp.roll(search, -gy_count, axis=-1)]
    ppermute x0 -> x14, waiting for transfers between devices: none -> 32.7 us  [tree_gather(): other = lax.ppermute(values, axis, [(i, i ^ stride) for i in range(count)])]
    mul x0 -> x12, local copies, waits for them, and re-layouts: none -> 28.8 us  [the longest x11 28.8 us: coarse_image(): term = jnp.sum(block[:, :, None, :] * vectors[None, :, :, :], axis=1)]
    sub x26 -> x4, other arithmetic: 27.3 us -> 3.37 us  [the longest x2 3.15 us: body(): coarse_halves[:, :, 0] + alpha_real * search_halves[:, :, 0]]
  transfers between devices with their start and end apart: 17 -> 31, of which waited for: 7 -> 18; matrix products, arithmetic and copies ran while one was open for 18% -> 26% of each run, Pallas kernels for 0% -> 0%
where the time goes in v3:
time: 701 us; the launch traced here: 688 us
  other arithmetic  381 us (54%)
  local copies, waits for them, and re-layouts  176 us (25%)
  waiting for transfers between devices  50.1 us (7%)
  matrix products  32.2 us (5%)
  starting transfers between devices  28.8 us (4%)
  between operations  17.8 us (3%)
    reduce_sum x83, other arithmetic, coarse_image(): term = jnp.sum(block[:, :, None, :] * vectors[None, :, :, :], axis=1)  177 us
    sub x40, other arithmetic, sweep(): defect = residual - apply_operator(padded, edge_set, diagonal)  59.6 us
    while x200, local copies, waits for them, and re-layouts  57.1 us
    ppermute x14, waiting for transfers between devices, tree_gather(): other = lax.ppermute(values, axis, [(i, i ^ stride) for i in range(count)])  32.7 us
    mul x11, local copies, waits for them, and re-layouts, coarse_image(): term = jnp.sum(block[:, :, None, :] * vectors[None, :, :, :], axis=1)  28.8 us
    add x40, other arithmetic, sweep(): return iterate + step_scale * jnp.stack([update_real, update_imag], axis=1)  26.8 us
    reduce_sum x14, other arithmetic, body(): jnp.sum(image_halves[:, :, 0] * search_halves[:, :, 0] + image_halves[:,...  20.4 us
    unnamed x291, local copies, waits for them, and re-layouts  19.2 us
  transfers between devices with their start and end apart: 31, of which 18 were waited for; matrix products, arithmetic and copies ran while one was open for 26% of the time, Pallas kernels for 0%

profile of v3, /device:TPU:16, one launch (start us, length us, event | category | flops | bytes accessed | tf_op | source)
XLA Modules:
  0.0 688.4 jit_solution(5474052927948976537)
XLA Ops:
  8.4 5.7 collective-permute-start.1
  14.9 3.3 copy_multiply_fusion
  18.8 5.1 collective-permute-start.4
  23.8 3.1 fusion.221
  27.0 2.6 copy.2284
  32.2 2.6 copy.2278
  38.8 3.1 copy.2283
  41.9 3.3 collective-permute-start.7
  46.7 2.4 copy.2279
  49.2 2.7 maximum_multiply_fusion.5
  55.2 3.5 fusion.23
  60.4 9.2 %fusion.42 = f32[6,40,40]{2,1,0:T(8,128)S(1)} fusion(f32[40,128,128]{2,0,1:T(8,128)} %copy-done.37, f32[128,128]{1,0:T(8,128)S(1)} %get-tuple-element.597, f32[128,128]{1,0:T(8,128)S(1)} %get-tuple-element.596, f32[128,128]{1,0:T(8,128)S(1)} %get-tuple-element.595, f32[128,128]{1,0:T(8,128)S(1)} %get-tuple-element.594, f32[128,128]{1,0:T(8,128)S(1)} %get-tuple-element.593), kind=kOutput, calls=%fused_computation.152 | convolution fusion | flops 320471040 | bytes 5591040 | tf_op jit(solution)/shard_map/dot_general | solution.py:170
  72.9 5.1 collective-permute-done.9
  79.5 2.2 fusion.47
  84.6 4.2 collective-permute-done.12
  89.0 4.9 collective-permute-done.13
  94.0 84.9 %while.26 = (s32[]{:T(128)}, f32[6,2,160,160]{3,2,1,0:T(8,128)S(1)}, f32[160,160]{1,0:T(8,128)S(1)}, f32[160,160]{1,0:T(8,128)S(1)}, f32[160,160]{1,0:T(8,128)S(...) while((s32[]{:T(128)}, ...), condition=%wide.region_1.2_spmd.clone, body=%wide.region_0.1_spmd.clone.sunk | while | flops 6604803 | bytes 21606564 | solution.py:102
  178.9 2.7 copy.2281
  188.0 10.6 %slice_bitcast_fusion.4 = (f32[40,40,128]{1,0,2:T(8,128)}, f32[40,40,128]{1,0,2:T(8,128)}, f32[40,40,128]{1,0,2:T(8,128)}, f32[40,40,128]{1,0,2:T(8,128)}, f32[4...) fusion(f32[6,40,40,128]{2,1,0,3:T(8,128)} %bitcast.766), kind=kLoop, calls=%fused_computation.131 | loop fusion | bytes 9830400 | tf_op jit(solution)/shard_map/mul | solution.py:216
  198.5 3.0 copy.2298
  203.4 2.8 copy.2296
  206.2 3.1 copy.2294
  209.3 3.1 copy.2292
  212.4 3.5 copy.2290
  215.9 3.1 multiply_reduce_fusion.79
  219.1 3.0 multiply_reduce_fusion.80
  226.1 4.7 multiply_reduce_fusion.78
  234.8 2.1 multiply_reduce_fusion.77
  245.5 2.2 multiply_reduce_fusion.76
  251.7 2.1 multiply_reduce_fusion.71
  262.5 2.4 multiply_reduce_fusion.70
  281.8 2.2 multiply_reduce_fusion.64
  294.3 2.1 multiply_reduce_fusion.54
  303.0 2.2 multiply_reduce_fusion.58
  323.9 2.5 multiply_reduce_fusion.52
  342.4 2.2 multiply_reduce_fusion.45
  354.4 4.9 fusion.32
  361.6 5.0 collective-permute-done.15
  379.0 2.8 maximum_multiply_fusion.6
  386.1 5.3 collective-permute-done.19
  394.0 2.4 copy.2319
  397.4 2.4 copy.2318
  402.4 2.4 copy.2321
  404.9 2.6 collective-permute-done.21
  407.5 2.5 copy.2320
  409.9 3.2 maximum_multiply_fusion.4
  415.2 3.5 fusion.21
  419.2 3.4 collective-permute-done.23
  422.6 2.7 collective-permute-start.24
  425.3 2.4 collective-permute-done.24
  429.1 3.7 collective-permute-done.26
  433.0 5.4 collective-permute-done.27
  438.5 3.6 copy.2322
  445.5 85.5 %while.27 = (s32[]{:T(128)}, f32[6,2,160,160]{3,2,1,0:T(8,128)S(1)}, f32[160,160]{1,0:T(8,128)S(1)}, f32[160,160]{1,0:T(8,128)S(1)}, f32[160,160]{1,0:T(8,128)S(...) while((s32[]{:T(128)}, ...), condition=%wide.region_73.74_spmd.clone, body=%wide.region_72.73_spmd.clone.sunk | while | flops 6604803 | bytes 22835448 | solution.py:102
  531.0 2.7 copy.2323
  545.6 2.3 multiply_reduce_fusion.41
  562.5 2.4 multiply_reduce_fusion.33
  580.8 2.2 multiply_reduce_fusion.27
  600.8 2.2 multiply_reduce_fusion.21
  622.1 2.4 multiply_reduce_fusion.15
  641.4 2.2 multiply_reduce_fusion.8
  650.7 2.1 fusion.70
  662.4 2.2 multiply_reduce_fusion.2
  675.0 5.3 fusion.33
  (1117 shorter events, 461.1 us)
Async XLA Ops:
  6.5 181.4 %all-gather.3.cloned.1.call-start = ((), (), s32[]{:S(2)}) async-start(), calls=%async_computation | async-start | bytes 15851520 | tf_op jit(solution)/shard_map/all_gather | solution.py:201
  8.4 22.2 %collective-permute-start.1 = (f32[14,17,128]{2,1,0:T(8,128)S(1)}, f32[14,17,128]{2,1,0:T(8,128)S(1)}, u32[]{:S(2)}, u32[]{:S(2)}) collective-permute-start(f32[14,17,128]{2,1,0:T(8,128)S(1)} %get-tuple-element.635), channel_id=1, source_target_pairs={{4,0},{8,4},{12,8},{16,12},{20,16},{24,20},{28,24},{32,28},{36,32}... | collective-permute-start | bytes 365576 | tf_op jit(solution)/shard_map/ppermute | solution.py:28
  14.2 16.4 %collective-permute-start = (f32[14,17,128]{2,1,0:T(8,128)S(1)}, f32[14,17,128]{2,1,0:T(8,128)S(1)}, u32[]{:S(2)}, u32[]{:S(2)}) collective-permute-start(f32[14,17,128]{2,1,0:T(8,128)S(1)} %get-tuple-element.634), channel_id=1, source_target_pairs={{0,4},{4,8},{8,12},{12,16},{16,20},{20,24},{24,28},{28,32},{32,36}... | collective-permute-start | bytes 365576 | tf_op jit(solution)/shard_map/ppermute | solution.py:26
  18.1 8.8 %copy-start.37 = (f32[40,128,128]{2,0,1:T(8,128)}, f32[40,128,128]{2,0,1:T(8,128)S(1)}, u32[]{:S(2)}) copy-start(f32[40,128,128]{2,0,1:T(8,128)S(1)} %copy_multiply_fusion) | copy-start | bytes 7864324
  18.8 50.9 %collective-permute-start.4 = (f32[40,128]{1,0:T(8,128)}, f32[40,128]{1,0:T(8,128)}, u32[]{:S(2)}, u32[]{:S(2)}) collective-permute-start(f32[40,128]{1,0:T(8,128)} %get-tuple-element.621), channel_id=1, source_target_pairs={{4,0},{8,4},{12,8},{16,12},{20,16},{24,20},{28,24},{32,28},{36,32}... | collective-permute-start | bytes 61448 | tf_op jit(solution)/shard_map/ppermute | solution.py:178
  23.8 46.8 %collective-permute-start.5 = (f32[40,128]{1,0:T(8,128)}, f32[40,128]{1,0:T(8,128)}, u32[]{:S(2)}, u32[]{:S(2)}) collective-permute-start(f32[40,128]{1,0:T(8,128)} %get-tuple-element.620), channel_id=1, source_target_pairs={{0,4},{4,8},{8,12},{12,16},{16,20},{20,24},{24,28},{28,32},{32,36}... | collective-permute-start | bytes 61448 | tf_op jit(solution)/shard_map/ppermute | solution.py:179
  29.5 42.2 %collective-permute-start.6 = (f32[40,128]{1,0:T(8,128)S(1)}, f32[40,128]{1,0:T(8,128)}, u32[]{:S(2)}, u32[]{:S(2)}) collective-permute-start(f32[40,128]{1,0:T(8,128)S(1)} %bitcast.837), channel_id=1, source_target_pairs={{1,0},{2,1},{3,2},{0,3},{5,4},{6,5},{7,6},{4,7},{9,8},{10,9},{11,1... | collective-permute-start | bytes 61448 | tf_op jit(solution)/shard_map/ppermute | solution.py:180
  34.8 7.1 %collective-permute-start.3 = (f32[14,162,17]{1,0,2:T(8,128)}, f32[14,162,17]{1,0,2:T(8,128)S(1)}, u32[]{:S(2)}, u32[]{:S(2)}) collective-permute-start(f32[14,162,17]{1,0,2:T(8,128)} %copy.2278), channel_id=1, source_target_pairs={{1,0},{2,1},{3,2},{0,3},{5,4},{6,5},{7,6},{4,7},{9,8},{10,9},{11,1... | collective-permute-start | bytes 462680 | tf_op jit(solution)/shard_map/ppermute | solution.py:28
  36.7 10.1 %collective-permute-start.2 = (f32[14,162,17]{1,0,2:T(8,128)}, f32[14,162,17]{1,0,2:T(8,128)}, u32[]{:S(2)}, u32[]{:S(2)}) collective-permute-start(f32[14,162,17]{1,0,2:T(8,128)} %copy.2277), channel_id=1, source_target_pairs={{0,1},{1,2},{2,3},{3,0},{4,5},{5,6},{6,7},{7,4},{8,9},{9,10},{10,1... | collective-permute-start | bytes 462680 | tf_op jit(solution)/shard_map/ppermute | solution.py:26
  41.9 36.2 %collective-permute-start.7 = (f32[40,128]{1,0:T(8,128)}, f32[40,128]{1,0:T(8,128)}, u32[]{:S(2)}, u32[]{:S(2)}) collective-permute-start(f32[40,128]{1,0:T(8,128)} %bitcast.15), channel_id=1, source_target_pairs={{0,1},{1,2},{2,3},{3,0},{4,5},{5,6},{6,7},{7,4},{8,9},{9,10},{10,1... | collective-permute-start | bytes 61448 | tf_op jit(solution)/shard_map/ppermute | solution.py:181
  53.4 6.8 copy-start.122
  58.8 14.0 %collective-permute-start.8 = (f32[1,480]{1,0:T(1,128)S(1)}, f32[1,480]{1,0:T(1,128)S(1)}, u32[]{:S(2)}, u32[]{:S(2)}) collective-permute-start(f32[1,480]{1,0:T(1,128)S(1)} %broadcast_in_dim_reshape_reshape.6), channel_id=1, source_target_pairs={{0,1},{1,0},{2,3},{3,2},{4,5},{5,4},{6,7},{7,6},{8,9},{9,8},{10,11... | collective-permute-start | bytes 5768 | tf_op jit(solution)/shard_map/ppermute | solution.py:58
  60.3 9.3 %copy-start.116 = (f32[128,128]{1,0:T(8,128)}, f32[128,128]{1,0:T(8,128)S(1)}, u32[]{:S(2)}) copy-start(f32[128,128]{1,0:T(8,128)S(1)} %get-tuple-element.593) | copy-start | bytes 196612
  60.3 9.3 %copy-start.118 = (f32[128,128]{1,0:T(8,128)}, f32[128,128]{1,0:T(8,128)S(1)}, u32[]{:S(2)}) copy-start(f32[128,128]{1,0:T(8,128)S(1)} %get-tuple-element.594) | copy-start | bytes 196612
  60.3 10.2 %copy-start.120 = (f32[128,128]{1,0:T(8,128)}, f32[128,128]{1,0:T(8,128)S(1)}, u32[]{:S(2)}) copy-start(f32[128,128]{1,0:T(8,128)S(1)} %get-tuple-element.595) | copy-start | bytes 196612
  60.3 11.2 %copy-start.106 = (f32[128,128]{1,0:T(8,128)}, f32[128,128]{1,0:T(8,128)S(1)}, u32[]{:S(2)}) copy-start(f32[128,128]{1,0:T(8,128)S(1)} %get-tuple-element.596) | copy-start | bytes 196612
  60.4 12.3 %copy-start.108 = (f32[128,128]{1,0:T(8,128)}, f32[128,128]{1,0:T(8,128)S(1)}, u32[]{:S(2)}) copy-start(f32[128,128]{1,0:T(8,128)S(1)} %get-tuple-element.597) | copy-start | bytes 196612
  60.4 9.3 %copy-start.38 = (f32[40,128,128]{2,0,1:T(8,128)S(1)}, f32[40,128,128]{2,0,1:T(8,128)}, u32[]{:S(2)}) copy-start(f32[40,128,128]{2,0,1:T(8,128)} %copy-done.37) | copy-start | bytes 7864324
  72.8 5.2 collective-permute-start.9
  78.0 1.3 collective-permute-start.10
  79.3 9.6 %copy-start.146 = (f32[160]{0:T(256)S(1)}, f32[160]{0:T(256)}, u32[]{:S(2)}) copy-start(f32[160]{0:T(256)} %broadcast_select_fusion.3) | copy-start | bytes 1924
  79.3 4.0 collective-permute-start.11
  83.3 5.5 collective-permute-start.12
  88.8 5.0 collective-permute-start.13
  93.9 87.7 %collective-permute-start.14 = (f32[16,4,480]{2,1,0:T(4,128)S(1)}, f32[16,4,480]{2,1,0:T(4,128)S(1)}, u32[]{:S(2)}, u32[]{:S(2)}) collective-permute-start(f32[16,4,480]{2,1,0:T(4,128)S(1)} %maximum_select_fusion.2), channel_id=1, source_target_pairs={{0,64},{4,68},{8,72},{12,76},{16,80},{20,84},{24,88},{28,92},{32,9... | collective-permute-start | bytes 368648 | tf_op jit(solution)/shard_map/ppermute | solution.py:58
  182.2 65.9 %copy-start.62 = (f32[40,6,1,128]{3,2,1,0:T(1,128)}, f32[40,6,1,128]{3,2,1,0:T(1,128)S(1)}, u32[]{:S(2)}) copy-start(f32[40,6,1,128]{3,2,1,0:T(1,128)S(1)} %get-tuple-element.766) | copy-start | bytes 368644
  182.2 65.9 %copy-start.63 = (f32[40,6,1,128]{3,2,1,0:T(1,128)}, f32[40,6,1,128]{3,2,1,0:T(1,128)S(1)}, u32[]{:S(2)}) copy-start(f32[40,6,1,128]{3,2,1,0:T(1,128)S(1)} %get-tuple-element.767) | copy-start | bytes 368644
  206.2 131.8 %copy-start.4 = (f32[40,40,128]{2,1,0:T(8,128)}, f32[40,40,128]{2,1,0:T(8,128)S(1)}, u32[]{:S(2)}) copy-start(f32[40,40,128]{2,1,0:T(8,128)S(1)} %copy.2296) | copy-start | bytes 2457604
  209.3 130.9 %copy-start.2 = (f32[40,40,128]{2,1,0:T(8,128)}, f32[40,40,128]{2,1,0:T(8,128)S(1)}, u32[]{:S(2)}) copy-start(f32[40,40,128]{2,1,0:T(8,128)S(1)} %copy.2294) | copy-start | bytes 2457604
  212.4 130.0 %copy-start = (f32[40,40,128]{2,1,0:T(8,128)}, f32[40,40,128]{2,1,0:T(8,128)S(1)}, u32[]{:S(2)}) copy-start(f32[40,40,128]{2,1,0:T(8,128)S(1)} %copy.2292) | copy-start | bytes 2457604
  215.9 6.1 copy-start.102
  215.9 8.2 %copy-start.103 = (f32[40,12,128]{2,0,1:T(8,128)S(1)}, f32[40,12,128]{2,0,1:T(8,128)}, u32[]{:S(2)}) copy-start(f32[40,12,128]{2,0,1:T(8,128)} %copy.2291) | copy-start | bytes 737284
  215.9 10.2 %copy-start.6 = (f32[40,40,128]{2,1,0:T(8,128)S(1)}, f32[40,40,128]{2,1,0:T(8,128)}, u32[]{:S(2)}) copy-start(f32[40,40,128]{2,1,0:T(8,128)} %copy.2298) | copy-start | bytes 2457604
  215.9 10.2 %copy-start.20 = (f32[40,40,128]{2,1,0:T(8,128)S(1)}, f32[40,40,128]{2,1,0:T(8,128)}, u32[]{:S(2)}) copy-start(f32[40,40,128]{2,1,0:T(8,128)} %copy.2285) | copy-start | bytes 2457604
  215.9 10.2 %copy-start.104 = (f32[40,12,128]{2,0,1:T(8,128)S(1)}, f32[40,12,128]{2,0,1:T(8,128)}, u32[]{:S(2)}) copy-start(f32[40,12,128]{2,0,1:T(8,128)} %copy.2289) | copy-start | bytes 737284
  215.9 10.2 %copy-start.105 = (f32[40,6,2,128]{3,0,2,1:T(8,128)S(1)}, f32[40,6,2,128]{3,0,2,1:T(8,128)}, u32[]{:S(2)}) copy-start(f32[40,6,2,128]{3,0,2,1:T(8,128)} %pad_maximum_fusion.11) | copy-start | bytes 737284
  302.8 5.3 copy-start.69
  344.7 5.9 copy-start.129
  348.7 5.7 copy-start.40
  360.2 1.4 collective-permute-start.16
  360.2 6.4 collective-permute-start.15
  371.4 3.8 collective-permute-start.18
  373.6 3.7 collective-permute-start.17
  383.4 10.6 %copy-start.60 = (f32[6,2,128,128]{3,0,2,1:T(8,128)}, f32[6,2,128,128]{3,0,2,1:T(8,128)S(1)}, u32[]{:S(2)}) copy-start(f32[6,2,128,128]{3,0,2,1:T(8,128)S(1)} %fusion.61) | copy-start | bytes 2359300
  383.5 2.6 collective-permute-start.20
  383.5 7.8 %collective-permute-start.19 = (f32[6,2,16,128]{3,0,2,1:T(8,128)S(1)}, f32[6,2,16,128]{3,0,2,1:T(8,128)S(1)}, u32[]{:S(2)}, u32[]{:S(2)}) collective-permute-start(f32[6,2,16,128]{3,0,2,1:T(8,128)S(1)} %get-tuple-element.630), channel_id=1, source_target_pairs={{0,4},{4,8},{8,12},{12,16},{16,20},{20,24},{24,28},{28,32},{32,36}... | collective-permute-start | bytes 294920 | tf_op jit(solution)/shard_map/ppermute | solution.py:26
  386.0 5.3 copy-start.110
  396.5 6.0 collective-permute-start.22
  399.9 7.6 %collective-permute-start.21 = (f32[6,2,160,16]{2,3,1,0:T(8,128)}, f32[6,2,160,16]{2,3,1,0:T(8,128)}, u32[]{:S(2)}, u32[]{:S(2)}) collective-permute-start(f32[6,2,160,16]{2,3,1,0:T(8,128)} %copy.2318), channel_id=1, source_target_pairs={{0,1},{1,2},{2,3},{3,0},{4,5},{5,6},{6,7},{7,4},{8,9},{9,10},{10,1... | collective-permute-start | bytes 368648 | tf_op jit(solution)/shard_map/ppermute | solution.py:26
  418.7 26.8 %copy-start.43 = (f32[160,160]{1,0:T(8,128)S(1)}, f32[160,160]{1,0:T(8,128)}, u32[]{:S(2)}) copy-start(f32[160,160]{1,0:T(8,128)} %copy-done.42) | copy-start | bytes 307204
  418.8 26.8 %copy-start.45 = (f32[160,160]{1,0:T(8,128)S(1)}, f32[160,160]{1,0:T(8,128)}, u32[]{:S(2)}) copy-start(f32[160,160]{1,0:T(8,128)} %copy-done.44) | copy-start | bytes 307204
  418.8 26.8 %copy-start.47 = (f32[160,160]{1,0:T(8,128)S(1)}, f32[160,160]{1,0:T(8,128)}, u32[]{:S(2)}) copy-start(f32[160,160]{1,0:T(8,128)} %copy-done.46) | copy-start | bytes 307204
  418.8 26.8 %copy-start.49 = (f32[160,160]{1,0:T(8,128)S(1)}, f32[160,160]{1,0:T(8,128)}, u32[]{:S(2)}) copy-start(f32[160,160]{1,0:T(8,128)} %copy-done.48) | copy-start | bytes 307204
  418.9 3.7 collective-permute-start.23
  422.6 5.2 collective-permute-start.24
  427.8 1.3 collective-permute-start.25
  429.0 3.8 collective-permute-start.26
  432.9 5.5 collective-permute-start.27
  438.4 4.5 collective-permute-start.28
  444.5 89.3 %collective-permute-start.29 = (f32[16,4,480]{2,1,0:T(4,128)}, f32[16,4,480]{2,1,0:T(4,128)}, u32[]{:S(2)}, u32[]{:S(2)}) collective-permute-start(f32[16,4,480]{2,1,0:T(4,128)} %maximum_select_fusion.3), channel_id=1, source_target_pairs={{0,64},{4,68},{8,72},{12,76},{16,80},{20,84},{24,88},{28,92},{32,9... | collective-permute-start | bytes 368648 | tf_op jit(solution)/shard_map/ppermute | solution.py:58
  667.0 4.8 copy-start.73
  667.0 4.8 copy-start.75
  667.0 4.8 copy-start.79
  667.0 4.8 copy-start.81
  (209 other events, 413.7 us)
Sparse Core Ops, SparseCore 0:
  84.8 77.2 all-gather.2

commit v4 on v3

--- a/solution.py
+++ b/solution.py
@@ -198,7 +198,7 @@
         [self_block, next_x_block, prev_x_block, next_y_block, prev_y_block, squeeze_number * gram_block]
     )
     tile_total = gx_count * gy_count
-    all_blocks = jnp.moveaxis(lax.all_gather(block_set, ("gx", "gy")), 0, -1)
+    all_blocks = lax.all_gather(block_set, ("gx", "gy"), axis=3)
 
     def coarse_image(search):
         halves = search.reshape(basis_total, mode_count, 2, tile_total)
@@ -223,9 +223,8 @@
     residual_wide = force_wide
     for outer_step in range(ITERS):
         if outer_step > 0:
-            padded = padded_2(solution, (("gx", 2), ("gy", 3)), 1) * unit_mask
-            owned_resid = forcing - apply_operator(padded, owned_edges, owned_diag)
-            residual_wide = padded_2(owned_resid, (("gx", 2), ("gy", 3)), MARGIN)
+            solution_deep = padded_2(solution, (("gx", 2), ("gy", 3)), deep_width) * plate_columns(deep_width, tile_cols)
+            residual_wide = force_wide - apply_operator(solution_deep, wide_edges, wide_diag)
             residual_wide = residual_wide * plate_columns(MARGIN, tile_cols)
         residual = residual_wide[:, :, MARGIN:-MARGIN, MARGIN:-MARGIN]
         local_part = local_solve(residual_wide, wide_edges, wide_diag, inside)[

time: 701 us -> 669 us (0.954)
  local copies, waits for them, and re-layouts: 176 us -> 163 us
  waiting for transfers between devices: 50.1 us -> 39 us
  other arithmetic: 381 us -> 373 us
    reduce_sum x83, other arithmetic: 177 us -> 192 us  [coarse_image(): term = jnp.sum(block[:, :, None, :] * vectors[None, :, :, :], axis=1)]
    while x200, local copies, waits for them, and re-layouts: 57.1 us -> 69.6 us
    reduce_sum x28, other arithmetic: 14.1 us -> 5.06 us  [body(): squares = jnp.sum(image_halves * image_halves, axis=(0, 2, 3))]
    neg x14, other arithmetic: 14.7 us -> 7.47 us  [coarse_image(): -halves[:, :, 1]]
    unnamed x291 -> x279, local copies, waits for them, and re-layouts: 19.2 us -> 17 us
  transfers between devices with their start and end apart: 31 -> 27, of which waited for: 18 -> 15; matrix products, arithmetic and copies ran while one was open for 26% -> 26% of each run, Pallas kernels for 0% -> 0%
where the time goes in v4:
time: 669 us; the launch traced here: 658 us
  other arithmetic  373 us (56%)
  local copies, waits for them, and re-layouts  163 us (24%)
  waiting for transfers between devices  39 us (6%)
  matrix products  32.8 us (5%)
  starting transfers between devices  29.1 us (4%)
  between operations  18 us (3%)
    reduce_sum x83, other arithmetic, coarse_image(): term = jnp.sum(block[:, :, None, :] * vectors[None, :, :, :], axis=1)  192 us
    while x200, local copies, waits for them, and re-layouts  69.6 us
    sub x40, other arithmetic, sweep(): defect = residual - apply_operator(padded, edge_set, diagonal)  59.6 us
    ppermute x14, waiting for transfers between devices, tree_gather(): other = lax.ppermute(values, axis, [(i, i ^ stride) for i in range(count)])  30.4 us
    mul x11, local copies, waits for them, and re-layouts, coarse_image(): term = jnp.sum(block[:, :, None, :] * vectors[None, :, :, :], axis=1)  28.4 us
    add x40, other arithmetic, sweep(): return iterate + step_scale * jnp.stack([update_real, update_imag], axis=1)  25.9 us
    reduce_sum x14, other arithmetic, body(): jnp.sum(image_halves[:, :, 0] * search_halves[:, :, 0] + image_halves[:,...  19.2 us
    unnamed x279, local copies, waits for them, and re-layouts  17 us
  transfers between devices with their start and end apart: 27, of which 15 were waited for; matrix products, arithmetic and copies ran while one was open for 26% of the time, Pallas kernels for 0%

profile of v4, /device:TPU:16, one launch (start us, length us, event | category | flops | bytes accessed | tf_op | source)
XLA Modules:
  0.0 658.0 jit_solution(6492031655958410882)
XLA Ops:
  9.2 5.7 collective-permute-start.1
  15.5 3.3 copy_multiply_fusion
  20.1 2.4 fusion.223
  30.0 2.5 copy.2052
  32.5 3.0 collective-permute-done.2
  39.2 2.4 copy.2049
  41.6 2.8 maximum_multiply_fusion.6
  48.2 3.5 fusion.23
  51.8 3.7 collective-permute-start.8
  55.7 9.3 %fusion.49 = f32[6,40,40]{2,1,0:T(8,128)S(1)} fusion(f32[40,128,128]{2,0,1:T(8,128)} %copy-done.36, f32[128,128]{1,0:T(8,128)S(1)} %get-tuple-element.587, f32[128,128]{1,0:T(8,128)S(1)} %get-tuple-element.586, f32[128,128]{1,0:T(8,128)S(1)} %get-tuple-element.585, f32[128,128]{1,0:T(8,128)S(1)} %get-tuple-element.584, f32[128,128]{1,0:T(8,128)S(1)} %get-tuple-element.583), kind=kOutput, calls=%fused_computation.165 | convolution fusion | flops 320471040 | bytes 5591040 | tf_op jit(solution)/shard_map/dot_general | solution.py:170
  68.2 5.1 collective-permute-done.9
  79.9 4.2 collective-permute-done.12
  85.3 3.1 collective-permute-done.13
  88.5 2.3 collective-permute-start.14
  90.8 84.4 %while.26 = (s32[]{:T(128)}, f32[6,2,160,160]{3,2,1,0:T(8,128)S(1)}, f32[160,160]{1,0:T(8,128)S(1)}, f32[160,160]{1,0:T(8,128)S(1)}, f32[160,160]{1,0:T(8,128)S(...) while((s32[]{:T(128)}, ...), condition=%wide.region_1.2_spmd.clone, body=%wide.region_0.1_spmd.clone.sunk | while | flops 6604803 | bytes 21606556 | solution.py:102
  175.2 2.7 copy.2050
  185.9 10.5 %slice_bitcast_fusion.4 = (f32[40,40,128]{1,0,2:T(8,128)}, f32[40,40,128]{1,0,2:T(8,128)}, f32[40,40,128]{1,0,2:T(8,128)}, f32[40,40,128]{1,0,2:T(8,128)}, f32[4...) fusion(f32[6,40,40,128]{2,1,0,3:T(8,128)} %all-gather.2.cloned.1.call-done), kind=kLoop, calls=%fused_computation.144 | loop fusion | bytes 9830400 | tf_op jit(solution)/shard_map/mul | solution.py:216
  196.4 3.0 copy.2059
  201.3 2.8 copy.2063
  204.1 3.1 copy.2065
  207.2 3.1 copy.2054
  210.3 3.2 copy.2067
  213.5 3.6 multiply_reduce_fusion.82
  217.1 3.3 multiply_reduce_fusion.81
  224.5 4.7 multiply_reduce_fusion.78
  232.7 3.2 multiply_reduce_fusion.77
  245.0 2.2 multiply_reduce_fusion.72
  250.8 3.2 multiply_reduce_fusion.71
  263.0 2.4 multiply_reduce_fusion.66
  269.9 3.2 multiply_reduce_fusion.65
  282.1 2.2 multiply_reduce_fusion.60
  289.6 3.2 multiply_reduce_fusion.59
  301.8 2.2 multiply_reduce_fusion.54
  309.3 3.2 multiply_reduce_fusion.53
  321.5 2.4 multiply_reduce_fusion.48
  328.4 3.2 multiply_reduce_fusion.47
  338.6 2.2 multiply_reduce_fusion.43
  349.0 5.5 fusion.39
  354.6 5.1 collective-permute-start.16
  359.7 2.7 collective-permute-done.15
  374.7 2.7 copy.2085
  377.4 2.8 maximum_multiply_fusion.4
  381.8 4.7 fusion.31
  389.2 3.5 fusion.21
  397.4 4.2 collective-permute-done.20
  403.0 3.7 collective-permute-done.22
  406.9 5.4 collective-permute-done.23
  412.9 3.6 copy.2087
  418.6 97.5 %while.27 = (s32[]{:T(128)}, f32[6,2,160,160]{3,2,1,0:T(8,128)S(1)}, f32[160,160]{1,0:T(8,128)}, f32[160,160]{1,0:T(8,128)}, f32[160,160]{1,0:T(8,128)}, /*index...) while((s32[]{:T(128)}, ...), condition=%wide.region_73.74_spmd.clone, body=%wide.region_72.73_spmd.clone.sunk | while | flops 6604803 | bytes 22835440 | solution.py:102
  516.1 2.7 copy.2088
  530.7 2.2 multiply_reduce_fusion.37
  537.0 3.2 multiply_reduce_fusion.35
  547.2 2.4 multiply_reduce_fusion.31
  553.5 3.2 multiply_reduce_fusion.29
  563.7 2.2 multiply_reduce_fusion.25
  571.3 3.2 multiply_reduce_fusion.23
  581.5 2.2 multiply_reduce_fusion.19
  588.6 3.2 multiply_reduce_fusion.17
  598.8 2.4 multiply_reduce_fusion.13
  606.1 3.2 multiply_reduce_fusion.11
  614.2 2.2 multiply_reduce_fusion.8
  624.0 3.2 multiply_reduce_fusion.5
  632.0 2.2 multiply_reduce_fusion.2
  644.7 5.3 fusion.40
  (1088 shorter events, 423.7 us)
Async XLA Ops:
  6.5 179.3 %all-gather.2.cloned.1.call-start = ((), (), s32[]{:S(2)}) async-start(), calls=%async_computation | async-start | bytes 15851520 | tf_op jit(solution)/shard_map/all_gather | solution.py:201
  9.2 15.2 %collective-permute-start = (f32[14,17,128]{2,1,0:T(8,128)}, f32[14,17,128]{2,1,0:T(8,128)}, u32[]{:S(2)}, u32[]{:S(2)}) collective-permute-start(f32[14,17,128]{2,1,0:T(8,128)} %get-tuple-element.621), channel_id=1, source_target_pairs={{0,4},{4,8},{8,12},{12,16},{16,20},{20,24},{24,28},{28,32},{32,36}... | collective-permute-start | bytes 365576 | tf_op jit(solution)/shard_map/ppermute | solution.py:26
  9.2 15.2 %collective-permute-start.1 = (f32[14,17,128]{2,1,0:T(8,128)}, f32[14,17,128]{2,1,0:T(8,128)}, u32[]{:S(2)}, u32[]{:S(2)}) collective-permute-start(f32[14,17,128]{2,1,0:T(8,128)} %get-tuple-element.622), channel_id=1, source_target_pairs={{4,0},{8,4},{12,8},{16,12},{20,16},{24,20},{28,24},{32,28},{36,32}... | collective-permute-start | bytes 365576 | tf_op jit(solution)/shard_map/ppermute | solution.py:28
  19.4 45.6 %collective-permute-start.4 = (f32[40,128]{1,0:T(8,128)}, f32[40,128]{1,0:T(8,128)}, u32[]{:S(2)}, u32[]{:S(2)}) collective-permute-start(f32[40,128]{1,0:T(8,128)} %get-tuple-element.614), channel_id=1, source_target_pairs={{4,0},{8,4},{12,8},{16,12},{20,16},{24,20},{28,24},{32,28},{36,32}... | collective-permute-start | bytes 61448 | tf_op jit(solution)/shard_map/ppermute | solution.py:178
  20.1 45.8 %collective-permute-start.5 = (f32[40,128]{1,0:T(8,128)}, f32[40,128]{1,0:T(8,128)}, u32[]{:S(2)}, u32[]{:S(2)}) collective-permute-start(f32[40,128]{1,0:T(8,128)} %get-tuple-element.613), channel_id=1, source_target_pairs={{0,4},{4,8},{8,12},{12,16},{16,20},{20,24},{24,28},{28,32},{32,36}... | collective-permute-start | bytes 61448 | tf_op jit(solution)/shard_map/ppermute | solution.py:179
  23.9 43.2 %collective-permute-start.6 = (f32[40,128]{1,0:T(8,128)}, f32[40,128]{1,0:T(8,128)}, u32[]{:S(2)}, u32[]{:S(2)}) collective-permute-start(f32[40,128]{1,0:T(8,128)} %bitcast.837), channel_id=1, source_target_pairs={{1,0},{2,1},{3,2},{0,3},{5,4},{6,5},{7,6},{4,7},{9,8},{10,9},{11,1... | collective-permute-start | bytes 61448 | tf_op jit(solution)/shard_map/ppermute | solution.py:180
  27.2 8.3 %collective-permute-start.2 = (f32[14,162,17]{1,0,2:T(8,128)}, f32[14,162,17]{1,0,2:T(8,128)S(1)}, u32[]{:S(2)}, u32[]{:S(2)}) collective-permute-start(f32[14,162,17]{1,0,2:T(8,128)} %copy.2046), channel_id=1, source_target_pairs={{0,1},{1,2},{2,3},{3,0},{4,5},{5,6},{6,7},{7,4},{8,9},{9,10},{10,1... | collective-permute-start | bytes 462680 | tf_op jit(solution)/shard_map/ppermute | solution.py:26
  29.5 9.7 %collective-permute-start.3 = (f32[14,162,17]{1,0,2:T(8,128)S(1)}, f32[14,162,17]{1,0,2:T(8,128)}, u32[]{:S(2)}, u32[]{:S(2)}) collective-permute-start(f32[14,162,17]{1,0,2:T(8,128)S(1)} %copy.2047), channel_id=1, source_target_pairs={{1,0},{2,1},{3,2},{0,3},{5,4},{6,5},{7,6},{4,7},{9,8},{10,9},{11,1... | collective-permute-start | bytes 462680 | tf_op jit(solution)/shard_map/ppermute | solution.py:28
  35.6 37.9 %collective-permute-start.7 = (f32[40,128]{1,0:T(8,128)S(1)}, f32[40,128]{1,0:T(8,128)}, u32[]{:S(2)}, u32[]{:S(2)}) collective-permute-start(f32[40,128]{1,0:T(8,128)S(1)} %bitcast.838), channel_id=1, source_target_pairs={{0,1},{1,2},{2,3},{3,0},{4,5},{5,6},{6,7},{7,4},{8,9},{9,10},{10,1... | collective-permute-start | bytes 61448 | tf_op jit(solution)/shard_map/ppermute | solution.py:181
  46.8 8.6 %copy-start.126 = (s32[128,128]{1,0:T(8,128)S(1)}, s32[128,128]{1,0:T(8,128)}, u32[]{:S(2)}) copy-start(s32[128,128]{1,0:T(8,128)} %param.11) | copy-start | bytes 196612
  51.8 16.3 %collective-permute-start.8 = (f32[1,480]{1,0:T(1,128)S(1)}, f32[1,480]{1,0:T(1,128)S(1)}, u32[]{:S(2)}, u32[]{:S(2)}) collective-permute-start(f32[1,480]{1,0:T(1,128)S(1)} %broadcast_in_dim_reshape_reshape.6), channel_id=1, source_target_pairs={{0,1},{1,0},{2,3},{3,2},{4,5},{5,4},{6,7},{7,6},{8,9},{9,8},{10,11... | collective-permute-start | bytes 5768 | tf_op jit(solution)/shard_map/ppermute | solution.py:58
  55.6 9.4 %copy-start.37 = (f32[40,128,128]{2,0,1:T(8,128)S(1)}, f32[40,128,128]{2,0,1:T(8,128)}, u32[]{:S(2)}) copy-start(f32[40,128,128]{2,0,1:T(8,128)} %copy-done.36) | copy-start | bytes 7864324
  55.7 17.8 %copy-start.128 = (f32[40,128,1]{1,0,2:T(8,128)S(1)}, f32[40,128,1]{1,0,2:T(8,128)}, u32[]{:S(2)}) copy-start(f32[40,128,1]{1,0,2:T(8,128)} %copy.2053) | copy-start | bytes 61444
  68.1 5.2 collective-permute-start.9
  73.3 1.3 collective-permute-start.10
  74.6 4.0 collective-permute-start.11
  78.6 5.5 collective-permute-start.12
  84.1 4.3 collective-permute-start.13
  88.5 89.4 %collective-permute-start.14 = (f32[16,4,480]{2,1,0:T(4,128)S(1)}, f32[16,4,480]{2,1,0:T(4,128)}, u32[]{:S(2)}, u32[]{:S(2)}) collective-permute-start(f32[16,4,480]{2,1,0:T(4,128)S(1)} %maximum_select_fusion.2), channel_id=1, source_target_pairs={{0,64},{4,68},{8,72},{12,76},{16,80},{20,84},{24,88},{28,92},{32,9... | collective-permute-start | bytes 368648 | tf_op jit(solution)/shard_map/ppermute | solution.py:58
  204.1 132.4 %copy-start.2 = (f32[40,40,128]{2,1,0:T(8,128)}, f32[40,40,128]{2,1,0:T(8,128)S(1)}, u32[]{:S(2)}) copy-start(f32[40,40,128]{2,1,0:T(8,128)S(1)} %copy.2063) | copy-start | bytes 2457604
  207.1 6.3 copy-start.117
  213.5 127.4 %copy-start = (f32[40,40,128]{2,1,0:T(8,128)}, f32[40,40,128]{2,1,0:T(8,128)S(1)}, u32[]{:S(2)}) copy-start(f32[40,40,128]{2,1,0:T(8,128)S(1)} %copy.2067) | copy-start | bytes 2457604
  213.5 6.9 %copy-start.118 = (f32[40,12,128]{2,0,1:T(8,128)S(1)}, f32[40,12,128]{2,0,1:T(8,128)}, u32[]{:S(2)}) copy-start(f32[40,12,128]{2,0,1:T(8,128)} %copy.2064) | copy-start | bytes 737284
  213.5 8.9 %copy-start.119 = (f32[40,12,128]{2,0,1:T(8,128)S(1)}, f32[40,12,128]{2,0,1:T(8,128)}, u32[]{:S(2)}) copy-start(f32[40,12,128]{2,0,1:T(8,128)} %copy.2066) | copy-start | bytes 737284
  213.5 11.0 %copy-start.30 = (f32[40,40,128]{2,1,0:T(8,128)S(1)}, f32[40,40,128]{2,1,0:T(8,128)}, u32[]{:S(2)}) copy-start(f32[40,40,128]{2,1,0:T(8,128)} %copy.2054) | copy-start | bytes 2457604
  213.5 11.0 %copy-start.120 = (f32[40,12,128]{2,0,1:T(8,128)S(1)}, f32[40,12,128]{2,0,1:T(8,128)}, u32[]{:S(2)}) copy-start(f32[40,12,128]{2,0,1:T(8,128)} %copy.2058) | copy-start | bytes 737284
  213.5 11.0 %copy-start.121 = (f32[40,6,2,128]{3,0,2,1:T(8,128)S(1)}, f32[40,6,2,128]{3,0,2,1:T(8,128)}, u32[]{:S(2)}) copy-start(f32[40,6,2,128]{3,0,2,1:T(8,128)} %pad_maximum_fusion.10) | copy-start | bytes 737284
  224.5 5.9 copy-start.53
  224.5 5.9 copy-start.57
  280.1 5.4 copy-start.65
  299.8 5.5 copy-start.66
  338.6 5.6 copy-start.61
  340.8 5.6 copy-start.55
  340.8 5.6 copy-start.59
  340.9 5.6 copy-start.77
  340.9 5.6 copy-start.79
  340.9 5.6 copy-start.86
  340.9 5.6 copy-start.88
  340.9 5.6 copy-start.94
  354.5 22.9 %copy-start.48 = (f32[6,2,128,128]{3,0,2,1:T(8,128)}, f32[6,2,128,128]{3,0,2,1:T(8,128)S(1)}, u32[]{:S(2)}) copy-start(f32[6,2,128,128]{3,0,2,1:T(8,128)S(1)} %fusion.39) | copy-start | bytes 2359300
  354.5 7.9 %collective-permute-start.15 = (f32[6,2,17,128]{3,0,2,1:T(8,128)S(1)}, f32[6,2,17,128]{3,0,2,1:T(8,128)S(1)}, u32[]{:S(2)}, u32[]{:S(2)}) collective-permute-start(f32[6,2,17,128]{3,0,2,1:T(8,128)S(1)} %get-tuple-element.619), channel_id=1, source_target_pairs={{0,4},{4,8},{8,12},{12,16},{16,20},{20,24},{24,28},{28,32},{32,36}... | collective-permute-start | bytes 313352 | tf_op jit(solution)/shard_map/ppermute | solution.py:26
  354.6 7.8 %collective-permute-start.16 = (f32[6,2,17,128]{3,0,2,1:T(8,128)S(1)}, f32[6,2,17,128]{3,0,2,1:T(8,128)S(1)}, u32[]{:S(2)}, u32[]{:S(2)}) collective-permute-start(f32[6,2,17,128]{3,0,2,1:T(8,128)S(1)} %get-tuple-element.620), channel_id=1, source_target_pairs={{4,0},{8,4},{12,8},{16,12},{20,16},{24,20},{28,24},{32,28},{36,32}... | collective-permute-start | bytes 313352 | tf_op jit(solution)/shard_map/ppermute | solution.py:28
  366.3 5.9 collective-permute-start.17
  368.8 6.0 collective-permute-start.18
  392.8 3.7 collective-permute-start.19
  396.5 5.2 collective-permute-start.20
  401.7 1.3 collective-permute-start.21
  402.9 3.8 collective-permute-start.22
  406.8 5.5 collective-permute-start.23
  412.3 4.5 collective-permute-start.24
  418.4 100.5 %collective-permute-start.25 = (f32[16,4,480]{2,1,0:T(4,128)}, f32[16,4,480]{2,1,0:T(4,128)}, u32[]{:S(2)}, u32[]{:S(2)}) collective-permute-start(f32[16,4,480]{2,1,0:T(4,128)} %maximum_select_fusion.3), channel_id=1, source_target_pairs={{0,64},{4,68},{8,72},{12,76},{16,80},{20,84},{24,88},{28,92},{32,9... | collective-permute-start | bytes 368648 | tf_op jit(solution)/shard_map/ppermute | solution.py:58
  521.2 4.9 copy-start.10
  528.5 4.8 copy-start.1
  588.1 15.7 %copy-start.129 = (f32[6]{0:T(128)}, f32[6]{0:T(128)S(1)}, u32[]{:S(2)}) copy-start(f32[6]{0:T(128)S(1)} %get-tuple-element.786) | copy-start | bytes 76
  603.6 5.8 copy-start.67
  605.6 15.4 %copy-start.131 = (f32[6]{0:T(128)}, f32[6]{0:T(128)S(1)}, u32[]{:S(2)}) copy-start(f32[6]{0:T(128)S(1)} %get-tuple-element.783) | copy-start | bytes 76
  605.6 15.4 %copy-start.133 = (f32[6]{0:T(128)}, f32[6]{0:T(128)S(1)}, u32[]{:S(2)}) copy-start(f32[6]{0:T(128)S(1)} %get-tuple-element.784) | copy-start | bytes 76
  605.8 17.1 %copy-start.105 = (f32[40,6,1,128]{3,0,2,1:T(8,128)}, f32[40,6,1,128]{3,0,2,1:T(8,128)S(1)}, u32[]{:S(2)}) copy-start(f32[40,6,1,128]{3,0,2,1:T(8,128)S(1)} %get-tuple-element.520) | copy-start | bytes 368644
  605.8 17.1 %copy-start.106 = (f32[40,6,1,128]{3,0,2,1:T(8,128)}, f32[40,6,1,128]{3,0,2,1:T(8,128)S(1)}, u32[]{:S(2)}) copy-start(f32[40,6,1,128]{3,0,2,1:T(8,128)S(1)} %get-tuple-element.642) | copy-start | bytes 368644
  634.4 5.4 copy-start.124
  634.4 5.4 copy-start.125
  634.4 5.4 copy-start.136
  634.4 5.4 copy-start.139
  636.5 4.8 copy-start.72
  (199 other events, 416.9 us)
Sparse Core Ops, SparseCore 0:
  80.0 78.8 all-gather.1

commit v5 on v4

--- a/solution.py
+++ b/solution.py
@@ -198,7 +198,8 @@
         [self_block, next_x_block, prev_x_block, next_y_block, prev_y_block, squeeze_number * gram_block]
     )
     tile_total = gx_count * gy_count
-    all_blocks = lax.all_gather(block_set, ("gx", "gy"), axis=3)
+    gathered_blocks = lax.all_gather(block_set.reshape(1, -1), ("gx", "gy"), axis=0, tiled=True)
+    all_blocks = gathered_blocks.T.reshape(block_set.shape + (tile_total,))
 
     def coarse_image(search):
         halves = search.reshape(basis_total, mode_count, 2, tile_total)

time: 669 us -> 666 us (level)
    mul x11 -> x4, local copies, waits for them, and re-layouts: 28.4 us -> 0.9 us  [coarse_image(): term = jnp.sum(block[:, :, None, :] * vectors[None, :, :, :], axis=1)]
    reduce_sum x83, other arithmetic: 192 us -> 175 us  [coarse_image(): term = jnp.sum(block[:, :, None, :] * vectors[None, :, :, :], axis=1)]
    all_gather x0 -> x1, local copies, waits for them, and re-layouts: none -> 11.2 us  [body(): lax.all_gather(block_set.reshape(1, -1), ('gx', 'gy'), axis=0, tiled=True)]
    reduce_sum x28, other arithmetic: 5.06 us -> 13.1 us  [body(): squares = jnp.sum(image_halves * image_halves, axis=(0, 2, 3))]
    unnamed x279 -> x300, local copies, waits for them, and re-layouts: 17 us -> 19.9 us
  transfers between devices with their start and end apart: 27 -> 27, of which waited for: 15 -> 14; matrix products, arithmetic and copies ran while one was open for 26% -> 27% of each run, Pallas kernels for 0% -> 0%
where the time goes in v5:
time: 666 us; the launch traced here: 655 us
  other arithmetic  377 us (57%)
  local copies, waits for them, and re-layouts  158 us (24%)
  waiting for transfers between devices  36.9 us (6%)
  matrix products  32.2 us (5%)
  starting transfers between devices  29.5 us (4%)
  between operations  18 us (3%)
    reduce_sum x83, other arithmetic, coarse_image(): term = jnp.sum(block[:, :, None, :] * vectors[None, :, :, :], axis=1)  175 us
    while x200, local copies, waits for them, and re-layouts  69.2 us
    sub x40, other arithmetic, sweep(): defect = residual - apply_operator(padded, edge_set, diagonal)  59.6 us
    ppermute x14, waiting for transfers between devices, tree_gather(): other = lax.ppermute(values, axis, [(i, i ^ stride) for i in range(count)])  29.7 us
    add x40, other arithmetic, sweep(): return iterate + step_scale * jnp.stack([update_real, update_imag], axis=1)  26.7 us
    unnamed x300, local copies, waits for them, and re-layouts  19.9 us
    reduce_sum x14, other arithmetic, body(): jnp.sum(image_halves[:, :, 0] * search_halves[:, :, 0] + image_halves[:,...  19.8 us
    dot_general x6, matrix products, pair(): lax.dot_general(left, right, (((1,), (1,)), ((), ())), precision=highest,...  15.1 us
  transfers between devices with their start and end apart: 27, of which 14 were waited for; matrix products, arithmetic and copies ran while one was open for 27% of the time, Pallas kernels for 0%

profile of v5, /device:TPU:16, one launch (start us, length us, event | category | flops | bytes accessed | tf_op | source)
XLA Modules:
  0.0 654.9 jit_solution(17983235330731507897)
XLA Ops:
  9.2 5.7 collective-permute-start.1
  15.5 3.3 copy_multiply_fusion
  19.6 2.4 fusion.224
  28.9 2.5 copy.2007
  31.5 3.1 collective-permute-done.2
  38.1 2.4 copy.2004
  40.5 2.8 maximum_multiply_fusion.6
  46.7 3.5 fusion.23
  50.2 3.7 collective-permute-start.8
  54.1 9.3 %fusion.49 = f32[6,40,40]{2,1,0:T(8,128)S(1)} fusion(f32[40,128,128]{2,0,1:T(8,128)} %copy-done.38, f32[128,128]{1,0:T(8,128)S(1)} %get-tuple-element.587, f32[128,128]{1,0:T(8,128)S(1)} %get-tuple-element.586, f32[128,128]{1,0:T(8,128)S(1)} %get-tuple-element.585, f32[128,128]{1,0:T(8,128)S(1)} %get-tuple-element.584, f32[128,128]{1,0:T(8,128)S(1)} %get-tuple-element.583), kind=kOutput, calls=%fused_computation.159 | convolution fusion | flops 320471040 | bytes 5591040 | tf_op jit(solution)/shard_map/dot_general | solution.py:170
  66.6 5.1 collective-permute-done.9
  73.2 2.2 fusion.54
  79.1 3.4 collective-permute-done.12
  83.7 3.1 collective-permute-done.13
  86.9 2.3 collective-permute-start.14
  89.2 84.5 %while.26 = (s32[]{:T(128)}, f32[6,2,160,160]{3,2,1,0:T(8,128)S(1)}, f32[160,160]{1,0:T(8,128)S(1)}, f32[160,160]{1,0:T(8,128)S(1)}, f32[160,160]{1,0:T(8,128)S(...) while((s32[]{:T(128)}, ...), condition=%wide.region_1.2_spmd.clone, body=%wide.region_0.1_spmd.clone.sunk | while | flops 6604803 | bytes 21606556 | solution.py:102
  173.7 2.6 copy.2005
  182.8 11.2 %copy.2009 = f32[128,1,9600]{0,2,1:T(8,128)} copy(f32[128,1,9600]{2,1,0:T(1,128)} %all-gather.3.cloned.1.call-done) | data formatting | bytes 9830400 | tf_op jit(solution)/shard_map/all_gather | solution.py:201
  193.9 2.8 fusion.223
  205.0 5.0 multiply_reduce_fusion.78
  215.9 2.1 multiply_reduce_fusion.76
  218.1 2.1 multiply_reduce_fusion.75
  224.5 2.2 multiply_reduce_fusion.72
  232.7 2.1 multiply_reduce_fusion.70
  241.3 2.2 multiply_reduce_fusion.66
  260.1 2.4 multiply_reduce_fusion.60
  281.1 2.2 multiply_reduce_fusion.54
  293.2 2.1 multiply_reduce_fusion.52
  299.8 2.2 multiply_reduce_fusion.49
  319.8 2.5 multiply_reduce_fusion.43
  331.8 4.9 fusion.39
  336.8 5.1 collective-permute-start.16
  341.9 2.7 collective-permute-done.15
  348.0 2.5 copy.2032
  350.5 2.5 copy.2033
  353.0 2.2 collective-permute-start.18
  356.6 2.7 copy.2034
  359.3 2.7 copy.2035
  361.9 3.2 maximum_multiply_fusion.4
  366.9 4.4 fusion.31
  373.4 3.5 fusion.21
  377.1 2.5 collective-permute-start.19
  382.3 4.0 collective-permute-done.20
  387.7 3.7 collective-permute-done.22
  391.5 5.4 collective-permute-done.23
  397.4 3.6 copy.2037
  403.2 98.2 %while.27 = (s32[]{:T(128)}, f32[6,2,160,160]{3,2,1,0:T(8,128)S(1)}, f32[160,160]{1,0:T(8,128)}, f32[160,160]{1,0:T(8,128)}, f32[160,160]{1,0:T(8,128)}, /*index...) while((s32[]{:T(128)}, ...), condition=%wide.region_73.74_spmd.clone, body=%wide.region_72.73_spmd.clone.sunk | while | flops 6604803 | bytes 22835440 | solution.py:102
  501.4 2.7 copy.2038
  511.4 2.1 multiply_reduce_fusion.39
  516.0 2.2 multiply_reduce_fusion.37
  526.4 2.1 multiply_reduce_fusion.34
  528.6 2.1 multiply_reduce_fusion.33
  533.0 2.2 multiply_reduce_fusion.31
  543.2 2.1 multiply_reduce_fusion.28
  545.4 2.1 multiply_reduce_fusion.27
  549.8 2.4 multiply_reduce_fusion.25
  562.4 2.1 multiply_reduce_fusion.22
  564.6 2.1 multiply_reduce_fusion.21
  569.0 2.2 multiply_reduce_fusion.19
  604.3 2.1 multiply_reduce_fusion.10
  606.5 2.1 multiply_reduce_fusion.9
  608.7 2.4 multiply_reduce_fusion.8
  629.0 2.2 multiply_reduce_fusion.2
  641.6 5.3 fusion.40
  (1104 shorter events, 439.9 us)
Async XLA Ops:
  6.5 176.2 %all-gather.3.cloned.1.call-start = ((), (), s32[]{:S(2)}) async-start(), calls=%async_computation | async-start | bytes 4953600 | tf_op jit(solution)/shard_map/all_gather | solution.py:201
  7.4 11.4 %copy-start.111 = (f32[1,128,128]{2,1,0:T(8,128)}, f32[1,128,128]{2,1,0:T(8,128)S(1)}, u32[]{:S(2)}) copy-start(f32[1,128,128]{2,1,0:T(8,128)S(1)} %fusion.169) | copy-start | bytes 196612
  9.2 14.0 %collective-permute-start = (f32[14,17,128]{2,1,0:T(8,128)}, f32[14,17,128]{2,1,0:T(8,128)}, u32[]{:S(2)}, u32[]{:S(2)}) collective-permute-start(f32[14,17,128]{2,1,0:T(8,128)} %get-tuple-element.621), channel_id=1, source_target_pairs={{0,4},{4,8},{8,12},{12,16},{16,20},{20,24},{24,28},{28,32},{32,36}... | collective-permute-start | bytes 365576 | tf_op jit(solution)/shard_map/ppermute | solution.py:26
  9.2 14.0 %collective-permute-start.1 = (f32[14,17,128]{2,1,0:T(8,128)}, f32[14,17,128]{2,1,0:T(8,128)}, u32[]{:S(2)}, u32[]{:S(2)}) collective-permute-start(f32[14,17,128]{2,1,0:T(8,128)} %get-tuple-element.622), channel_id=1, source_target_pairs={{4,0},{8,4},{12,8},{16,12},{20,16},{24,20},{28,24},{32,28},{36,32}... | collective-permute-start | bytes 365576 | tf_op jit(solution)/shard_map/ppermute | solution.py:28
  18.8 44.6 %collective-permute-start.4 = (f32[40,128]{1,0:T(8,128)S(1)}, f32[40,128]{1,0:T(8,128)}, u32[]{:S(2)}, u32[]{:S(2)}) collective-permute-start(f32[40,128]{1,0:T(8,128)S(1)} %get-tuple-element.614), channel_id=1, source_target_pairs={{4,0},{8,4},{12,8},{16,12},{20,16},{24,20},{28,24},{32,28},{36,32}... | collective-permute-start | bytes 61448 | tf_op jit(solution)/shard_map/ppermute | solution.py:178
  19.6 44.8 %collective-permute-start.5 = (f32[40,128]{1,0:T(8,128)S(1)}, f32[40,128]{1,0:T(8,128)}, u32[]{:S(2)}, u32[]{:S(2)}) collective-permute-start(f32[40,128]{1,0:T(8,128)S(1)} %get-tuple-element.613), channel_id=1, source_target_pairs={{0,4},{4,8},{8,12},{12,16},{16,20},{20,24},{24,28},{28,32},{32,36}... | collective-permute-start | bytes 61448 | tf_op jit(solution)/shard_map/ppermute | solution.py:179
  22.7 42.7 %collective-permute-start.6 = (f32[40,128]{1,0:T(8,128)S(1)}, f32[40,128]{1,0:T(8,128)}, u32[]{:S(2)}, u32[]{:S(2)}) collective-permute-start(f32[40,128]{1,0:T(8,128)S(1)} %bitcast.917), channel_id=1, source_target_pairs={{1,0},{2,1},{3,2},{0,3},{5,4},{6,5},{7,6},{4,7},{9,8},{10,9},{11,1... | collective-permute-start | bytes 61448 | tf_op jit(solution)/shard_map/ppermute | solution.py:180
  26.2 8.4 %collective-permute-start.2 = (f32[14,162,17]{1,0,2:T(8,128)}, f32[14,162,17]{1,0,2:T(8,128)S(1)}, u32[]{:S(2)}, u32[]{:S(2)}) collective-permute-start(f32[14,162,17]{1,0,2:T(8,128)} %copy.2001), channel_id=1, source_target_pairs={{0,1},{1,2},{2,3},{3,0},{4,5},{5,6},{6,7},{7,4},{8,9},{9,10},{10,1... | collective-permute-start | bytes 462680 | tf_op jit(solution)/shard_map/ppermute | solution.py:26
  28.4 9.7 %collective-permute-start.3 = (f32[14,162,17]{1,0,2:T(8,128)S(1)}, f32[14,162,17]{1,0,2:T(8,128)}, u32[]{:S(2)}, u32[]{:S(2)}) collective-permute-start(f32[14,162,17]{1,0,2:T(8,128)S(1)} %copy.2002), channel_id=1, source_target_pairs={{1,0},{2,1},{3,2},{0,3},{5,4},{6,5},{7,6},{4,7},{9,8},{10,9},{11,1... | collective-permute-start | bytes 462680 | tf_op jit(solution)/shard_map/ppermute | solution.py:28
  28.9 11.6 %copy-start.112 = (f32[1,128,128]{2,1,0:T(8,128)S(1)}, f32[1,128,128]{2,1,0:T(8,128)}, u32[]{:S(2)}) copy-start(f32[1,128,128]{2,1,0:T(8,128)} %copy-done.111) | copy-start | bytes 196612
  31.5 11.9 %copy-start.149 = (f32[162]{0:T(256)}, f32[162]{0:T(256)S(1)}, u32[]{:S(2)}) copy-start(f32[162]{0:T(256)S(1)} %and_convert_fusion) | copy-start | bytes 1948
  34.6 37.2 %collective-permute-start.7 = (f32[40,128]{1,0:T(8,128)S(1)}, f32[40,128]{1,0:T(8,128)}, u32[]{:S(2)}, u32[]{:S(2)}) collective-permute-start(f32[40,128]{1,0:T(8,128)S(1)} %bitcast.918), channel_id=1, source_target_pairs={{0,1},{1,2},{2,3},{3,0},{4,5},{5,6},{6,7},{7,4},{8,9},{9,10},{10,1... | collective-permute-start | bytes 61448 | tf_op jit(solution)/shard_map/ppermute | solution.py:181
  44.9 9.0 %copy-start.125 = (s32[128,128]{1,0:T(8,128)S(1)}, s32[128,128]{1,0:T(8,128)}, u32[]{:S(2)}) copy-start(s32[128,128]{1,0:T(8,128)} %param.11) | copy-start | bytes 196612
  50.2 16.2 %collective-permute-start.8 = (f32[1,480]{1,0:T(1,128)S(1)}, f32[1,480]{1,0:T(1,128)S(1)}, u32[]{:S(2)}, u32[]{:S(2)}) collective-permute-start(f32[1,480]{1,0:T(1,128)S(1)} %broadcast_in_dim_reshape_reshape.6), channel_id=1, source_target_pairs={{0,1},{1,0},{2,3},{3,2},{4,5},{5,4},{6,7},{7,6},{8,9},{9,8},{10,11... | collective-permute-start | bytes 5768 | tf_op jit(solution)/shard_map/ppermute | solution.py:58
  54.1 9.3 %copy-start.39 = (f32[40,128,128]{2,0,1:T(8,128)S(1)}, f32[40,128,128]{2,0,1:T(8,128)}, u32[]{:S(2)}) copy-start(f32[40,128,128]{2,0,1:T(8,128)} %copy-done.38) | copy-start | bytes 7864324
  66.5 5.2 collective-permute-start.9
  71.7 1.3 collective-permute-start.10
  73.0 4.0 collective-permute-start.11
  77.0 5.5 collective-permute-start.12
  82.5 4.3 collective-permute-start.13
  86.9 89.5 %collective-permute-start.14 = (f32[16,4,480]{2,1,0:T(4,128)S(1)}, f32[16,4,480]{2,1,0:T(4,128)S(1)}, u32[]{:S(2)}, u32[]{:S(2)}) collective-permute-start(f32[16,4,480]{2,1,0:T(4,128)S(1)} %maximum_select_fusion.2), channel_id=1, source_target_pairs={{0,64},{4,68},{8,72},{12,76},{16,80},{20,84},{24,88},{28,92},{32,9... | collective-permute-start | bytes 368648 | tf_op jit(solution)/shard_map/ppermute | solution.py:58
  182.0 45.0 %copy-start.66 = (f32[40,6,1,128]{3,2,1,0:T(1,128)}, f32[40,6,1,128]{3,2,1,0:T(1,128)S(1)}, u32[]{:S(2)}) copy-start(f32[40,6,1,128]{3,2,1,0:T(1,128)S(1)} %get-tuple-element.753) | copy-start | bytes 368644
  182.0 45.0 %copy-start.67 = (f32[40,6,1,128]{3,2,1,0:T(1,128)}, f32[40,6,1,128]{3,2,1,0:T(1,128)S(1)}, u32[]{:S(2)}) copy-start(f32[40,6,1,128]{3,2,1,0:T(1,128)S(1)} %get-tuple-element.754) | copy-start | bytes 368644
  193.9 4.9 copy-start.114
  196.7 8.3 %copy-start.4 = (f32[1600,128]{1,0:T(8,128)}, f32[1600,128]{1,0:T(8,128)S(1)}, u32[]{:S(2)}) copy-start(f32[1600,128]{1,0:T(8,128)S(1)} %get-tuple-element.607) | copy-start | bytes 2457604
  196.7 8.3 %copy-start.18 = (f32[1600,128]{1,0:T(8,128)}, f32[1600,128]{1,0:T(8,128)S(1)}, u32[]{:S(2)}) copy-start(f32[1600,128]{1,0:T(8,128)S(1)} %get-tuple-element.603) | copy-start | bytes 2457604
  196.7 114.0 %copy-start.32 = (f32[1600,128]{1,0:T(8,128)}, f32[1600,128]{1,0:T(8,128)S(1)}, u32[]{:S(2)}) copy-start(f32[1600,128]{1,0:T(8,128)S(1)} %get-tuple-element.608) | copy-start | bytes 2457604
  196.7 120.9 %copy-start.2 = (f32[1600,128]{1,0:T(8,128)}, f32[1600,128]{1,0:T(8,128)S(1)}, u32[]{:S(2)}) copy-start(f32[1600,128]{1,0:T(8,128)S(1)} %get-tuple-element.606) | copy-start | bytes 2457604
  196.7 123.0 %copy-start = (f32[1600,128]{1,0:T(8,128)}, f32[1600,128]{1,0:T(8,128)S(1)}, u32[]{:S(2)}) copy-start(f32[1600,128]{1,0:T(8,128)S(1)} %get-tuple-element.605) | copy-start | bytes 2457604
  196.8 6.2 copy-start.116
  196.8 8.2 %copy-start.117 = (f32[40,12,128]{2,0,1:T(8,128)S(1)}, f32[40,12,128]{2,0,1:T(8,128)}, u32[]{:S(2)}) copy-start(f32[40,12,128]{2,0,1:T(8,128)} %copy.2013) | copy-start | bytes 737284
  196.8 8.2 %copy-start.118 = (f32[40,6,2,128]{3,0,2,1:T(8,128)S(1)}, f32[40,6,2,128]{3,0,2,1:T(8,128)}, u32[]{:S(2)}) copy-start(f32[40,6,2,128]{3,0,2,1:T(8,128)} %pad_maximum_fusion.10) | copy-start | bytes 737284
  279.0 7.1 %copy-start.76 = (f32[40,12,128]{2,0,1:T(8,128)S(1)}, f32[40,12,128]{2,0,1:T(8,128)}, u32[]{:S(2)}) copy-start(f32[40,12,128]{2,0,1:T(8,128)} %copy.2024) | copy-start | bytes 737284
  319.8 6.3 copy-start.123
  319.8 6.3 copy-start.124
  319.8 6.3 copy-start.146
  319.8 6.3 copy-start.148
  322.3 5.8 copy-start.131
  326.2 5.6 copy-start.41
  336.7 7.9 %copy-start.62 = (f32[6,2,128,128]{3,0,2,1:T(8,128)}, f32[6,2,128,128]{3,0,2,1:T(8,128)S(1)}, u32[]{:S(2)}) copy-start(f32[6,2,128,128]{3,0,2,1:T(8,128)S(1)} %fusion.39) | copy-start | bytes 2359300
  336.7 7.9 %collective-permute-start.15 = (f32[6,2,17,128]{3,0,2,1:T(8,128)S(1)}, f32[6,2,17,128]{3,0,2,1:T(8,128)S(1)}, u32[]{:S(2)}, u32[]{:S(2)}) collective-permute-start(f32[6,2,17,128]{3,0,2,1:T(8,128)S(1)} %get-tuple-element.619), channel_id=1, source_target_pairs={{0,4},{4,8},{8,12},{12,16},{16,20},{20,24},{24,28},{28,32},{32,36}... | collective-permute-start | bytes 313352 | tf_op jit(solution)/shard_map/ppermute | solution.py:26
  336.8 7.8 %collective-permute-start.16 = (f32[6,2,17,128]{3,0,2,1:T(8,128)S(1)}, f32[6,2,17,128]{3,0,2,1:T(8,128)S(1)}, u32[]{:S(2)}, u32[]{:S(2)}) collective-permute-start(f32[6,2,17,128]{3,0,2,1:T(8,128)S(1)} %get-tuple-element.620), channel_id=1, source_target_pairs={{4,0},{8,4},{12,8},{16,12},{20,16},{24,20},{28,24},{32,28},{36,32}... | collective-permute-start | bytes 313352 | tf_op jit(solution)/shard_map/ppermute | solution.py:28
  350.5 11.5 %copy-start.150 = (f32[162]{0:T(256)S(1)}, f32[162]{0:T(256)}, u32[]{:S(2)}) copy-start(f32[162]{0:T(256)} %copy-done.149) | copy-start | bytes 1948
  350.5 6.1 collective-permute-start.17
  353.0 6.3 collective-permute-start.18
  377.0 26.3 %copy-start.45 = (f32[160,160]{1,0:T(8,128)S(1)}, f32[160,160]{1,0:T(8,128)}, u32[]{:S(2)}) copy-start(f32[160,160]{1,0:T(8,128)} %copy-done.43) | copy-start | bytes 307204
  377.0 26.3 %copy-start.48 = (f32[160,160]{1,0:T(8,128)S(1)}, f32[160,160]{1,0:T(8,128)}, u32[]{:S(2)}) copy-start(f32[160,160]{1,0:T(8,128)} %copy-done.46) | copy-start | bytes 307204
  377.0 26.3 %copy-start.51 = (f32[160,160]{1,0:T(8,128)S(1)}, f32[160,160]{1,0:T(8,128)}, u32[]{:S(2)}) copy-start(f32[160,160]{1,0:T(8,128)} %copy-done.49) | copy-start | bytes 307204
  377.0 26.2 %copy-start.54 = (f32[160,160]{1,0:T(8,128)S(1)}, f32[160,160]{1,0:T(8,128)}, u32[]{:S(2)}) copy-start(f32[160,160]{1,0:T(8,128)} %copy-done.52) | copy-start | bytes 307204
  377.1 4.0 collective-permute-start.19
  381.2 5.2 collective-permute-start.20
  386.4 1.3 collective-permute-start.21
  387.6 3.8 collective-permute-start.22
  391.5 5.5 collective-permute-start.23
  397.0 4.5 collective-permute-start.24
  403.0 101.1 %collective-permute-start.25 = (f32[16,4,480]{2,1,0:T(4,128)}, f32[16,4,480]{2,1,0:T(4,128)}, u32[]{:S(2)}, u32[]{:S(2)}) collective-permute-start(f32[16,4,480]{2,1,0:T(4,128)} %maximum_select_fusion.3), channel_id=1, source_target_pairs={{0,64},{4,68},{8,72},{12,76},{16,80},{20,84},{24,88},{28,92},{32,9... | collective-permute-start | bytes 368648 | tf_op jit(solution)/shard_map/ppermute | solution.py:58
  506.5 4.9 copy-start.11
  518.4 19.1 %copy-start.68 = (f32[40,6,1,128]{3,2,1,0:T(1,128)}, f32[40,6,1,128]{3,2,1,0:T(1,128)S(1)}, u32[]{:S(2)}) copy-start(f32[40,6,1,128]{3,2,1,0:T(1,128)S(1)} %get-tuple-element.703) | copy-start | bytes 368644
  518.5 19.1 %copy-start.70 = (f32[40,6,1,128]{3,2,1,0:T(1,128)}, f32[40,6,1,128]{3,2,1,0:T(1,128)S(1)}, u32[]{:S(2)}) copy-start(f32[40,6,1,128]{3,2,1,0:T(1,128)S(1)} %get-tuple-element.704) | copy-start | bytes 368644
  590.2 6.9 %copy-start.77 = (f32[40,12,128]{2,0,1:T(8,128)S(1)}, f32[40,12,128]{2,0,1:T(8,128)}, u32[]{:S(2)}) copy-start(f32[40,12,128]{2,0,1:T(8,128)} %copy.2053) | copy-start | bytes 737284
  631.3 5.4 copy-start.121
  631.3 5.4 copy-start.122
  631.3 5.4 copy-start.140
  631.3 5.4 copy-start.143
  (209 other events, 390.0 us)
Sparse Core Ops, SparseCore 0:
  79.2 66.4 all-gather.2

commit v6 on v5

--- a/solution.py
+++ b/solution.py
@@ -1,6 +1,8 @@
 import jax
 import jax.numpy as jnp
 from jax import lax
+from jax.experimental import pallas as pl
+from jax.experimental.pallas import tpu as pltpu
 from jax.sharding import PartitionSpec as P
 
 MARGIN = 16
@@ -88,18 +90,65 @@
     return diagonal * centre - beside_all + squeeze_number * turned
 
 
+INTERPRET = False
+
+
+def sweep_kernel(resid_ref, north_ref, south_ref, east_ref, west_ref, diag_ref, real_ref, scale_ref, out_ref):
+    pairs, _, rows, lanes = out_ref.shape
+    out_ref[...] = jnp.zeros(out_ref.shape, jnp.float32)
+
+    def sweep(sweep_index, carry):
+        for pair_index in range(pairs):
+            centre_real = out_ref[pair_index, 0]
+            centre_imag = out_ref[pair_index, 1]
+            defects = []
+            for part, (centre, turned) in enumerate(((centre_real, -centre_imag), (centre_imag, centre_real))):
+                beside = (
+                    north_ref[...] * pltpu.roll(centre, rows - 1, 0)
+                    + south_ref[...] * pltpu.roll(centre, 1, 0)
+                    + east_ref[...] * pltpu.roll(centre, lanes - 1, 1)
+                    + west_ref[...] * pltpu.roll(centre, 1, 1)
+                )
+                applied = diag_ref[...] * centre - beside + squeeze_number * turned
+                defects.append(resid_ref[pair_index, part] - applied)
+            real_diag = real_ref[...]
+            step_scale = scale_ref[...]
+            update_real = real_diag * defects[0] + squeeze_number * defects[1]
+            update_imag = real_diag * defects[1] - squeeze_number * defects[0]
+            out_ref[pair_index, 0] = centre_real + step_scale * update_real
+            out_ref[pair_index, 1] = centre_imag + step_scale * update_imag
+        return carry
+
+    lax.fori_loop(0, SWEEPS, sweep, 0)
+
+
 def local_solve(residual, edge_set, diagonal, inside):
     real_diag = jnp.where(inside > 0, diagonal, 1.0)
     step_scale = relaxation * inside / (real_diag * real_diag + squeeze_number * squeeze_number)
-
-    def sweep(sweep_index, iterate):
-        padded = jnp.pad(iterate, ((0, 0), (0, 0), (1, 1), (1, 1)))
-        defect = residual - apply_operator(padded, edge_set, diagonal)
-        update_real = real_diag * defect[:, 0] + squeeze_number * defect[:, 1]
-        update_imag = real_diag * defect[:, 1] - squeeze_number * defect[:, 0]
-        return iterate + step_scale * jnp.stack([update_real, update_imag], axis=1)
-
-    return lax.fori_loop(0, SWEEPS, sweep, jnp.zeros_like(residual))
+    rows, cols = diagonal.shape
+    lanes = -(-cols // 128) * 128
+    row_ids = jnp.arange(rows)[:, None]
+    col_ids = jnp.arange(cols)[None, :]
+    north_edge, south_edge, east_edge, west_edge = edge_set
+    fields = [
+        north_edge * (row_ids < rows - 1),
+        south_edge * (row_ids > 0),
+        east_edge * (col_ids < cols - 1),
+        west_edge * (col_ids > 0),
+        diagonal,
+        real_diag,
+        step_scale,
+    ]
+    widen = lambda field: jnp.pad(field, [(0, 0)] * (field.ndim - 1) + [(0, lanes - cols)])
+    vmem = pl.BlockSpec(memory_space=pltpu.VMEM)
+    result = pl.pallas_call(
+        sweep_kernel,
+        out_shape=jax.ShapeDtypeStruct(residual.shape[:2] + (rows, lanes), jnp.float32),
+        in_specs=[vmem] * 8,
+        out_specs=vmem,
+        interpret=INTERPRET,
+    )(widen(residual), *[widen(field.astype(jnp.float32)) for field in fields])
+    return result[..., :cols]
 
 
 def complex_scale(alpha_real, alpha_imag, vectors):

time: 666 us -> 584 us (0.88)
  other arithmetic: 377 us -> 271 us
  Pallas kernels: 0 us -> 78.2 us
  local copies, waits for them, and re-layouts: 158 us -> 109 us
  waiting for transfers between devices: 36.9 us -> 48.5 us
  matrix products: 32.2 us -> 24.4 us
    pallas_call x0 -> x2, Pallas kernels: none -> 78.2 us  [local_solve(): pl.pallas_call(sweep_kernel, out_shape=jax.ShapeDtypeStruct(residual.shap...]
    while x202 -> x0, local copies, waits for them, and re-layouts: 74.5 us -> none
    sub x40 -> x0, other arithmetic: 59.6 us -> none  [sweep(): defect = residual - apply_operator(padded, edge_set, diagonal)]
    add x80 -> x2, other arithmetic: 36 us -> 4.26 us  [body(): solution = solution + local_part + prolong(own_coarse)]
    ppermute x14, waiting for transfers between devices: 29.7 us -> 41.8 us  [tree_gather(): other = lax.ppermute(values, axis, [(i, i ^ stride) for i in range(count)])]
    pad x0 -> x9, local copies, waits for them, and re-layouts: none -> 10.8 us  [local_solve(): jnp.pad(field, [(0, 0)] * (field.ndim - 1) + [(0, lanes - cols)])]
    while x40 -> x0, other arithmetic: 9.04 us -> none
    unnamed x300 -> x227, local copies, waits for them, and re-layouts: 19.9 us -> 18.4 us
  transfers between devices with their start and end apart: 27 -> 27, of which waited for: 14 -> 15; matrix products, arithmetic and copies ran while one was open for 27% -> 11% of each run, Pallas kernels for 0% -> 14%
where the time goes in v6:
time: 584 us; the launch traced here: 575 us
  other arithmetic  271 us (46%)
  local copies, waits for them, and re-layouts  109 us (19%)
  Pallas kernels  78.2 us (13%)
  waiting for transfers between devices  48.5 us (8%)
  starting transfers between devices  26.7 us (5%)
  matrix products  24.4 us (4%)
  between operations  17.3 us (3%)
    reduce_sum x83, other arithmetic, coarse_image(): term = jnp.sum(block[:, :, None, :] * vectors[None, :, :, :], axis=1)  179 us
    pallas_call x2, Pallas kernels, local_solve(): pl.pallas_call(sweep_kernel, out_shape=jax.ShapeDtypeStruct(residual.shap...  78.2 us
    ppermute x14, waiting for transfers between devices, tree_gather(): other = lax.ppermute(values, axis, [(i, i ^ stride) for i in range(count)])  41.8 us
    reduce_sum x14, other arithmetic, body(): jnp.sum(image_halves[:, :, 0] * search_halves[:, :, 0] + image_halves[:,...  21 us
    unnamed x227, local copies, waits for them, and re-layouts  18.4 us
    neg x14, other arithmetic, coarse_image(): -halves[:, :, 1]  14.1 us
    reduce_sum x28, other arithmetic, body(): squares = jnp.sum(image_halves * image_halves, axis=(0, 2, 3))  11.8 us
    ppermute x4, starting transfers between devices, padded_2(): lax.ppermute(head, axis, [((i + 1) % count, i) for i in range(count)])  11.8 us
  transfers between devices with their start and end apart: 27, of which 15 were waited for; matrix products, arithmetic and copies ran while one was open for 11% of the time, Pallas kernels for 14%

profile of v6, /device:TPU:16, one launch (start us, length us, event | category | flops | bytes accessed | tf_op | source)
XLA Modules:
  0.0 575.0 jit_solution(6517710738385969335)
XLA Ops:
  8.6 5.7 collective-permute-start.1
  15.0 3.3 copy_multiply_fusion
  21.5 2.6 copy.1962
  25.5 2.6 copy.1963
  28.9 3.1 fusion.206
  32.0 3.1 copy.1968
  35.6 3.1 copy.1967
  40.5 2.4 copy.1964
  42.9 2.5 copy.1965
  45.4 2.8 maximum_multiply_fusion
  49.9 3.2 fusion.39
  57.1 2.2 fusion.44
  60.1 2.2 slice.880
  64.6 3.8 fusion.15
  68.4 2.6 collective-permute-start.8
  73.7 4.0 collective-permute-done.9
  79.2 3.7 collective-permute-done.11
  83.1 5.3 collective-permute-done.12
  88.5 4.2 collective-permute-done.13
  96.7 3.1 pad.40.resid_ref
  104.6 38.9 %shard_map.55 = f32[6,2,160,256]{3,2,1,0:T(8,128)} custom-call(f32[6,2,160,256]{3,2,1,0:T(8,128)} %pad.40.resid_ref, f32[160,256]{1,0:T(8,128)} %pad.41.north_ref, f32[160,256]{1,0:T(8,128)} %pad.42.south_ref, f32[160,256]{1,0:T(8,128)} %pad.43.east_ref, f32[160,256]{1,0:T(8,128)} %pad.44.west_ref, f32[160,256]{1,0:T(8,128)} %pad.45.diag_ref, ...), custom_call_target="tpu_custom_call" | custom-call | tf_op jit(solution)/shard_map/pallas_call | solution.py:144
  149.8 11.3 %copy.1969 = f32[128,1,9600]{0,2,1:T(8,128)} copy(f32[128,1,9600]{2,1,0:T(1,128)} %all-gather.3.cloned.1.call-done) | data formatting | bytes 9830400 | tf_op jit(solution)/shard_map/all_gather | solution.py:250
  161.2 2.8 fusion.205
  173.0 4.8 multiply_reduce_fusion.78
  181.3 3.2 multiply_reduce_fusion.77
  193.5 2.2 multiply_reduce_fusion.72
  199.4 3.2 multiply_reduce_fusion.71
  211.5 2.4 multiply_reduce_fusion.66
  215.2 2.1 fusion.129
  230.5 2.2 multiply_reduce_fusion.60
  234.5 2.1 fusion.121
  250.5 2.2 multiply_reduce_fusion.54
  255.6 2.2 fusion.113
  269.5 2.4 multiply_reduce_fusion.49
  276.9 2.2 fusion.105
  290.9 2.2 multiply_reduce_fusion.43
  304.7 4.9 fusion.18
  311.4 5.1 collective-permute-start.16
  316.5 2.8 collective-permute-done.15
  326.1 2.4 copy.1994
  330.0 2.3 copy.1995
  332.3 2.5 collective-permute-done.18
  334.8 2.3 copy.1996
  337.2 2.9 maximum_multiply_fusion.1
  340.8 2.2 fusion.28
  346.0 3.5 fusion.13
  351.1 2.2 collective-permute-done.19
  353.3 5.1 collective-permute-done.20
  359.8 3.7 collective-permute-done.22
  363.6 5.4 collective-permute-done.23
  369.2 4.3 collective-permute-done.24
  374.2 3.0 pad.49.resid_ref
  377.2 39.3 %shard_map.56 = f32[6,2,160,256]{3,2,1,0:T(8,128)} custom-call(f32[6,2,160,256]{3,2,1,0:T(8,128)} %pad.49.resid_ref, f32[160,256]{1,0:T(8,128)} %pad.41.north_ref, f32[160,256]{1,0:T(8,128)} %pad.42.south_ref, f32[160,256]{1,0:T(8,128)} %pad.43.east_ref, f32[160,256]{1,0:T(8,128)} %pad.44.west_ref, f32[160,256]{1,0:T(8,128)} %pad.45.diag_ref, ...), custom_call_target="tpu_custom_call" | custom-call | tf_op jit(solution)/shard_map/pallas_call | solution.py:144
  436.9 2.2 multiply_reduce_fusion.36
  442.6 3.2 multiply_reduce_fusion.35
  454.7 2.2 multiply_reduce_fusion.30
  460.6 3.2 multiply_reduce_fusion.29
  472.8 2.4 multiply_reduce_fusion.24
  488.8 2.2 multiply_reduce_fusion.19
  508.7 2.2 multiply_reduce_fusion.13
  530.0 2.4 multiply_reduce_fusion.7
  550.6 2.2 multiply_reduce_fusion.1
  562.1 3.2 fusion.17
  565.3 2.6 fusion.55
  (636 shorter events, 283.8 us)
Async XLA Ops:
  6.5 13.1 %copy-start.71 = (f32[128,128]{1,0:T(8,128)S(1)}, f32[128,128]{1,0:T(8,128)}, u32[]{:S(2)}) copy-start(f32[128,128]{1,0:T(8,128)} %param.6) | copy-start | bytes 196612
  6.5 13.1 %copy-start.34 = (f32[6,2,128,128]{3,2,1,0:T(8,128)S(1)}, f32[6,2,128,128]{3,2,1,0:T(8,128)}, u32[]{:S(2)}) copy-start(f32[6,2,128,128]{3,2,1,0:T(8,128)} %param.5) | copy-start | bytes 2359300
  6.5 143.2 %all-gather.3.cloned.1.call-start = ((), (), s32[]{:S(2)}) async-start(), calls=%async_computation | async-start | bytes 4953600 | tf_op jit(solution)/shard_map/all_gather | solution.py:250
  8.5 11.1 %collective-permute-start = (f32[14,17,128]{2,1,0:T(8,128)S(1)}, f32[14,17,128]{2,1,0:T(8,128)S(1)}, u32[]{:S(2)}, u32[]{:S(2)}) collective-permute-start(f32[14,17,128]{2,1,0:T(8,128)S(1)} %get-tuple-element.133), channel_id=1, source_target_pairs={{0,4},{4,8},{8,12},{12,16},{16,20},{20,24},{24,28},{28,32},{32,36}... | collective-permute-start | bytes 365576 | tf_op jit(solution)/shard_map/ppermute | solution.py:28
  8.6 11.0 %collective-permute-start.1 = (f32[14,17,128]{2,1,0:T(8,128)S(1)}, f32[14,17,128]{2,1,0:T(8,128)S(1)}, u32[]{:S(2)}, u32[]{:S(2)}) collective-permute-start(f32[14,17,128]{2,1,0:T(8,128)S(1)} %get-tuple-element.134), channel_id=1, source_target_pairs={{4,0},{8,4},{12,8},{16,12},{20,16},{24,20},{28,24},{32,28},{36,32}... | collective-permute-start | bytes 365576 | tf_op jit(solution)/shard_map/ppermute | solution.py:30
  15.0 49.5 %copy-start.105 = (f32[40]{0:T(128)}, f32[40]{0:T(128)S(1)}, u32[]{:S(2)}) copy-start(f32[40]{0:T(128)S(1)} %compare_convert_fusion) | copy-start | bytes 484
  18.9 34.3 %collective-permute-start.4 = (f32[40,128]{1,0:T(8,128)}, f32[40,128]{1,0:T(8,128)}, u32[]{:S(2)}, u32[]{:S(2)}) collective-permute-start(f32[40,128]{1,0:T(8,128)} %get-tuple-element.126), channel_id=1, source_target_pairs={{4,0},{8,4},{12,8},{16,12},{20,16},{24,20},{28,24},{32,28},{36,32}... | collective-permute-start | bytes 61448 | tf_op jit(solution)/shard_map/ppermute | solution.py:227
  19.6 34.5 %collective-permute-start.5 = (f32[40,128]{1,0:T(8,128)}, f32[40,128]{1,0:T(8,128)}, u32[]{:S(2)}, u32[]{:S(2)}) collective-permute-start(f32[40,128]{1,0:T(8,128)} %get-tuple-element.125), channel_id=1, source_target_pairs={{0,4},{4,8},{8,12},{12,16},{16,20},{20,24},{24,28},{28,32},{32,36}... | collective-permute-start | bytes 61448 | tf_op jit(solution)/shard_map/ppermute | solution.py:228
  24.2 14.5 %collective-permute-start.2 = (f32[14,162,17]{1,0,2:T(8,128)}, f32[14,162,17]{1,0,2:T(8,128)}, u32[]{:S(2)}, u32[]{:S(2)}) collective-permute-start(f32[14,162,17]{1,0,2:T(8,128)} %copy.1962), channel_id=1, source_target_pairs={{0,1},{1,2},{2,3},{3,0},{4,5},{5,6},{6,7},{7,4},{8,9},{9,10},{10,1... | collective-permute-start | bytes 462680 | tf_op jit(solution)/shard_map/ppermute | solution.py:28
  28.1 14.8 %collective-permute-start.3 = (f32[14,162,17]{1,0,2:T(8,128)}, f32[14,162,17]{1,0,2:T(8,128)}, u32[]{:S(2)}, u32[]{:S(2)}) collective-permute-start(f32[14,162,17]{1,0,2:T(8,128)} %copy.1963), channel_id=1, source_target_pairs={{1,0},{2,1},{3,2},{0,3},{5,4},{6,5},{7,6},{4,7},{9,8},{10,9},{11,1... | collective-permute-start | bytes 462680 | tf_op jit(solution)/shard_map/ppermute | solution.py:30
  35.1 20.1 %collective-permute-start.6 = (f32[40,128]{1,0:T(8,128)}, f32[40,128]{1,0:T(8,128)}, u32[]{:S(2)}, u32[]{:S(2)}) collective-permute-start(f32[40,128]{1,0:T(8,128)} %bitcast.908), channel_id=1, source_target_pairs={{1,0},{2,1},{3,2},{0,3},{5,4},{6,5},{7,6},{4,7},{9,8},{10,9},{11,1... | collective-permute-start | bytes 61448 | tf_op jit(solution)/shard_map/ppermute | solution.py:229
  38.7 11.2 %copy-start.108 = (f32[162]{0:T(256)}, f32[162]{0:T(256)S(1)}, u32[]{:S(2)}) copy-start(f32[162]{0:T(256)S(1)} %and_convert_fusion) | copy-start | bytes 1948
  38.7 17.5 %collective-permute-start.7 = (f32[40,128]{1,0:T(8,128)}, f32[40,128]{1,0:T(8,128)}, u32[]{:S(2)}, u32[]{:S(2)}) collective-permute-start(f32[40,128]{1,0:T(8,128)} %bitcast.909), channel_id=1, source_target_pairs={{0,1},{1,2},{2,3},{3,0},{4,5},{5,6},{6,7},{7,4},{8,9},{9,10},{10,1... | collective-permute-start | bytes 61448 | tf_op jit(solution)/shard_map/ppermute | solution.py:230
  68.4 4.1 collective-permute-start.8
  72.6 5.2 collective-permute-start.9
  77.8 1.3 collective-permute-start.10
  79.0 3.9 collective-permute-start.11
  82.9 5.5 collective-permute-start.12
  88.4 4.3 collective-permute-start.13
  92.8 50.7 %collective-permute-start.14 = (f32[16,4,480]{2,1,0:T(4,128)S(1)}, f32[16,4,480]{2,1,0:T(4,128)S(1)}, u32[]{:S(2)}, u32[]{:S(2)}) collective-permute-start(f32[16,4,480]{2,1,0:T(4,128)S(1)} %maximum_select_fusion.2), channel_id=1, source_target_pairs={{0,64},{4,68},{8,72},{12,76},{16,80},{20,84},{24,88},{28,92},{32,9... | collective-permute-start | bytes 368648 | tf_op jit(solution)/shard_map/ppermute | solution.py:60
  161.1 7.8 %copy-start.76 = (f32[40,12,128]{2,0,1:T(8,128)S(1)}, f32[40,12,128]{2,0,1:T(8,128)}, u32[]{:S(2)}) copy-start(f32[40,12,128]{2,0,1:T(8,128)} %copy.1976) | copy-start | bytes 737284
  161.1 9.8 %copy-start.77 = (f32[40,12,128]{2,0,1:T(8,128)S(1)}, f32[40,12,128]{2,0,1:T(8,128)}, u32[]{:S(2)}) copy-start(f32[40,12,128]{2,0,1:T(8,128)} %copy.1977) | copy-start | bytes 737284
  163.9 14.1 %copy-start.14 = (f32[1600,128]{1,0:T(8,128)}, f32[1600,128]{1,0:T(8,128)S(1)}, u32[]{:S(2)}) copy-start(f32[1600,128]{1,0:T(8,128)S(1)} %get-tuple-element.122) | copy-start | bytes 2457604
  164.0 9.0 %copy-start.78 = (f32[40,12,128]{2,0,1:T(8,128)S(1)}, f32[40,12,128]{2,0,1:T(8,128)}, u32[]{:S(2)}) copy-start(f32[40,12,128]{2,0,1:T(8,128)} %copy.1973) | copy-start | bytes 737284
  164.0 9.0 %copy-start.79 = (f32[40,6,2,128]{3,0,2,1:T(8,128)S(1)}, f32[40,6,2,128]{3,0,2,1:T(8,128)}, u32[]{:S(2)}) copy-start(f32[40,6,2,128]{3,0,2,1:T(8,128)} %pad_maximum_fusion.10) | copy-start | bytes 737284
  187.1 8.9 %copy-start.39 = (f32[40,12,128]{2,0,1:T(8,128)S(1)}, f32[40,12,128]{2,0,1:T(8,128)}, u32[]{:S(2)}) copy-start(f32[40,12,128]{2,0,1:T(8,128)} %copy-done.38) | copy-start | bytes 737284
  234.5 7.5 %copy-start.4 = (f32[1600,128]{1,0:T(8,128)S(1)}, f32[1600,128]{1,0:T(8,128)}, u32[]{:S(2)}) copy-start(f32[1600,128]{1,0:T(8,128)} %copy-done) | copy-start | bytes 2457604
  237.3 6.8 %copy-start.94 = (f32[6]{0:T(128)}, f32[6]{0:T(128)S(1)}, u32[]{:S(2)}) copy-start(f32[6]{0:T(128)S(1)} %get-tuple-element.322) | copy-start | bytes 76
  255.6 7.4 %copy-start.5 = (f32[1600,128]{1,0:T(8,128)S(1)}, f32[1600,128]{1,0:T(8,128)}, u32[]{:S(2)}) copy-start(f32[1600,128]{1,0:T(8,128)} %copy-done) | copy-start | bytes 2457604
  258.4 6.8 %copy-start.99 = (f32[6]{0:T(128)}, f32[6]{0:T(128)S(1)}, u32[]{:S(2)}) copy-start(f32[6]{0:T(128)S(1)} %get-tuple-element.319) | copy-start | bytes 76
  276.9 7.5 %copy-start.6 = (f32[1600,128]{1,0:T(8,128)S(1)}, f32[1600,128]{1,0:T(8,128)}, u32[]{:S(2)}) copy-start(f32[1600,128]{1,0:T(8,128)} %copy-done) | copy-start | bytes 2457604
  279.7 6.8 %copy-start.103 = (f32[6]{0:T(128)}, f32[6]{0:T(128)S(1)}, u32[]{:S(2)}) copy-start(f32[6]{0:T(128)S(1)} %get-tuple-element.317) | copy-start | bytes 76
  311.3 8.0 %copy-start.30 = (f32[6,2,128,128]{3,2,1,0:T(8,128)}, f32[6,2,128,128]{3,2,1,0:T(8,128)S(1)}, u32[]{:S(2)}) copy-start(f32[6,2,128,128]{3,2,1,0:T(8,128)S(1)} %slice_add_fusion.1) | copy-start | bytes 2359300
  311.3 8.0 %collective-permute-start.15 = (f32[6,2,17,128]{3,2,1,0:T(8,128)S(1)}, f32[6,2,17,128]{3,2,1,0:T(8,128)S(1)}, u32[]{:S(2)}, u32[]{:S(2)}) collective-permute-start(f32[6,2,17,128]{3,2,1,0:T(8,128)S(1)} %get-tuple-element.135), channel_id=1, source_target_pairs={{0,4},{4,8},{8,12},{12,16},{16,20},{20,24},{24,28},{28,32},{32,36}... | collective-permute-start | bytes 313352 | tf_op jit(solution)/shard_map/ppermute | solution.py:28
  311.4 7.9 %collective-permute-start.16 = (f32[6,2,17,128]{3,2,1,0:T(8,128)S(1)}, f32[6,2,17,128]{3,2,1,0:T(8,128)S(1)}, u32[]{:S(2)}, u32[]{:S(2)}) collective-permute-start(f32[6,2,17,128]{3,2,1,0:T(8,128)S(1)} %get-tuple-element.136), channel_id=1, source_target_pairs={{4,0},{8,4},{12,8},{16,12},{20,16},{24,20},{28,24},{32,28},{36,32}... | collective-permute-start | bytes 313352 | tf_op jit(solution)/shard_map/ppermute | solution.py:30
  320.7 16.5 %copy-start.109 = (f32[162]{0:T(256)S(1)}, f32[162]{0:T(256)}, u32[]{:S(2)}) copy-start(f32[162]{0:T(256)} %copy-done.108) | copy-start | bytes 1948
  324.0 6.0 %collective-permute-start.17 = (f32[6,2,162,17]{2,1,3,0:T(2,128)S(1)}, f32[6,2,162,17]{2,1,3,0:T(2,128)}, u32[]{:S(2)}, u32[]{:S(2)}) collective-permute-start(f32[6,2,162,17]{2,1,3,0:T(2,128)S(1)} %copy.1993), channel_id=1, source_target_pairs={{0,1},{1,2},{2,3},{3,0},{4,5},{5,6},{6,7},{7,4},{8,9},{9,10},{10,1... | collective-permute-start | bytes 396584 | tf_op jit(solution)/shard_map/ppermute | solution.py:28
  328.5 6.3 %collective-permute-start.18 = (f32[6,2,162,17]{2,1,3,0:T(2,128)}, f32[6,2,162,17]{2,1,3,0:T(2,128)}, u32[]{:S(2)}, u32[]{:S(2)}) collective-permute-start(f32[6,2,162,17]{2,1,3,0:T(2,128)} %copy.1994), channel_id=1, source_target_pairs={{1,0},{2,1},{3,2},{0,3},{5,4},{6,5},{7,6},{4,7},{9,8},{10,9},{11,1... | collective-permute-start | bytes 396584 | tf_op jit(solution)/shard_map/ppermute | solution.py:30
  332.3 8.4 %copy-start.73 = (f32[160,160]{1,0:T(8,128)S(1)}, f32[160,160]{1,0:T(8,128)}, u32[]{:S(2)}) copy-start(f32[160,160]{1,0:T(8,128)} %copy-done.72) | copy-start | bytes 307204
  349.6 3.7 collective-permute-start.19
  353.2 5.2 collective-permute-start.20
  358.4 1.3 collective-permute-start.21
  359.7 3.8 collective-permute-start.22
  363.5 5.5 collective-permute-start.23
  369.1 4.4 collective-permute-start.24
  373.5 42.9 %copy-start.88 = (f32[16,4,480]{2,1,0:T(4,128)}, f32[16,4,480]{2,1,0:T(4,128)S(1)}, u32[]{:S(2)}) copy-start(f32[16,4,480]{2,1,0:T(4,128)S(1)} %maximum_select_fusion.3) | copy-start | bytes 368644
  373.5 42.9 %collective-permute-start.25 = (f32[16,4,480]{2,1,0:T(4,128)S(1)}, f32[16,4,480]{2,1,0:T(4,128)}, u32[]{:S(2)}, u32[]{:S(2)}) collective-permute-start(f32[16,4,480]{2,1,0:T(4,128)S(1)} %maximum_select_fusion.3), channel_id=1, source_target_pairs={{0,64},{4,68},{8,72},{12,76},{16,80},{20,84},{24,88},{28,92},{32,9... | collective-permute-start | bytes 368648 | tf_op jit(solution)/shard_map/ppermute | solution.py:60
  419.5 10.2 %copy-start.65 = (f32[480,128]{1,0:T(8,128)}, f32[480,128]{1,0:T(8,128)S(1)}, u32[]{:S(2)}) copy-start(f32[480,128]{1,0:T(8,128)S(1)} %copy.1998) | copy-start | bytes 737284
  420.3 7.4 %copy-start.19 = (f32[1600,128]{1,0:T(8,128)S(1)}, f32[1600,128]{1,0:T(8,128)}, u32[]{:S(2)}) copy-start(f32[1600,128]{1,0:T(8,128)} %copy-done.14) | copy-start | bytes 2457604
  436.8 20.5 %copy-start.35 = (f32[40,6,1,128]{3,2,1,0:T(1,128)}, f32[40,6,1,128]{3,2,1,0:T(1,128)S(1)}, u32[]{:S(2)}) copy-start(f32[40,6,1,128]{3,2,1,0:T(1,128)S(1)} %get-tuple-element.217) | copy-start | bytes 368644
  436.8 20.5 %copy-start.36 = (f32[40,6,1,128]{3,2,1,0:T(1,128)}, f32[40,6,1,128]{3,2,1,0:T(1,128)S(1)}, u32[]{:S(2)}) copy-start(f32[40,6,1,128]{3,2,1,0:T(1,128)S(1)} %get-tuple-element.218) | copy-start | bytes 368644
  448.4 9.0 %copy-start.41 = (f32[40,12,128]{2,0,1:T(8,128)S(1)}, f32[40,12,128]{2,0,1:T(8,128)}, u32[]{:S(2)}) copy-start(f32[40,12,128]{2,0,1:T(8,128)} %copy-done.40) | copy-start | bytes 737284
  494.8 7.4 %copy-start.11 = (f32[1600,128]{1,0:T(8,128)S(1)}, f32[1600,128]{1,0:T(8,128)}, u32[]{:S(2)}) copy-start(f32[1600,128]{1,0:T(8,128)} %copy-done) | copy-start | bytes 2457604
  504.4 11.7 %copy-start.42 = (f32[40,12,128]{2,0,1:T(8,128)S(1)}, f32[40,12,128]{2,0,1:T(8,128)}, u32[]{:S(2)}) copy-start(f32[40,12,128]{2,0,1:T(8,128)} %copy.2010) | copy-start | bytes 737284
  516.0 7.4 %copy-start.12 = (f32[1600,128]{1,0:T(8,128)S(1)}, f32[1600,128]{1,0:T(8,128)}, u32[]{:S(2)}) copy-start(f32[1600,128]{1,0:T(8,128)} %copy-done) | copy-start | bytes 2457604
  535.3 10.8 %copy-start.37 = (f32[40,12,128]{2,0,1:T(8,128)}, f32[40,12,128]{2,0,1:T(8,128)S(1)}, u32[]{:S(2)}) copy-start(f32[40,12,128]{2,0,1:T(8,128)S(1)} %copy.2012) | copy-start | bytes 737284
  536.8 7.2 %copy-start.13 = (f32[1600,128]{1,0:T(8,128)S(1)}, f32[1600,128]{1,0:T(8,128)}, u32[]{:S(2)}) copy-start(f32[1600,128]{1,0:T(8,128)} %copy-done) | copy-start | bytes 2457604
  546.2 9.8 %copy-start.102 = (f32[6]{0:T(128)S(1)}, f32[6]{0:T(128)}, u32[]{:S(2)}) copy-start(f32[6]{0:T(128)} %copy-done.101) | copy-start | bytes 76
  548.3 10.1 %copy-start.93 = (f32[6]{0:T(128)S(1)}, f32[6]{0:T(128)}, u32[]{:S(2)}) copy-start(f32[6]{0:T(128)} %copy-done.92) | copy-start | bytes 76
  548.3 10.1 %copy-start.96 = (f32[6]{0:T(128)S(1)}, f32[6]{0:T(128)}, u32[]{:S(2)}) copy-start(f32[6]{0:T(128)} %copy-done.95) | copy-start | bytes 76
  548.3 10.1 %copy-start.98 = (f32[6]{0:T(128)S(1)}, f32[6]{0:T(128)}, u32[]{:S(2)}) copy-start(f32[6]{0:T(128)} %copy-done.97) | copy-start | bytes 76
  552.8 9.3 %copy-start.26 = (f32[40,128,128]{2,1,0:T(8,128)S(1)}, f32[40,128,128]{2,1,0:T(8,128)}, u32[]{:S(2)}) copy-start(f32[40,128,128]{2,1,0:T(8,128)} %param.8) | copy-start | bytes 7864324
  552.8 9.3 %copy-start.107 = (f32[40]{0:T(128)S(1)}, f32[40]{0:T(128)}, u32[]{:S(2)}) copy-start(f32[40]{0:T(128)} %copy-done.105) | copy-start | bytes 484
  555.1 10.3 %copy-start.31 = (f32[6,2,128,128]{3,2,1,0:T(8,128)S(1)}, f32[6,2,128,128]{3,2,1,0:T(8,128)}, u32[]{:S(2)}) copy-start(f32[6,2,128,128]{3,2,1,0:T(8,128)} %copy-done.30) | copy-start | bytes 2359300
  (73 other events, 183.1 us)
Sparse Core Ops, SparseCore 0:
  60.2 66.6 all-gather.2

commit v7 on v6

--- a/solution.py
+++ b/solution.py
@@ -244,15 +244,15 @@
     next_y_block = -pair(base_field[:, :, -1] * east_edge[:, -1], from_next_y) * has_next_y
     prev_y_block = -pair(base_field[:, :, 0] * west_edge[:, 0], from_prev_y) * has_prev_y
     block_set = jnp.stack(
-        [self_block, next_x_block, prev_x_block, next_y_block, prev_y_block, squeeze_number * gram_block]
+        [self_block.T, next_x_block.T, prev_x_block.T, next_y_block.T, prev_y_block.T, squeeze_number * gram_block.T]
     )
     tile_total = gx_count * gy_count
     gathered_blocks = lax.all_gather(block_set.reshape(1, -1), ("gx", "gy"), axis=0, tiled=True)
     all_blocks = gathered_blocks.T.reshape(block_set.shape + (tile_total,))
 
     def coarse_image(search):
-        halves = search.reshape(basis_total, mode_count, 2, tile_total)
-        turned = jnp.stack([-halves[:, :, 1], halves[:, :, 0]], axis=2).reshape(search.shape)
+        halves = search.reshape(mode_count, 2, basis_total, tile_total)
+        turned = jnp.stack([-halves[:, 1], halves[:, 0]], axis=1).reshape(search.shape)
         shifted = (
             search,
             jnp.roll(search, -gy_count, axis=-1),
@@ -263,7 +263,7 @@
         )
         total = None
         for block, vectors in zip(all_blocks, shifted):
-            term = jnp.sum(block[:, :, None, :] * vectors[None, :, :, :], axis=1)
+            term = jnp.sum(block[None, :, :, :] * vectors[:, :, None, :], axis=1)
             total = term if total is None else total + term
         return total
 
@@ -281,40 +281,40 @@
             :, :, MARGIN:-MARGIN, MARGIN:-MARGIN
         ]
         gathered = tree_gather(restrict(residual).reshape(-1), ("gy", "gx"))
-        search = gathered.reshape(tile_total, -1).T.reshape(basis_total, 2 * mode_count, tile_total)
+        search = gathered.reshape(tile_total, basis_total, 2 * mode_count).transpose(2, 1, 0)
         coarse = jnp.zeros_like(search)
         for coarse_step in range(CSTEPS):
             images = coarse_image(search)
-            image_halves = images.reshape(basis_total, mode_count, 2, tile_total)
-            search_halves = search.reshape(basis_total, mode_count, 2, tile_total)
+            image_halves = images.reshape(mode_count, 2, basis_total, tile_total)
+            search_halves = search.reshape(mode_count, 2, basis_total, tile_total)
             num_real = jnp.sum(
-                image_halves[:, :, 0] * search_halves[:, :, 0] + image_halves[:, :, 1] * search_halves[:, :, 1],
-                axis=(0, 2),
+                image_halves[:, 0] * search_halves[:, 0] + image_halves[:, 1] * search_halves[:, 1],
+                axis=(1, 2),
             )
             num_imag = jnp.sum(
-                image_halves[:, :, 0] * search_halves[:, :, 1] - image_halves[:, :, 1] * search_halves[:, :, 0],
-                axis=(0, 2),
+                image_halves[:, 0] * search_halves[:, 1] - image_halves[:, 1] * search_halves[:, 0],
+                axis=(1, 2),
             )
-            squares = jnp.sum(image_halves * image_halves, axis=(0, 2, 3))
+            squares = jnp.sum(image_halves * image_halves, axis=(1, 2, 3))
             denominator = squares + guard_value
-            alpha_real = (num_real / denominator)[None, :, None]
-            alpha_imag = (num_imag / denominator)[None, :, None]
+            alpha_real = (num_real / denominator)[:, None, None]
+            alpha_imag = (num_imag / denominator)[:, None, None]
             coarse_halves = coarse.reshape(search_halves.shape)
             coarse = jnp.stack(
                 [
-                    coarse_halves[:, :, 0] + alpha_real * search_halves[:, :, 0] - alpha_imag * search_halves[:, :, 1],
-                    coarse_halves[:, :, 1] + alpha_real * search_halves[:, :, 1] + alpha_imag * search_halves[:, :, 0],
+                    coarse_halves[:, 0] + alpha_real * search_halves[:, 0] - alpha_imag * search_halves[:, 1],
+                    coarse_halves[:, 1] + alpha_real * search_halves[:, 1] + alpha_imag * search_halves[:, 0],
                 ],
-                axis=2,
+                axis=1,
             ).reshape(search.shape)
             search = jnp.stack(
                 [
-                    search_halves[:, :, 0] - (alpha_real * image_halves[:, :, 0] - alpha_imag * image_halves[:, :, 1]),
-                    search_halves[:, :, 1] - (alpha_real * image_halves[:, :, 1] + alpha_imag * image_halves[:, :, 0]),
+                    search_halves[:, 0] - (alpha_real * image_halves[:, 0] - alpha_imag * image_halves[:, 1]),
+                    search_halves[:, 1] - (alpha_real * image_halves[:, 1] + alpha_imag * image_halves[:, 0]),
                 ],
-                axis=2,
+                axis=1,
             ).reshape(search.shape)
-        own_coarse = lax.dynamic_index_in_dim(coarse, tile_index, axis=2, keepdims=False)
+        own_coarse = lax.dynamic_index_in_dim(coarse, tile_index, axis=2, keepdims=False).T
         solution = solution + local_part + prolong(own_coarse)
     return solution
 

time: 584 us -> 543 us (0.930)
  other arithmetic: 271 us -> 183 us
  local copies, waits for them, and re-layouts: 109 us -> 149 us
    reduce_sum x125 -> x123, other arithmetic: 212 us -> 116 us  [the longest x81 78.8 us: coarse_image(): term = jnp.sum(block[None, :, :, :] * vectors[:, :, None, :], axis=1)]
    slice x2 -> x10, local copies, waits for them, and re-layouts: 0.38 us -> 18.9 us  [the longest x4 10.3 us: coarse_image(): jnp.roll(search, gy_count, axis=-1)]
    slice x28 -> x32, local copies, waits for them, and re-layouts: 5.88 us -> 21.9 us  [coarse_image(): jnp.roll(search, -gy_count, axis=-1)]
    slice x28 -> x32, local copies, waits for them, and re-layouts: 4.68 us -> 17.6 us  [coarse_image(): jnp.roll(search, -1, axis=-1)]
    add x14 -> x0, local copies, waits for them, and re-layouts: 6.63 us -> none  [coarse_image(): total = term if total is None else total + term]
    unnamed x227 -> x209, local copies, waits for them, and re-layouts: 18.4 us -> 17.6 us
  transfers between devices with their start and end apart: 27 -> 27, of which waited for: 15 -> 15; matrix products, arithmetic and copies ran while one was open for 11% -> 16% of each run, Pallas kernels for 14% -> 15%
where the time goes in v7:
time: 543 us; the launch traced here: 534 us
  other arithmetic  183 us (34%)
  local copies, waits for them, and re-layouts  149 us (27%)
  Pallas kernels  78.1 us (14%)
  waiting for transfers between devices  49.8 us (9%)
  starting transfers between devices  32.4 us (6%)
  matrix products  24.6 us (5%)
  between operations  17.3 us (3%)
    reduce_sum x81, other arithmetic, coarse_image(): term = jnp.sum(block[None, :, :, :] * vectors[:, :, None, :], axis=1)  78.8 us
    pallas_call x2, Pallas kernels, local_solve(): pl.pallas_call(sweep_kernel, out_shape=jax.ShapeDtypeStruct(residual.shap...  78.1 us
    ppermute x14, waiting for transfers between devices, tree_gather(): other = lax.ppermute(values, axis, [(i, i ^ stride) for i in range(count)])  43.4 us
    slice x32, local copies, waits for them, and re-layouts, coarse_image(): jnp.roll(search, -gy_count, axis=-1)  21.9 us
    reduce_sum x14, other arithmetic, body(): jnp.sum(image_halves[:, 0] * search_halves[:, 0] + image_halves[:, 1] * s...  20.8 us
    unnamed x209, local copies, waits for them, and re-layouts  17.6 us
    slice x32, local copies, waits for them, and re-layouts, coarse_image(): jnp.roll(search, -1, axis=-1)  17.6 us
    reduce_sum x28, other arithmetic, body(): squares = jnp.sum(image_halves * image_halves, axis=(1, 2, 3))  16.8 us
  transfers between devices with their start and end apart: 27, of which 15 were waited for; matrix products, arithmetic and copies ran while one was open for 16% of the time, Pallas kernels for 15%

profile of v7, /device:TPU:16, one launch (start us, length us, event | category | flops | bytes accessed | tf_op | source)
XLA Modules:
  0.0 533.6 jit_solution(11921744687163828261)
XLA Ops:
  8.6 5.7 %collective-permute-start.1 = (f32[14,17,128]{2,1,0:T(8,128)S(1)}, f32[14,17,128]{2,1,0:T(8,128)S(1)}, u32[]{:S(2)}, u32[]{:S(2)}) collective-permute-start(f32[14,17,128]{2,1,0:T(8,128)S(1)} %get-tuple-element.150), channel_id=1, source_target_pairs={{4,0},{8,4},{12,8},{16,12},{20,16},{24,20},{28,24},{32,28},{36,32}... | collective-permute-start | bytes 365576 | tf_op jit(solution)/shard_map/ppermute | solution.py:30
  15.0 3.3 copy_multiply_fusion
  18.9 5.1 collective-permute-start.4
  25.9 2.6 copy.417
  28.6 2.6 copy.418
  33.2 3.2 fusion.324
  36.4 3.1 copy.422
  40.0 3.1 copy.423
  43.1 2.3 collective-permute-start.7
  45.4 2.4 copy.419
  47.9 2.4 copy.420
  50.3 2.8 maximum_multiply_fusion
  54.8 3.2 fusion.39
  62.0 2.2 fusion.44
  65.0 2.2 slice.880
  69.5 4.0 fusion.15
  73.6 3.3 collective-permute-start.8
  79.5 4.2 collective-permute-done.9
  85.1 3.7 collective-permute-done.11
  89.0 5.3 collective-permute-done.12
  94.4 4.9 collective-permute-done.13
  102.2 3.1 pad.40.resid_ref
  109.9 38.8 %shard_map.55 = f32[6,2,160,256]{3,2,1,0:T(8,128)} custom-call(f32[6,2,160,256]{3,2,1,0:T(8,128)} %pad.40.resid_ref, f32[160,256]{1,0:T(8,128)} %pad.41.north_ref, f32[160,256]{1,0:T(8,128)} %pad.42.south_ref, f32[160,256]{1,0:T(8,128)} %pad.43.east_ref, f32[160,256]{1,0:T(8,128)} %pad.44.west_ref, f32[160,256]{1,0:T(8,128)} %pad.45.diag_ref, ...), custom_call_target="tpu_custom_call" | custom-call | tf_op jit(solution)/shard_map/pallas_call | solution.py:144
  155.8 2.5 fusion.320
  158.3 3.2 copy.428
  161.5 3.2 copy.431
  164.7 2.6 fusion.322
  167.4 2.6 copy.432
  170.0 2.5 copy.435
  175.9 11.2 %copy.424 = f32[128,1,9600]{0,2,1:T(8,128)} copy(f32[128,1,9600]{2,1,0:T(1,128)} %all-gather.3.cloned.1.call-done) | data formatting | bytes 9830400 | tf_op jit(solution)/shard_map/all_gather | solution.py:250
  187.1 2.8 fusion.315
  215.4 2.1 fusion.173
  227.3 2.1 fusion.161
  241.7 2.1 fusion.147
  275.6 4.9 fusion.18
  282.3 5.1 collective-permute-start.16
  287.4 2.8 collective-permute-done.15
  296.8 2.4 copy.484
  300.9 2.3 copy.485
  303.2 2.3 collective-permute-done.18
  305.5 2.3 copy.486
  307.8 2.9 maximum_multiply_fusion.1
  311.4 2.2 fusion.28
  316.6 3.5 fusion.13
  321.5 2.4 collective-permute-done.19
  324.0 5.1 collective-permute-done.20
  330.4 3.7 collective-permute-done.22
  334.3 5.4 %collective-permute-done.23 = f32[4,4,480]{2,1,0:T(4,128)S(1)} collective-permute-done((f32[4,4,480]{2,1,0:T(4,128)S(1)}, f32[4,4,480]{2,1,0:T(4,128)S(1)}, u32[]{:S(2)}, u32[]{:S(2)}) %collective-permute-start.23) | collective-permute-done | bytes 30752 | tf_op jit(solution)/shard_map/ppermute | solution.py:60
  339.8 4.9 collective-permute-done.24
  344.7 2.2 collective-permute-start.25
  346.9 3.0 pad.49.resid_ref
  349.9 39.3 %shard_map.56 = f32[6,2,160,256]{3,2,1,0:T(8,128)} custom-call(f32[6,2,160,256]{3,2,1,0:T(8,128)} %pad.49.resid_ref, f32[160,256]{1,0:T(8,128)} %pad.41.north_ref, f32[160,256]{1,0:T(8,128)} %pad.42.south_ref, f32[160,256]{1,0:T(8,128)} %pad.43.east_ref, f32[160,256]{1,0:T(8,128)} %pad.44.west_ref, f32[160,256]{1,0:T(8,128)} %pad.45.diag_ref, ...), custom_call_target="tpu_custom_call" | custom-call | tf_op jit(solution)/shard_map/pallas_call | solution.py:144
  390.4 2.5 select_n.240
  395.9 2.5 copy.488
  399.8 2.5 multiply_reduce_fusion.41
  402.3 5.2 fusion.316
  407.5 2.7 fusion.318
  414.9 2.6 multiply_reduce_fusion.36
  420.5 3.2 copy.489
  426.2 3.2 copy.492
  432.1 3.3 copy.493
  437.9 3.3 copy.496
  520.6 3.2 fusion.17
  523.8 2.6 fusion.55
  (626 shorter events, 232.4 us)
Async XLA Ops:
  6.5 17.5 %copy-start.58 = (f32[128,128]{1,0:T(8,128)S(1)}, f32[128,128]{1,0:T(8,128)}, u32[]{:S(2)}) copy-start(f32[128,128]{1,0:T(8,128)} %param.6) | copy-start | bytes 196612
  6.5 17.5 %copy-start.25 = (f32[6,2,128,128]{3,2,1,0:T(8,128)S(1)}, f32[6,2,128,128]{3,2,1,0:T(8,128)}, u32[]{:S(2)}) copy-start(f32[6,2,128,128]{3,2,1,0:T(8,128)} %param.5) | copy-start | bytes 2359300
  6.5 169.4 %all-gather.3.cloned.1.call-start = ((), (), s32[]{:S(2)}) async-start(), calls=%async_computation | async-start | bytes 4953600 | tf_op jit(solution)/shard_map/all_gather | solution.py:250
  8.5 15.5 %collective-permute-start = (f32[14,17,128]{2,1,0:T(8,128)S(1)}, f32[14,17,128]{2,1,0:T(8,128)S(1)}, u32[]{:S(2)}, u32[]{:S(2)}) collective-permute-start(f32[14,17,128]{2,1,0:T(8,128)S(1)} %get-tuple-element.149), channel_id=1, source_target_pairs={{0,4},{4,8},{8,12},{12,16},{16,20},{20,24},{24,28},{28,32},{32,36}... | collective-permute-start | bytes 365576 | tf_op jit(solution)/shard_map/ppermute | solution.py:28
  8.6 15.4 %collective-permute-start.1 = (f32[14,17,128]{2,1,0:T(8,128)S(1)}, f32[14,17,128]{2,1,0:T(8,128)S(1)}, u32[]{:S(2)}, u32[]{:S(2)}) collective-permute-start(f32[14,17,128]{2,1,0:T(8,128)S(1)} %get-tuple-element.150), channel_id=1, source_target_pairs={{4,0},{8,4},{12,8},{16,12},{20,16},{24,20},{28,24},{32,28},{36,32}... | collective-permute-start | bytes 365576 | tf_op jit(solution)/shard_map/ppermute | solution.py:30
  15.0 54.5 %copy-start.97 = (f32[40]{0:T(128)}, f32[40]{0:T(128)S(1)}, u32[]{:S(2)}) copy-start(f32[40]{0:T(128)S(1)} %compare_convert_fusion) | copy-start | bytes 484
  18.9 40.1 %collective-permute-start.5 = (f32[40,128]{1,0:T(8,128)}, f32[40,128]{1,0:T(8,128)}, u32[]{:S(2)}, u32[]{:S(2)}) collective-permute-start(f32[40,128]{1,0:T(8,128)} %get-tuple-element.141), channel_id=1, source_target_pairs={{0,4},{4,8},{8,12},{12,16},{16,20},{20,24},{24,28},{28,32},{32,36}... | collective-permute-start | bytes 61448 | tf_op jit(solution)/shard_map/ppermute | solution.py:228
  18.9 39.1 %collective-permute-start.4 = (f32[40,128]{1,0:T(8,128)}, f32[40,128]{1,0:T(8,128)}, u32[]{:S(2)}, u32[]{:S(2)}) collective-permute-start(f32[40,128]{1,0:T(8,128)} %get-tuple-element.142), channel_id=1, source_target_pairs={{4,0},{8,4},{12,8},{16,12},{20,16},{24,20},{28,24},{32,28},{36,32}... | collective-permute-start | bytes 61448 | tf_op jit(solution)/shard_map/ppermute | solution.py:227
  31.2 16.7 %collective-permute-start.3 = (f32[14,162,17]{1,0,2:T(8,128)}, f32[14,162,17]{1,0,2:T(8,128)}, u32[]{:S(2)}, u32[]{:S(2)}) collective-permute-start(f32[14,162,17]{1,0,2:T(8,128)} %copy.418), channel_id=1, source_target_pairs={{1,0},{2,1},{3,2},{0,3},{5,4},{6,5},{7,6},{4,7},{9,8},{10,9},{11,1... | collective-permute-start | bytes 462680 | tf_op jit(solution)/shard_map/ppermute | solution.py:30
  31.7 11.4 %collective-permute-start.2 = (f32[14,162,17]{1,0,2:T(8,128)}, f32[14,162,17]{1,0,2:T(8,128)}, u32[]{:S(2)}, u32[]{:S(2)}) collective-permute-start(f32[14,162,17]{1,0,2:T(8,128)} %copy.417), channel_id=1, source_target_pairs={{0,1},{1,2},{2,3},{3,0},{4,5},{5,6},{6,7},{7,4},{8,9},{9,10},{10,1... | collective-permute-start | bytes 462680 | tf_op jit(solution)/shard_map/ppermute | solution.py:28
  39.5 20.5 %collective-permute-start.6 = (f32[40,128]{1,0:T(8,128)}, f32[40,128]{1,0:T(8,128)}, u32[]{:S(2)}, u32[]{:S(2)}) collective-permute-start(f32[40,128]{1,0:T(8,128)} %bitcast.1448), channel_id=1, source_target_pairs={{1,0},{2,1},{3,2},{0,3},{5,4},{6,5},{7,6},{4,7},{9,8},{10,9},{11,1... | collective-permute-start | bytes 61448 | tf_op jit(solution)/shard_map/ppermute | solution.py:229
  43.1 11.7 %copy-start.100 = (f32[162]{0:T(256)}, f32[162]{0:T(256)S(1)}, u32[]{:S(2)}) copy-start(f32[162]{0:T(256)S(1)} %and_convert_fusion) | copy-start | bytes 1948
  43.1 18.0 %collective-permute-start.7 = (f32[40,128]{1,0:T(8,128)}, f32[40,128]{1,0:T(8,128)}, u32[]{:S(2)}, u32[]{:S(2)}) collective-permute-start(f32[40,128]{1,0:T(8,128)} %bitcast.1449), channel_id=1, source_target_pairs={{0,1},{1,2},{2,3},{3,0},{4,5},{5,6},{6,7},{7,4},{8,9},{9,10},{10,1... | collective-permute-start | bytes 61448 | tf_op jit(solution)/shard_map/ppermute | solution.py:230
  54.8 5.3 copy-start.81
  54.8 6.3 %copy-start.80 = (f32[40,128,1]{1,0,2:T(8,128)S(1)}, f32[40,128,1]{1,0,2:T(8,128)}, u32[]{:S(2)}) copy-start(f32[40,128,1]{1,0,2:T(8,128)} %copy.422) | copy-start | bytes 61444
  64.2 5.3 copy-start.15
  73.6 4.9 collective-permute-start.8
  78.5 5.2 collective-permute-start.9
  83.7 1.3 collective-permute-start.10
  85.0 3.8 collective-permute-start.11
  88.8 5.5 %collective-permute-start.12 = (f32[4,4,480]{2,1,0:T(4,128)S(1)}, f32[4,4,480]{2,1,0:T(4,128)S(1)}, u32[]{:S(2)}, u32[]{:S(2)}) collective-permute-start(f32[4,4,480]{2,1,0:T(4,128)S(1)} %maximum_select_fusion.6), channel_id=1, source_target_pairs={{0,16},{4,20},{8,24},{12,28},{16,0},{20,4},{24,8},{28,12},{32,48},... | collective-permute-start | bytes 92168 | tf_op jit(solution)/shard_map/ppermute | solution.py:60
  94.3 5.0 collective-permute-start.13
  99.3 49.4 %collective-permute-start.14 = (f32[16,4,480]{2,1,0:T(4,128)S(1)}, f32[16,4,480]{2,1,0:T(4,128)S(1)}, u32[]{:S(2)}, u32[]{:S(2)}) collective-permute-start(f32[16,4,480]{2,1,0:T(4,128)S(1)} %maximum_select_fusion.2), channel_id=1, source_target_pairs={{0,64},{4,68},{8,72},{12,76},{16,80},{20,84},{24,88},{28,92},{32,9... | collective-permute-start | bytes 368648 | tf_op jit(solution)/shard_map/ppermute | solution.py:60
  102.2 7.1 %copy-start.59 = (f32[160,160]{1,0:T(8,128)}, f32[160,160]{1,0:T(8,128)S(1)}, u32[]{:S(2)}) copy-start(f32[160,160]{1,0:T(8,128)S(1)} %get-tuple-element.112) | copy-start | bytes 307204
  167.3 6.0 %copy-start.66 = (f32[12,40,4]{2,1,0:T(8,128)S(1)}, f32[12,40,4]{2,1,0:T(8,128)}, u32[]{:S(2)}) copy-start(f32[12,40,4]{2,1,0:T(8,128)} %copy.430) | copy-start | bytes 23044
  167.3 6.0 %copy-start.69 = (f32[12,40,124]{2,1,0:T(8,128)S(1)}, f32[12,40,124]{2,1,0:T(8,128)}, u32[]{:S(2)}) copy-start(f32[12,40,124]{2,1,0:T(8,128)} %copy.431) | copy-start | bytes 714244
  167.3 7.7 %copy-start.64 = (f32[12,40,1]{2,1,0:T(8,128)S(1)}, f32[12,40,1]{2,1,0:T(8,128)}, u32[]{:S(2)}) copy-start(f32[12,40,1]{2,1,0:T(8,128)} %copy.434) | copy-start | bytes 5764
  189.9 6.2 %copy-start = (f32[1600,128]{1,0:T(8,128)}, f32[1600,128]{1,0:T(8,128)S(1)}, u32[]{:S(2)}) copy-start(f32[1600,128]{1,0:T(8,128)S(1)} %get-tuple-element.118) | copy-start | bytes 2457604
  189.9 6.2 %copy-start.13 = (f32[1600,128]{1,0:T(8,128)}, f32[1600,128]{1,0:T(8,128)S(1)}, u32[]{:S(2)}) copy-start(f32[1600,128]{1,0:T(8,128)S(1)} %get-tuple-element.122) | copy-start | bytes 2457604
  215.4 6.5 %copy-start.3 = (f32[1600,128]{1,0:T(8,128)S(1)}, f32[1600,128]{1,0:T(8,128)}, u32[]{:S(2)}) copy-start(f32[1600,128]{1,0:T(8,128)} %copy-done) | copy-start | bytes 2457604
  227.3 7.2 %copy-start.4 = (f32[1600,128]{1,0:T(8,128)S(1)}, f32[1600,128]{1,0:T(8,128)}, u32[]{:S(2)}) copy-start(f32[1600,128]{1,0:T(8,128)} %copy-done) | copy-start | bytes 2457604
  241.7 7.1 %copy-start.5 = (f32[1600,128]{1,0:T(8,128)S(1)}, f32[1600,128]{1,0:T(8,128)}, u32[]{:S(2)}) copy-start(f32[1600,128]{1,0:T(8,128)} %copy-done) | copy-start | bytes 2457604
  244.5 5.8 %copy-start.89 = (f32[6]{0:T(128)}, f32[6]{0:T(128)S(1)}, u32[]{:S(2)}) copy-start(f32[6]{0:T(128)S(1)} %get-tuple-element.315) | copy-start | bytes 76
  255.5 7.1 %copy-start.6 = (f32[1600,128]{1,0:T(8,128)S(1)}, f32[1600,128]{1,0:T(8,128)}, u32[]{:S(2)}) copy-start(f32[1600,128]{1,0:T(8,128)} %copy-done) | copy-start | bytes 2457604
  258.2 5.8 %copy-start.95 = (f32[6]{0:T(128)}, f32[6]{0:T(128)S(1)}, u32[]{:S(2)}) copy-start(f32[6]{0:T(128)S(1)} %get-tuple-element.313) | copy-start | bytes 76
  282.2 8.0 %copy-start.21 = (f32[6,2,128,128]{3,2,1,0:T(8,128)}, f32[6,2,128,128]{3,2,1,0:T(8,128)S(1)}, u32[]{:S(2)}) copy-start(f32[6,2,128,128]{3,2,1,0:T(8,128)S(1)} %slice_add_fusion.1) | copy-start | bytes 2359300
  282.2 8.0 %collective-permute-start.15 = (f32[6,2,17,128]{3,2,1,0:T(8,128)S(1)}, f32[6,2,17,128]{3,2,1,0:T(8,128)S(1)}, u32[]{:S(2)}, u32[]{:S(2)}) collective-permute-start(f32[6,2,17,128]{3,2,1,0:T(8,128)S(1)} %get-tuple-element.151), channel_id=1, source_target_pairs={{0,4},{4,8},{8,12},{12,16},{16,20},{20,24},{24,28},{28,32},{32,36}... | collective-permute-start | bytes 313352 | tf_op jit(solution)/shard_map/ppermute | solution.py:28
  282.3 7.9 %collective-permute-start.16 = (f32[6,2,17,128]{3,2,1,0:T(8,128)S(1)}, f32[6,2,17,128]{3,2,1,0:T(8,128)S(1)}, u32[]{:S(2)}, u32[]{:S(2)}) collective-permute-start(f32[6,2,17,128]{3,2,1,0:T(8,128)S(1)} %get-tuple-element.152), channel_id=1, source_target_pairs={{4,0},{8,4},{12,8},{16,12},{20,16},{24,20},{28,24},{32,28},{36,32}... | collective-permute-start | bytes 313352 | tf_op jit(solution)/shard_map/ppermute | solution.py:30
  291.6 16.1 %copy-start.101 = (f32[162]{0:T(256)S(1)}, f32[162]{0:T(256)}, u32[]{:S(2)}) copy-start(f32[162]{0:T(256)} %copy-done.100) | copy-start | bytes 1948
  295.0 6.0 %collective-permute-start.17 = (f32[6,2,162,17]{2,1,3,0:T(2,128)S(1)}, f32[6,2,162,17]{2,1,3,0:T(2,128)}, u32[]{:S(2)}, u32[]{:S(2)}) collective-permute-start(f32[6,2,162,17]{2,1,3,0:T(2,128)S(1)} %copy.483), channel_id=1, source_target_pairs={{0,1},{1,2},{2,3},{3,0},{4,5},{5,6},{6,7},{7,4},{8,9},{9,10},{10,1... | collective-permute-start | bytes 396584 | tf_op jit(solution)/shard_map/ppermute | solution.py:28
  299.2 6.3 %collective-permute-start.18 = (f32[6,2,162,17]{2,1,3,0:T(2,128)}, f32[6,2,162,17]{2,1,3,0:T(2,128)}, u32[]{:S(2)}, u32[]{:S(2)}) collective-permute-start(f32[6,2,162,17]{2,1,3,0:T(2,128)} %copy.484), channel_id=1, source_target_pairs={{1,0},{2,1},{3,2},{0,3},{5,4},{6,5},{7,6},{4,7},{9,8},{10,9},{11,1... | collective-permute-start | bytes 396584 | tf_op jit(solution)/shard_map/ppermute | solution.py:30
  303.2 8.1 %copy-start.60 = (f32[160,160]{1,0:T(8,128)S(1)}, f32[160,160]{1,0:T(8,128)}, u32[]{:S(2)}) copy-start(f32[160,160]{1,0:T(8,128)} %copy-done.59) | copy-start | bytes 307204
  320.2 3.7 collective-permute-start.19
  323.9 5.2 collective-permute-start.20
  329.1 1.3 collective-permute-start.21
  330.3 3.8 collective-permute-start.22
  334.2 5.5 %collective-permute-start.23 = (f32[4,4,480]{2,1,0:T(4,128)S(1)}, f32[4,4,480]{2,1,0:T(4,128)S(1)}, u32[]{:S(2)}, u32[]{:S(2)}) collective-permute-start(f32[4,4,480]{2,1,0:T(4,128)S(1)} %maximum_select_fusion.7), channel_id=1, source_target_pairs={{0,16},{4,20},{8,24},{12,28},{16,0},{20,4},{24,8},{28,12},{32,48},... | collective-permute-start | bytes 92168 | tf_op jit(solution)/shard_map/ppermute | solution.py:60
  339.7 5.0 collective-permute-start.24
  344.7 44.5 %copy-start.78 = (f32[16,4,480]{2,1,0:T(4,128)}, f32[16,4,480]{2,1,0:T(4,128)S(1)}, u32[]{:S(2)}) copy-start(f32[16,4,480]{2,1,0:T(4,128)S(1)} %maximum_select_fusion.3) | copy-start | bytes 368644
  344.7 44.5 %collective-permute-start.25 = (f32[16,4,480]{2,1,0:T(4,128)S(1)}, f32[16,4,480]{2,1,0:T(4,128)}, u32[]{:S(2)}, u32[]{:S(2)}) collective-permute-start(f32[16,4,480]{2,1,0:T(4,128)S(1)} %maximum_select_fusion.3), channel_id=1, source_target_pairs={{0,64},{4,68},{8,72},{12,76},{16,80},{20,84},{24,88},{28,92},{32,9... | collective-permute-start | bytes 368648 | tf_op jit(solution)/shard_map/ppermute | solution.py:60
  398.4 55.8 %copy-start.20 = (f32[12,40,128]{2,1,0:T(8,128)}, f32[12,40,128]{2,1,0:T(8,128)S(1)}, u32[]{:S(2)}) copy-start(f32[12,40,128]{2,1,0:T(8,128)S(1)} %copy.488) | copy-start | bytes 737284
  464.0 6.2 %copy-start.9 = (f32[1600,128]{1,0:T(8,128)S(1)}, f32[1600,128]{1,0:T(8,128)}, u32[]{:S(2)}) copy-start(f32[1600,128]{1,0:T(8,128)} %copy-done) | copy-start | bytes 2457604
  475.9 6.9 %copy-start.10 = (f32[1600,128]{1,0:T(8,128)S(1)}, f32[1600,128]{1,0:T(8,128)}, u32[]{:S(2)}) copy-start(f32[1600,128]{1,0:T(8,128)} %copy-done) | copy-start | bytes 2457604
  483.4 6.0 %copy-start.31 = (f32[12,40,128]{2,1,0:T(8,128)S(1)}, f32[12,40,128]{2,1,0:T(8,128)}, u32[]{:S(2)}) copy-start(f32[12,40,128]{2,1,0:T(8,128)} %get-tuple-element.50) | copy-start | bytes 737284
  489.4 7.0 %copy-start.11 = (f32[1600,128]{1,0:T(8,128)S(1)}, f32[1600,128]{1,0:T(8,128)}, u32[]{:S(2)}) copy-start(f32[1600,128]{1,0:T(8,128)} %copy-done) | copy-start | bytes 2457604
  501.3 9.0 %copy-start.26 = (f32[12,40,128]{2,1,0:T(8,128)}, f32[12,40,128]{2,1,0:T(8,128)S(1)}, u32[]{:S(2)}) copy-start(f32[12,40,128]{2,1,0:T(8,128)S(1)} %get-tuple-element.38) | copy-start | bytes 737284
  502.6 6.8 %copy-start.12 = (f32[1600,128]{1,0:T(8,128)S(1)}, f32[1600,128]{1,0:T(8,128)}, u32[]{:S(2)}) copy-start(f32[1600,128]{1,0:T(8,128)} %copy-done) | copy-start | bytes 2457604
  510.3 6.5 %copy-start.83 = (f32[6]{0:T(128)S(1)}, f32[6]{0:T(128)}, u32[]{:S(2)}) copy-start(f32[6]{0:T(128)} %copy-done.82) | copy-start | bytes 76
  511.0 5.9 %copy-start.86 = (f32[6]{0:T(128)S(1)}, f32[6]{0:T(128)}, u32[]{:S(2)}) copy-start(f32[6]{0:T(128)} %copy-done.85) | copy-start | bytes 76
  511.0 5.9 %copy-start.88 = (f32[6]{0:T(128)S(1)}, f32[6]{0:T(128)}, u32[]{:S(2)}) copy-start(f32[6]{0:T(128)} %copy-done.87) | copy-start | bytes 76
  511.0 5.9 %copy-start.94 = (f32[6]{0:T(128)S(1)}, f32[6]{0:T(128)}, u32[]{:S(2)}) copy-start(f32[6]{0:T(128)} %copy-done.93) | copy-start | bytes 76
  512.6 7.9 %copy-start.17 = (f32[40,128,128]{2,1,0:T(8,128)S(1)}, f32[40,128,128]{2,1,0:T(8,128)}, u32[]{:S(2)}) copy-start(f32[40,128,128]{2,1,0:T(8,128)} %param.8) | copy-start | bytes 7864324
  512.6 7.9 %copy-start.99 = (f32[40]{0:T(128)S(1)}, f32[40]{0:T(128)}, u32[]{:S(2)}) copy-start(f32[40]{0:T(128)} %copy-done.97) | copy-start | bytes 484
  514.2 9.5 %copy-start.22 = (f32[6,2,128,128]{3,2,1,0:T(8,128)S(1)}, f32[6,2,128,128]{3,2,1,0:T(8,128)}, u32[]{:S(2)}) copy-start(f32[6,2,128,128]{3,2,1,0:T(8,128)} %copy-done.21) | copy-start | bytes 2359300
  (65 other events, 133.7 us)
Sparse Core Ops, SparseCore 0:
  65.1 64.8 all-gather.2

commit v8 on v7

--- a/solution.py
+++ b/solution.py
@@ -250,17 +250,23 @@
     gathered_blocks = lax.all_gather(block_set.reshape(1, -1), ("gx", "gy"), axis=0, tiled=True)
     all_blocks = gathered_blocks.T.reshape(block_set.shape + (tile_total,))
 
+    tile_ids = jnp.arange(tile_total)
+    movers = [
+        (tile_ids[:, None] == (tile_ids[None, :] + offset) % tile_total).astype(jnp.float32)
+        for offset in (gy_count, -gy_count, 1, -1)
+    ]
+
     def coarse_image(search):
         halves = search.reshape(mode_count, 2, basis_total, tile_total)
         turned = jnp.stack([-halves[:, 1], halves[:, 0]], axis=1).reshape(search.shape)
-        shifted = (
-            search,
-            jnp.roll(search, -gy_count, axis=-1),
-            jnp.roll(search, gy_count, axis=-1),
-            jnp.roll(search, -1, axis=-1),
-            jnp.roll(search, 1, axis=-1),
-            turned,
-        )
+        flat = search.reshape(-1, tile_total)
+        moved = [
+            lax.dot_general(
+                flat, mover, (((1,), (0,)), ((), ())), precision=highest, preferred_element_type=jnp.float32
+            ).reshape(search.shape)
+            for mover in movers
+        ]
+        shifted = (search, *moved, turned)
         total = None
         for block, vectors in zip(all_blocks, shifted):
             term = jnp.sum(block[None, :, :, :] * vectors[:, :, None, :], axis=1)

time: 543 us -> 486 us (0.90)
  local copies, waits for them, and re-layouts: 149 us -> 92.3 us
  matrix products: 24.6 us -> 41.4 us
  other arithmetic: 183 us -> 172 us
    slice x72 -> x0, local copies, waits for them, and re-layouts: 57.7 us -> none  [the longest x32 21.9 us: coarse_image(): jnp.roll(search, -gy_count, axis=-1)]
    dot_general x0 -> x56, matrix products: none -> 16.9 us  [coarse_image(): lax.dot_general(flat, mover, (((1,), (0,)), ((), ())), precision=highest,...]
    concatenate x56 -> x0, other arithmetic: 14.5 us -> none  [the longest x14 3.63 us: coarse_image(): jnp.roll(search, 1, axis=-1)]
    reduce_sum x81 -> x83, other arithmetic: 78.8 us -> 75.2 us  [coarse_image(): term = jnp.sum(block[None, :, :, :] * vectors[:, :, None, :], axis=1)]
    unnamed x209 -> x211, local copies, waits for them, and re-layouts: 17.6 us -> 17.1 us
  transfers between devices with their start and end apart: 27 -> 27, of which waited for: 15 -> 15; matrix products, arithmetic and copies ran while one was open for 16% -> 14% of each run, Pallas kernels for 15% -> 16%
where the time goes in v8:
time: 486 us; the launch traced here: 477 us
  other arithmetic  172 us (35%)
  local copies, waits for them, and re-layouts  92.3 us (19%)
  Pallas kernels  78.2 us (16%)
  waiting for transfers between devices  48.3 us (10%)
  matrix products  41.4 us (9%)
  starting transfers between devices  27.2 us (6%)
  between operations  17.2 us (4%)
    pallas_call x2, Pallas kernels, local_solve(): pl.pallas_call(sweep_kernel, out_shape=jax.ShapeDtypeStruct(residual.shap...  78.2 us
    reduce_sum x83, other arithmetic, coarse_image(): term = jnp.sum(block[None, :, :, :] * vectors[:, :, None, :], axis=1)  75.2 us
    ppermute x14, waiting for transfers between devices, tree_gather(): other = lax.ppermute(values, axis, [(i, i ^ stride) for i in range(count)])  41.7 us
    reduce_sum x14, other arithmetic, body(): jnp.sum(image_halves[:, 0] * search_halves[:, 0] + image_halves[:, 1] * s...  23.9 us
    reduce_sum x28, other arithmetic, body(): squares = jnp.sum(image_halves * image_halves, axis=(1, 2, 3))  20.5 us
    unnamed x211, local copies, waits for them, and re-layouts  17.1 us
    dot_general x56, matrix products, coarse_image(): lax.dot_general(flat, mover, (((1,), (0,)), ((), ())), precision=highest,...  16.9 us
    neg x14, other arithmetic, coarse_image(): -halves[:, 1]  13.8 us
  transfers between devices with their start and end apart: 27, of which 15 were waited for; matrix products, arithmetic and copies ran while one was open for 14% of the time, Pallas kernels for 16%

profile of v8, /device:TPU:16, one launch (start us, length us, event | category | flops | bytes accessed | tf_op | source)
XLA Modules:
  0.0 477.0 jit_solution(13460029583887349891)
XLA Ops:
  8.6 5.7 %collective-permute-start.1 = (f32[14,17,128]{2,1,0:T(8,128)S(1)}, f32[14,17,128]{2,1,0:T(8,128)S(1)}, u32[]{:S(2)}, u32[]{:S(2)}) collective-permute-start(f32[14,17,128]{2,1,0:T(8,128)S(1)} %get-tuple-element.134), channel_id=1, source_target_pairs={{4,0},{8,4},{12,8},{16,12},{20,16},{24,20},{28,24},{32,28},{36,32}... | collective-permute-start | bytes 365576 | tf_op jit(solution)/shard_map/ppermute | solution.py:30
  15.0 3.3 copy_multiply_fusion
  21.5 2.6 copy.421
  25.5 2.6 copy.422
  28.9 3.1 fusion.492
  32.0 3.1 copy.426
  35.6 3.1 copy.427
  38.7 1.9 collective-permute-start.7
  40.5 2.4 copy.423
  42.9 2.5 copy.424
  45.4 2.8 maximum_multiply_fusion
  49.9 3.2 fusion.39
  57.1 2.2 fusion.44
  60.1 2.2 slice.424
  64.6 3.9 fusion.15
  68.6 2.6 collective-permute-start.8
  73.9 4.0 collective-permute-done.9
  79.4 3.7 collective-permute-done.11
  83.3 5.3 %collective-permute-done.12 = f32[4,4,480]{2,1,0:T(4,128)S(1)} collective-permute-done((f32[4,4,480]{2,1,0:T(4,128)S(1)}, f32[4,4,480]{2,1,0:T(4,128)S(1)}, u32[]{:S(2)}, u32[]{:S(2)}) %collective-permute-start.12) | collective-permute-done | bytes 30752 | tf_op jit(solution)/shard_map/ppermute | solution.py:60
  88.7 4.2 collective-permute-done.13
  93.0 1.9 collective-permute-start.14
  94.9 2.1 add_divide_fusion
  97.0 3.1 pad.40.resid_ref
  104.8 38.9 %shard_map.55 = f32[6,2,160,256]{3,2,1,0:T(8,128)} custom-call(f32[6,2,160,256]{3,2,1,0:T(8,128)} %pad.40.resid_ref, f32[160,256]{1,0:T(8,128)} %pad.41.north_ref, f32[160,256]{1,0:T(8,128)} %pad.42.south_ref, f32[160,256]{1,0:T(8,128)} %pad.43.east_ref, f32[160,256]{1,0:T(8,128)} %pad.44.west_ref, f32[160,256]{1,0:T(8,128)} %pad.45.diag_ref, ...), custom_call_target="tpu_custom_call" | custom-call | tf_op jit(solution)/shard_map/pallas_call | solution.py:144
  150.2 11.1 %copy.428 = f32[128,1,9600]{0,2,1:T(8,128)} copy(f32[128,1,9600]{2,1,0:T(1,128)} %all-gather.3.cloned.1.call-done) | data formatting | bytes 9830400 | tf_op jit(solution)/shard_map/all_gather | solution.py:250
  161.3 2.8 fusion.491
  167.8 2.1 multiply_reduce_fusion.78
  174.1 1.9 multiply_reduce_fusion.77
  185.5 1.9 multiply_reduce_fusion.71
  194.6 2.1 fusion.173
  199.6 1.9 multiply_reduce_fusion.65
  208.5 2.1 fusion.161
  213.5 1.9 multiply_reduce_fusion.59
  222.6 2.1 fusion.147
  227.6 1.9 multiply_reduce_fusion.53
  236.4 2.1 fusion.244
  241.3 1.9 multiply_reduce_fusion.47
  256.9 4.9 %fusion.18 = f32[6,2,128,128]{3,0,2,1:T(8,128)S(1)} fusion(f32[6,2,40,1]{2,1,0,3:T(2,128)S(1)} %bitcast.1563, f32[40]{0:T(128)} %copy-done.98, f32[40,128,128]{2,1,0:T(8,128)} %param.8), kind=kOutput, calls=%fused_computation.104 | convolution fusion | flops 95027200 | bytes 3409952 | tf_op jit(solution)/shard_map/dot_general | solution.py:209
  263.6 5.1 %collective-permute-start.16 = (f32[6,2,17,128]{3,2,1,0:T(8,128)S(1)}, f32[6,2,17,128]{3,2,1,0:T(8,128)S(1)}, u32[]{:S(2)}, u32[]{:S(2)}) collective-permute-start(f32[6,2,17,128]{3,2,1,0:T(8,128)S(1)} %get-tuple-element.136), channel_id=1, source_target_pairs={{4,0},{8,4},{12,8},{16,12},{20,16},{24,20},{28,24},{32,28},{36,32}... | collective-permute-start | bytes 313352 | tf_op jit(solution)/shard_map/ppermute | solution.py:30
  268.7 2.8 collective-permute-done.15
  276.3 2.0 collective-permute-start.17
  278.3 2.4 copy.484
  282.3 2.3 copy.485
  284.6 2.5 collective-permute-done.18
  287.0 2.3 copy.486
  289.4 2.9 maximum_multiply_fusion.1
  293.0 2.2 fusion.28
  298.2 3.5 fusion.13
  303.2 2.2 collective-permute-done.19
  305.6 5.1 %collective-permute-done.20 = f32[2,480]{1,0:T(2,128)S(1)} collective-permute-done((f32[2,480]{1,0:T(2,128)S(1)}, f32[2,480]{1,0:T(2,128)S(1)}, u32[]{:S(2)}, u32[]{:S(2)}) %collective-permute-start.20) | collective-permute-done | bytes 3872 | tf_op jit(solution)/shard_map/ppermute | solution.py:60
  312.0 3.7 collective-permute-done.22
  315.8 5.4 %collective-permute-done.23 = f32[4,4,480]{2,1,0:T(4,128)S(1)} collective-permute-done((f32[4,4,480]{2,1,0:T(4,128)S(1)}, f32[4,4,480]{2,1,0:T(4,128)S(1)}, u32[]{:S(2)}, u32[]{:S(2)}) %collective-permute-start.23) | collective-permute-done | bytes 30752 | tf_op jit(solution)/shard_map/ppermute | solution.py:60
  321.6 4.2 collective-permute-done.24
  326.7 3.0 pad.49.resid_ref
  329.7 39.3 %shard_map.56 = f32[6,2,160,256]{3,2,1,0:T(8,128)} custom-call(f32[6,2,160,256]{3,2,1,0:T(8,128)} %pad.49.resid_ref, f32[160,256]{1,0:T(8,128)} %pad.41.north_ref, f32[160,256]{1,0:T(8,128)} %pad.42.south_ref, f32[160,256]{1,0:T(8,128)} %pad.43.east_ref, f32[160,256]{1,0:T(8,128)} %pad.44.west_ref, f32[160,256]{1,0:T(8,128)} %pad.45.diag_ref, ...), custom_call_target="tpu_custom_call" | custom-call | tf_op jit(solution)/shard_map/pallas_call | solution.py:144
  370.1 2.5 select_n.386
  372.6 2.5 copy.488
  406.0 2.0 fusion.84
  419.4 2.0 fusion.72
  424.3 2.1 multiply_reduce_fusion.17
  433.1 2.0 fusion.58
  445.8 2.0 fusion.236
  463.9 3.2 fusion.17
  467.2 2.6 fusion.55
  (560 shorter events, 197.2 us)
Async XLA Ops:
  6.5 13.1 %copy-start.55 = (f32[128,128]{1,0:T(8,128)S(1)}, f32[128,128]{1,0:T(8,128)}, u32[]{:S(2)}) copy-start(f32[128,128]{1,0:T(8,128)} %param.6) | copy-start | bytes 196612
  6.5 13.1 %copy-start.24 = (f32[6,2,128,128]{3,2,1,0:T(8,128)S(1)}, f32[6,2,128,128]{3,2,1,0:T(8,128)}, u32[]{:S(2)}) copy-start(f32[6,2,128,128]{3,2,1,0:T(8,128)} %param.5) | copy-start | bytes 2359300
  6.5 143.7 %all-gather.3.cloned.1.call-start = ((), (), s32[]{:S(2)}) async-start(), calls=%async_computation | async-start | bytes 4953600 | tf_op jit(solution)/shard_map/all_gather | solution.py:250
  8.5 11.1 %collective-permute-start = (f32[14,17,128]{2,1,0:T(8,128)S(1)}, f32[14,17,128]{2,1,0:T(8,128)S(1)}, u32[]{:S(2)}, u32[]{:S(2)}) collective-permute-start(f32[14,17,128]{2,1,0:T(8,128)S(1)} %get-tuple-element.133), channel_id=1, source_target_pairs={{0,4},{4,8},{8,12},{12,16},{16,20},{20,24},{24,28},{28,32},{32,36}... | collective-permute-start | bytes 365576 | tf_op jit(solution)/shard_map/ppermute | solution.py:28
  8.6 11.0 %collective-permute-start.1 = (f32[14,17,128]{2,1,0:T(8,128)S(1)}, f32[14,17,128]{2,1,0:T(8,128)S(1)}, u32[]{:S(2)}, u32[]{:S(2)}) collective-permute-start(f32[14,17,128]{2,1,0:T(8,128)S(1)} %get-tuple-element.134), channel_id=1, source_target_pairs={{4,0},{8,4},{12,8},{16,12},{20,16},{24,20},{28,24},{32,28},{36,32}... | collective-permute-start | bytes 365576 | tf_op jit(solution)/shard_map/ppermute | solution.py:30
  15.0 49.5 %copy-start.98 = (f32[40]{0:T(128)}, f32[40]{0:T(128)S(1)}, u32[]{:S(2)}) copy-start(f32[40]{0:T(128)S(1)} %compare_convert_fusion) | copy-start | bytes 484
  18.9 34.3 %collective-permute-start.4 = (f32[40,128]{1,0:T(8,128)}, f32[40,128]{1,0:T(8,128)}, u32[]{:S(2)}, u32[]{:S(2)}) collective-permute-start(f32[40,128]{1,0:T(8,128)} %get-tuple-element.126), channel_id=1, source_target_pairs={{4,0},{8,4},{12,8},{16,12},{20,16},{24,20},{28,24},{32,28},{36,32}... | collective-permute-start | bytes 61448 | tf_op jit(solution)/shard_map/ppermute | solution.py:227
  19.6 34.5 %collective-permute-start.5 = (f32[40,128]{1,0:T(8,128)}, f32[40,128]{1,0:T(8,128)}, u32[]{:S(2)}, u32[]{:S(2)}) collective-permute-start(f32[40,128]{1,0:T(8,128)} %get-tuple-element.125), channel_id=1, source_target_pairs={{0,4},{4,8},{8,12},{12,16},{16,20},{20,24},{24,28},{28,32},{32,36}... | collective-permute-start | bytes 61448 | tf_op jit(solution)/shard_map/ppermute | solution.py:228
  24.2 14.5 %collective-permute-start.2 = (f32[14,162,17]{1,0,2:T(8,128)}, f32[14,162,17]{1,0,2:T(8,128)}, u32[]{:S(2)}, u32[]{:S(2)}) collective-permute-start(f32[14,162,17]{1,0,2:T(8,128)} %copy.421), channel_id=1, source_target_pairs={{0,1},{1,2},{2,3},{3,0},{4,5},{5,6},{6,7},{7,4},{8,9},{9,10},{10,1... | collective-permute-start | bytes 462680 | tf_op jit(solution)/shard_map/ppermute | solution.py:28
  28.1 14.8 %collective-permute-start.3 = (f32[14,162,17]{1,0,2:T(8,128)}, f32[14,162,17]{1,0,2:T(8,128)}, u32[]{:S(2)}, u32[]{:S(2)}) collective-permute-start(f32[14,162,17]{1,0,2:T(8,128)} %copy.422), channel_id=1, source_target_pairs={{1,0},{2,1},{3,2},{0,3},{5,4},{6,5},{7,6},{4,7},{9,8},{10,9},{11,1... | collective-permute-start | bytes 462680 | tf_op jit(solution)/shard_map/ppermute | solution.py:30
  35.1 20.1 %collective-permute-start.6 = (f32[40,128]{1,0:T(8,128)}, f32[40,128]{1,0:T(8,128)}, u32[]{:S(2)}, u32[]{:S(2)}) collective-permute-start(f32[40,128]{1,0:T(8,128)} %bitcast.1560), channel_id=1, source_target_pairs={{1,0},{2,1},{3,2},{0,3},{5,4},{6,5},{7,6},{4,7},{9,8},{10,9},{11,1... | collective-permute-start | bytes 61448 | tf_op jit(solution)/shard_map/ppermute | solution.py:229
  38.7 11.2 %copy-start.101 = (f32[162]{0:T(256)}, f32[162]{0:T(256)S(1)}, u32[]{:S(2)}) copy-start(f32[162]{0:T(256)S(1)} %and_convert_fusion) | copy-start | bytes 1948
  38.7 17.5 %collective-permute-start.7 = (f32[40,128]{1,0:T(8,128)}, f32[40,128]{1,0:T(8,128)}, u32[]{:S(2)}, u32[]{:S(2)}) collective-permute-start(f32[40,128]{1,0:T(8,128)} %bitcast.1561), channel_id=1, source_target_pairs={{0,1},{1,2},{2,3},{3,0},{4,5},{5,6},{6,7},{7,4},{8,9},{9,10},{10,1... | collective-permute-start | bytes 61448 | tf_op jit(solution)/shard_map/ppermute | solution.py:230
  49.9 6.3 %copy-start.73 = (f32[40,128,1]{1,0,2:T(8,128)S(1)}, f32[40,128,1]{1,0,2:T(8,128)}, u32[]{:S(2)}) copy-start(f32[40,128,1]{1,0,2:T(8,128)} %copy.426) | copy-start | bytes 61444
  68.6 4.1 collective-permute-start.8
  72.8 5.2 %collective-permute-start.9 = (f32[2,480]{1,0:T(2,128)S(1)}, f32[2,480]{1,0:T(2,128)S(1)}, u32[]{:S(2)}, u32[]{:S(2)}) collective-permute-start(f32[2,480]{1,0:T(2,128)S(1)} %maximum_select_fusion.12), channel_id=1, source_target_pairs={{0,2},{1,3},{2,0},{3,1},{4,6},{5,7},{6,4},{7,5},{8,10},{9,11},{10,... | collective-permute-start | bytes 11528 | tf_op jit(solution)/shard_map/ppermute | solution.py:60
  78.0 1.3 collective-permute-start.10
  79.2 3.8 collective-permute-start.11
  83.1 5.5 %collective-permute-start.12 = (f32[4,4,480]{2,1,0:T(4,128)S(1)}, f32[4,4,480]{2,1,0:T(4,128)S(1)}, u32[]{:S(2)}, u32[]{:S(2)}) collective-permute-start(f32[4,4,480]{2,1,0:T(4,128)S(1)} %maximum_select_fusion.6), channel_id=1, source_target_pairs={{0,16},{4,20},{8,24},{12,28},{16,0},{20,4},{24,8},{28,12},{32,48},... | collective-permute-start | bytes 92168 | tf_op jit(solution)/shard_map/ppermute | solution.py:60
  88.6 4.3 collective-permute-start.13
  93.0 50.8 %collective-permute-start.14 = (f32[16,4,480]{2,1,0:T(4,128)S(1)}, f32[16,4,480]{2,1,0:T(4,128)S(1)}, u32[]{:S(2)}, u32[]{:S(2)}) collective-permute-start(f32[16,4,480]{2,1,0:T(4,128)S(1)} %maximum_select_fusion.2), channel_id=1, source_target_pairs={{0,64},{4,68},{8,72},{12,76},{16,80},{20,84},{24,88},{28,92},{32,9... | collective-permute-start | bytes 368648 | tf_op jit(solution)/shard_map/ppermute | solution.py:60
  170.9 5.9 %copy-start.1 = (f32[1600,128]{1,0:T(8,128)S(1)}, f32[1600,128]{1,0:T(8,128)}, u32[]{:S(2)}) copy-start(f32[1600,128]{1,0:T(8,128)} %copy-done) | copy-start | bytes 2457604
  183.3 7.7 %copy-start.77 = (f32[6]{0:T(128)}, f32[6]{0:T(128)S(1)}, u32[]{:S(2)}) copy-start(f32[6]{0:T(128)S(1)} %get-tuple-element.210) | copy-start | bytes 76
  194.6 7.6 %copy-start.3 = (f32[1600,128]{1,0:T(8,128)S(1)}, f32[1600,128]{1,0:T(8,128)}, u32[]{:S(2)}) copy-start(f32[1600,128]{1,0:T(8,128)} %copy-done) | copy-start | bytes 2457604
  197.4 7.5 %copy-start.82 = (f32[6]{0:T(128)}, f32[6]{0:T(128)S(1)}, u32[]{:S(2)}) copy-start(f32[6]{0:T(128)S(1)} %get-tuple-element.207) | copy-start | bytes 76
  208.5 7.6 %copy-start.4 = (f32[1600,128]{1,0:T(8,128)S(1)}, f32[1600,128]{1,0:T(8,128)}, u32[]{:S(2)}) copy-start(f32[1600,128]{1,0:T(8,128)} %copy-done) | copy-start | bytes 2457604
  211.3 7.9 %copy-start.88 = (f32[6]{0:T(128)}, f32[6]{0:T(128)S(1)}, u32[]{:S(2)}) copy-start(f32[6]{0:T(128)S(1)} %get-tuple-element.205) | copy-start | bytes 76
  222.6 7.6 %copy-start.5 = (f32[1600,128]{1,0:T(8,128)S(1)}, f32[1600,128]{1,0:T(8,128)}, u32[]{:S(2)}) copy-start(f32[1600,128]{1,0:T(8,128)} %copy-done) | copy-start | bytes 2457604
  225.4 7.5 %copy-start.92 = (f32[6]{0:T(128)}, f32[6]{0:T(128)S(1)}, u32[]{:S(2)}) copy-start(f32[6]{0:T(128)S(1)} %get-tuple-element.203) | copy-start | bytes 76
  236.4 7.6 %copy-start.6 = (f32[1600,128]{1,0:T(8,128)S(1)}, f32[1600,128]{1,0:T(8,128)}, u32[]{:S(2)}) copy-start(f32[1600,128]{1,0:T(8,128)} %copy-done) | copy-start | bytes 2457604
  239.2 7.7 %copy-start.96 = (f32[6]{0:T(128)}, f32[6]{0:T(128)S(1)}, u32[]{:S(2)}) copy-start(f32[6]{0:T(128)S(1)} %get-tuple-element.201) | copy-start | bytes 76
  263.5 8.0 %copy-start.20 = (f32[6,2,128,128]{3,2,1,0:T(8,128)}, f32[6,2,128,128]{3,2,1,0:T(8,128)S(1)}, u32[]{:S(2)}) copy-start(f32[6,2,128,128]{3,2,1,0:T(8,128)S(1)} %slice_add_fusion.1) | copy-start | bytes 2359300
  263.6 8.0 %collective-permute-start.15 = (f32[6,2,17,128]{3,2,1,0:T(8,128)S(1)}, f32[6,2,17,128]{3,2,1,0:T(8,128)S(1)}, u32[]{:S(2)}, u32[]{:S(2)}) collective-permute-start(f32[6,2,17,128]{3,2,1,0:T(8,128)S(1)} %get-tuple-element.135), channel_id=1, source_target_pairs={{0,4},{4,8},{8,12},{12,16},{16,20},{20,24},{24,28},{28,32},{32,36}... | collective-permute-start | bytes 313352 | tf_op jit(solution)/shard_map/ppermute | solution.py:28
  263.6 7.9 %collective-permute-start.16 = (f32[6,2,17,128]{3,2,1,0:T(8,128)S(1)}, f32[6,2,17,128]{3,2,1,0:T(8,128)S(1)}, u32[]{:S(2)}, u32[]{:S(2)}) collective-permute-start(f32[6,2,17,128]{3,2,1,0:T(8,128)S(1)} %get-tuple-element.136), channel_id=1, source_target_pairs={{4,0},{8,4},{12,8},{16,12},{20,16},{24,20},{28,24},{32,28},{36,32}... | collective-permute-start | bytes 313352 | tf_op jit(solution)/shard_map/ppermute | solution.py:30
  272.9 16.4 %copy-start.102 = (f32[162]{0:T(256)S(1)}, f32[162]{0:T(256)}, u32[]{:S(2)}) copy-start(f32[162]{0:T(256)} %copy-done.101) | copy-start | bytes 1948
  276.3 6.0 %collective-permute-start.17 = (f32[6,2,162,17]{2,1,3,0:T(2,128)S(1)}, f32[6,2,162,17]{2,1,3,0:T(2,128)}, u32[]{:S(2)}, u32[]{:S(2)}) collective-permute-start(f32[6,2,162,17]{2,1,3,0:T(2,128)S(1)} %copy.483), channel_id=1, source_target_pairs={{0,1},{1,2},{2,3},{3,0},{4,5},{5,6},{6,7},{7,4},{8,9},{9,10},{10,1... | collective-permute-start | bytes 396584 | tf_op jit(solution)/shard_map/ppermute | solution.py:28
  280.7 6.3 %collective-permute-start.18 = (f32[6,2,162,17]{2,1,3,0:T(2,128)}, f32[6,2,162,17]{2,1,3,0:T(2,128)}, u32[]{:S(2)}, u32[]{:S(2)}) collective-permute-start(f32[6,2,162,17]{2,1,3,0:T(2,128)} %copy.484), channel_id=1, source_target_pairs={{1,0},{2,1},{3,2},{0,3},{5,4},{6,5},{7,6},{4,7},{9,8},{10,9},{11,1... | collective-permute-start | bytes 396584 | tf_op jit(solution)/shard_map/ppermute | solution.py:30
  284.6 8.4 %copy-start.57 = (f32[160,160]{1,0:T(8,128)S(1)}, f32[160,160]{1,0:T(8,128)}, u32[]{:S(2)}) copy-start(f32[160,160]{1,0:T(8,128)} %copy-done.56) | copy-start | bytes 307204
  301.8 3.7 collective-permute-start.19
  305.4 5.2 %collective-permute-start.20 = (f32[2,480]{1,0:T(2,128)S(1)}, f32[2,480]{1,0:T(2,128)S(1)}, u32[]{:S(2)}, u32[]{:S(2)}) collective-permute-start(f32[2,480]{1,0:T(2,128)S(1)} %maximum_select_fusion.13), channel_id=1, source_target_pairs={{0,2},{1,3},{2,0},{3,1},{4,6},{5,7},{6,4},{7,5},{8,10},{9,11},{10,... | collective-permute-start | bytes 11528 | tf_op jit(solution)/shard_map/ppermute | solution.py:60
  310.6 1.3 collective-permute-start.21
  311.9 3.8 collective-permute-start.22
  315.7 5.5 %collective-permute-start.23 = (f32[4,4,480]{2,1,0:T(4,128)S(1)}, f32[4,4,480]{2,1,0:T(4,128)S(1)}, u32[]{:S(2)}, u32[]{:S(2)}) collective-permute-start(f32[4,4,480]{2,1,0:T(4,128)S(1)} %maximum_select_fusion.7), channel_id=1, source_target_pairs={{0,16},{4,20},{8,24},{12,28},{16,0},{20,4},{24,8},{28,12},{32,48},... | collective-permute-start | bytes 92168 | tf_op jit(solution)/shard_map/ppermute | solution.py:60
  321.3 4.5 collective-permute-start.24
  325.8 43.1 %copy-start.71 = (f32[16,4,480]{2,1,0:T(4,128)}, f32[16,4,480]{2,1,0:T(4,128)S(1)}, u32[]{:S(2)}) copy-start(f32[16,4,480]{2,1,0:T(4,128)S(1)} %maximum_select_fusion.3) | copy-start | bytes 368644
  325.8 43.1 %collective-permute-start.25 = (f32[16,4,480]{2,1,0:T(4,128)S(1)}, f32[16,4,480]{2,1,0:T(4,128)}, u32[]{:S(2)}, u32[]{:S(2)}) collective-permute-start(f32[16,4,480]{2,1,0:T(4,128)S(1)} %maximum_select_fusion.3), channel_id=1, source_target_pairs={{0,64},{4,68},{8,72},{12,76},{16,80},{20,84},{24,88},{28,92},{32,9... | collective-permute-start | bytes 368648 | tf_op jit(solution)/shard_map/ppermute | solution.py:60
  375.2 18.2 %copy-start.17 = (f32[12,40,128]{2,1,0:T(8,128)}, f32[12,40,128]{2,1,0:T(8,128)S(1)}, u32[]{:S(2)}) copy-start(f32[12,40,128]{2,1,0:T(8,128)S(1)} %copy.488) | copy-start | bytes 737284
  383.7 5.9 %copy-start.7 = (f32[1600,128]{1,0:T(8,128)S(1)}, f32[1600,128]{1,0:T(8,128)}, u32[]{:S(2)}) copy-start(f32[1600,128]{1,0:T(8,128)} %copy-done) | copy-start | bytes 2457604
  395.8 7.5 %copy-start.75 = (f32[6]{0:T(128)}, f32[6]{0:T(128)S(1)}, u32[]{:S(2)}) copy-start(f32[6]{0:T(128)S(1)} %get-tuple-element.196) | copy-start | bytes 76
  406.0 7.3 %copy-start.9 = (f32[1600,128]{1,0:T(8,128)S(1)}, f32[1600,128]{1,0:T(8,128)}, u32[]{:S(2)}) copy-start(f32[1600,128]{1,0:T(8,128)} %copy-done) | copy-start | bytes 2457604
  408.6 7.4 %copy-start.78 = (f32[6]{0:T(128)}, f32[6]{0:T(128)S(1)}, u32[]{:S(2)}) copy-start(f32[6]{0:T(128)S(1)} %get-tuple-element.193) | copy-start | bytes 76
  419.4 7.7 %copy-start.10 = (f32[1600,128]{1,0:T(8,128)S(1)}, f32[1600,128]{1,0:T(8,128)}, u32[]{:S(2)}) copy-start(f32[1600,128]{1,0:T(8,128)} %copy-done) | copy-start | bytes 2457604
  426.6 6.4 %copy-start.28 = (f32[12,40,128]{2,1,0:T(8,128)S(1)}, f32[12,40,128]{2,1,0:T(8,128)}, u32[]{:S(2)}) copy-start(f32[12,40,128]{2,1,0:T(8,128)} %get-tuple-element.50) | copy-start | bytes 737284
  433.1 7.4 %copy-start.11 = (f32[1600,128]{1,0:T(8,128)S(1)}, f32[1600,128]{1,0:T(8,128)}, u32[]{:S(2)}) copy-start(f32[1600,128]{1,0:T(8,128)} %copy-done) | copy-start | bytes 2457604
  444.5 10.9 %copy-start.25 = (f32[12,40,128]{2,1,0:T(8,128)}, f32[12,40,128]{2,1,0:T(8,128)S(1)}, u32[]{:S(2)}) copy-start(f32[12,40,128]{2,1,0:T(8,128)S(1)} %get-tuple-element.38) | copy-start | bytes 737284
  445.8 7.3 %copy-start.12 = (f32[1600,128]{1,0:T(8,128)S(1)}, f32[1600,128]{1,0:T(8,128)}, u32[]{:S(2)}) copy-start(f32[1600,128]{1,0:T(8,128)} %copy-done) | copy-start | bytes 2457604
  452.9 7.3 %copy-start.76 = (f32[6]{0:T(128)S(1)}, f32[6]{0:T(128)}, u32[]{:S(2)}) copy-start(f32[6]{0:T(128)} %copy-done.75) | copy-start | bytes 76
  452.9 7.3 %copy-start.79 = (f32[6]{0:T(128)S(1)}, f32[6]{0:T(128)}, u32[]{:S(2)}) copy-start(f32[6]{0:T(128)} %copy-done.78) | copy-start | bytes 76
  452.9 7.3 %copy-start.81 = (f32[6]{0:T(128)S(1)}, f32[6]{0:T(128)}, u32[]{:S(2)}) copy-start(f32[6]{0:T(128)} %copy-done.80) | copy-start | bytes 76
  452.9 7.3 %copy-start.85 = (f32[6]{0:T(128)S(1)}, f32[6]{0:T(128)}, u32[]{:S(2)}) copy-start(f32[6]{0:T(128)} %copy-done.84) | copy-start | bytes 76
  453.2 7.0 %copy-start.87 = (f32[6]{0:T(128)S(1)}, f32[6]{0:T(128)}, u32[]{:S(2)}) copy-start(f32[6]{0:T(128)} %copy-done.86) | copy-start | bytes 76
  456.1 7.8 %copy-start.16 = (f32[40,128,128]{2,1,0:T(8,128)S(1)}, f32[40,128,128]{2,1,0:T(8,128)}, u32[]{:S(2)}) copy-start(f32[40,128,128]{2,1,0:T(8,128)} %param.8) | copy-start | bytes 7864324
  456.1 7.8 %copy-start.100 = (f32[40]{0:T(128)S(1)}, f32[40]{0:T(128)}, u32[]{:S(2)}) copy-start(f32[40]{0:T(128)} %copy-done.98) | copy-start | bytes 484
  457.6 9.5 %copy-start.21 = (f32[6,2,128,128]{3,2,1,0:T(8,128)S(1)}, f32[6,2,128,128]{3,2,1,0:T(8,128)}, u32[]{:S(2)}) copy-start(f32[6,2,128,128]{3,2,1,0:T(8,128)} %copy-done.20) | copy-start | bytes 2359300
  (66 other events, 138.4 us)
Sparse Core Ops, SparseCore 0:
  60.2 66.7 all-gather.2

commit v9 on v8

--- a/solution.py
+++ b/solution.py
@@ -248,7 +248,13 @@
     )
     tile_total = gx_count * gy_count
     gathered_blocks = lax.all_gather(block_set.reshape(1, -1), ("gx", "gy"), axis=0, tiled=True)
-    all_blocks = gathered_blocks.T.reshape(block_set.shape + (tile_total,))
+    all_blocks = lax.dot_general(
+        gathered_blocks,
+        jnp.eye(tile_total, dtype=jnp.float32),
+        (((0,), (0,)), ((), ())),
+        precision=highest,
+        preferred_element_type=jnp.float32,
+    ).reshape(block_set.shape + (tile_total,))
 
     tile_ids = jnp.arange(tile_total)
     movers = [

time: 486 us -> 478 us (0.984)
  local copies, waits for them, and re-layouts: 92.3 us -> 78.5 us
  matrix products: 41.4 us -> 48 us
    all_gather x1 -> x0, local copies, waits for them, and re-layouts: 11.1 us -> none  [body(): lax.all_gather(block_set.reshape(1, -1), ('gx', 'gy'), axis=0, tiled=True)]
    dot_general x0 -> x1, matrix products: none -> 6.48 us  [body(): lax.dot_general(gathered_blocks, jnp.eye(tile_total, dtype=jnp.float32),...]
  transfers between devices with their start and end apart: 27 -> 27, of which waited for: 15 -> 15; matrix products, arithmetic and copies ran while one was open for 14% -> 14% of each run, Pallas kernels for 16% -> 17%
where the time goes in v9:
time: 478 us; the launch traced here: 469 us
  other arithmetic  171 us (36%)
  local copies, waits for them, and re-layouts  78.5 us (16%)
  Pallas kernels  78.2 us (16%)
  waiting for transfers between devices  48.2 us (10%)
  matrix products  48 us (10%)
  starting transfers between devices  27.5 us (6%)
  between operations  17.2 us (4%)
    pallas_call x2, Pallas kernels, local_solve(): pl.pallas_call(sweep_kernel, out_shape=jax.ShapeDtypeStruct(residual.shap...  78.2 us
    reduce_sum x83, other arithmetic, coarse_image(): term = jnp.sum(block[None, :, :, :] * vectors[:, :, None, :], axis=1)  75.2 us
    ppermute x14, waiting for transfers between devices, tree_gather(): other = lax.ppermute(values, axis, [(i, i ^ stride) for i in range(count)])  41.5 us
    reduce_sum x14, other arithmetic, body(): jnp.sum(image_halves[:, 0] * search_halves[:, 0] + image_halves[:, 1] * s...  23.9 us
    reduce_sum x28, other arithmetic, body(): squares = jnp.sum(image_halves * image_halves, axis=(1, 2, 3))  19.9 us
    unnamed x211, local copies, waits for them, and re-layouts  17.1 us
    dot_general x56, matrix products, coarse_image(): lax.dot_general(flat, mover, (((1,), (0,)), ((), ())), precision=highest,...  17 us
    neg x14, other arithmetic, coarse_image(): -halves[:, 1]  13.8 us
  transfers between devices with their start and end apart: 27, of which 15 were waited for; matrix products, arithmetic and copies ran while one was open for 14% of the time, Pallas kernels for 17%

profile of v9, /device:TPU:16, one launch (start us, length us, event | category | flops | bytes accessed | tf_op | source)
XLA Modules:
  0.0 468.9 jit_solution(15261488624372015263)
XLA Ops:
  8.6 5.7 %collective-permute-start.1 = (f32[14,17,128]{2,1,0:T(8,128)S(1)}, f32[14,17,128]{2,1,0:T(8,128)S(1)}, u32[]{:S(2)}, u32[]{:S(2)}) collective-permute-start(f32[14,17,128]{2,1,0:T(8,128)S(1)} %get-tuple-element.134), channel_id=1, source_target_pairs={{4,0},{8,4},{12,8},{16,12},{20,16},{24,20},{28,24},{32,28},{36,32}... | collective-permute-start | bytes 365576 | tf_op jit(solution)/shard_map/ppermute | solution.py:30
  15.0 3.3 copy_multiply_fusion
  21.5 2.6 copy.412
  25.5 2.6 copy.413
  28.9 3.1 fusion.495
  32.0 3.1 copy.417
  35.6 3.1 copy.418
  38.7 1.9 collective-permute-start.7
  40.5 2.4 copy.414
  42.9 2.5 copy.415
  45.4 2.8 maximum_multiply_fusion
  49.9 3.2 fusion.42
  57.1 2.2 fusion.47
  60.1 2.2 slice.424
  64.7 3.9 fusion.18
  68.7 2.6 collective-permute-start.8
  74.0 4.0 collective-permute-done.9
  79.5 3.7 collective-permute-done.11
  83.4 5.3 %collective-permute-done.12 = f32[4,4,480]{2,1,0:T(4,128)S(1)} collective-permute-done((f32[4,4,480]{2,1,0:T(4,128)S(1)}, f32[4,4,480]{2,1,0:T(4,128)S(1)}, u32[]{:S(2)}, u32[]{:S(2)}) %collective-permute-start.12) | collective-permute-done | bytes 30752 | tf_op jit(solution)/shard_map/ppermute | solution.py:60
  88.8 4.2 collective-permute-done.13
  93.1 1.9 collective-permute-start.14
  95.0 2.1 add_divide_fusion
  97.1 3.0 pad.40.resid_ref
  104.8 38.9 %shard_map.55 = f32[6,2,160,256]{3,2,1,0:T(8,128)} custom-call(f32[6,2,160,256]{3,2,1,0:T(8,128)} %pad.40.resid_ref, f32[160,256]{1,0:T(8,128)} %pad.41.north_ref, f32[160,256]{1,0:T(8,128)} %pad.42.south_ref, f32[160,256]{1,0:T(8,128)} %pad.43.east_ref, f32[160,256]{1,0:T(8,128)} %pad.44.west_ref, f32[160,256]{1,0:T(8,128)} %pad.45.diag_ref, ...), custom_call_target="tpu_custom_call" | custom-call | tf_op jit(solution)/shard_map/pallas_call | solution.py:144
  150.2 6.5 %fusion = f32[9600,128]{1,0:T(8,128)S(1)} fusion(f32[128,1,9600]{2,1,0:T(1,128)} %all-gather.3.cloned.1.call-done), kind=kOutput, calls=%fused_computation.88 | convolution fusion | flops 1887453184 | bytes 9830400 | tf_op jit(solution)/shard_map/dot_general | solution.py:251
  160.7 2.1 multiply_reduce_fusion.78
  167.1 1.9 multiply_reduce_fusion.77
  178.4 1.9 multiply_reduce_fusion.71
  187.3 2.1 fusion.176
  192.2 1.9 multiply_reduce_fusion.65
  200.9 2.1 fusion.164
  205.8 1.9 multiply_reduce_fusion.59
  215.0 2.1 fusion.150
  228.5 2.1 fusion.247
  233.4 1.9 multiply_reduce_fusion.47
  248.8 4.9 %fusion.21 = f32[6,2,128,128]{3,0,2,1:T(8,128)S(1)} fusion(f32[6,2,40,1]{2,1,0,3:T(2,128)S(1)} %bitcast.1562, f32[40]{0:T(128)} %copy-done.98, f32[40,128,128]{2,1,0:T(8,128)} %param.8), kind=kOutput, calls=%fused_computation.107 | convolution fusion | flops 95027200 | bytes 3409952 | tf_op jit(solution)/shard_map/dot_general | solution.py:209
  255.5 5.1 %collective-permute-start.16 = (f32[6,2,17,128]{3,2,1,0:T(8,128)S(1)}, f32[6,2,17,128]{3,2,1,0:T(8,128)S(1)}, u32[]{:S(2)}, u32[]{:S(2)}) collective-permute-start(f32[6,2,17,128]{3,2,1,0:T(8,128)S(1)} %get-tuple-element.136), channel_id=1, source_target_pairs={{4,0},{8,4},{12,8},{16,12},{20,16},{24,20},{28,24},{32,28},{36,32}... | collective-permute-start | bytes 313352 | tf_op jit(solution)/shard_map/ppermute | solution.py:30
  260.6 2.8 collective-permute-done.15
  268.2 2.1 collective-permute-start.17
  270.2 2.4 copy.474
  274.1 2.3 copy.475
  276.4 2.5 collective-permute-done.18
  278.9 2.3 copy.476
  281.3 2.9 maximum_multiply_fusion.1
  284.9 2.2 fusion.31
  290.1 3.5 fusion.16
  295.2 2.2 collective-permute-done.19
  297.5 5.1 %collective-permute-done.20 = f32[2,480]{1,0:T(2,128)S(1)} collective-permute-done((f32[2,480]{1,0:T(2,128)S(1)}, f32[2,480]{1,0:T(2,128)S(1)}, u32[]{:S(2)}, u32[]{:S(2)}) %collective-permute-start.20) | collective-permute-done | bytes 3872 | tf_op jit(solution)/shard_map/ppermute | solution.py:60
  303.9 3.7 collective-permute-done.22
  307.7 5.4 %collective-permute-done.23 = f32[4,4,480]{2,1,0:T(4,128)S(1)} collective-permute-done((f32[4,4,480]{2,1,0:T(4,128)S(1)}, f32[4,4,480]{2,1,0:T(4,128)S(1)}, u32[]{:S(2)}, u32[]{:S(2)}) %collective-permute-start.23) | collective-permute-done | bytes 30752 | tf_op jit(solution)/shard_map/ppermute | solution.py:60
  313.8 4.1 collective-permute-done.24
  318.7 3.0 pad.49.resid_ref
  321.6 39.3 %shard_map.56 = f32[6,2,160,256]{3,2,1,0:T(8,128)} custom-call(f32[6,2,160,256]{3,2,1,0:T(8,128)} %pad.49.resid_ref, f32[160,256]{1,0:T(8,128)} %pad.41.north_ref, f32[160,256]{1,0:T(8,128)} %pad.42.south_ref, f32[160,256]{1,0:T(8,128)} %pad.43.east_ref, f32[160,256]{1,0:T(8,128)} %pad.44.west_ref, f32[160,256]{1,0:T(8,128)} %pad.45.diag_ref, ...), custom_call_target="tpu_custom_call" | custom-call | tf_op jit(solution)/shard_map/pallas_call | solution.py:144
  362.1 2.5 select_n.386
  364.6 2.5 copy.478
  370.0 1.9 multiply_reduce_fusion.40
  378.9 1.9 multiply_reduce_fusion.35
  398.0 2.0 fusion.87
  411.4 2.0 fusion.75
  416.2 2.1 multiply_reduce_fusion.17
  425.0 2.0 fusion.61
  437.8 2.0 fusion.239
  455.9 3.2 fusion.20
  459.1 2.6 fusion.58
  (560 shorter events, 194.9 us)
Async XLA Ops:
  6.5 13.1 %copy-start.55 = (f32[128,128]{1,0:T(8,128)S(1)}, f32[128,128]{1,0:T(8,128)}, u32[]{:S(2)}) copy-start(f32[128,128]{1,0:T(8,128)} %param.6) | copy-start | bytes 196612
  6.5 13.1 %copy-start.24 = (f32[6,2,128,128]{3,2,1,0:T(8,128)S(1)}, f32[6,2,128,128]{3,2,1,0:T(8,128)}, u32[]{:S(2)}) copy-start(f32[6,2,128,128]{3,2,1,0:T(8,128)} %param.5) | copy-start | bytes 2359300
  6.5 143.7 %all-gather.3.cloned.1.call-start = ((), (), s32[]{:S(2)}) async-start(), calls=%async_computation | async-start | bytes 4953600 | tf_op jit(solution)/shard_map/all_gather | solution.py:250
  8.5 11.1 %collective-permute-start = (f32[14,17,128]{2,1,0:T(8,128)S(1)}, f32[14,17,128]{2,1,0:T(8,128)S(1)}, u32[]{:S(2)}, u32[]{:S(2)}) collective-permute-start(f32[14,17,128]{2,1,0:T(8,128)S(1)} %get-tuple-element.133), channel_id=1, source_target_pairs={{0,4},{4,8},{8,12},{12,16},{16,20},{20,24},{24,28},{28,32},{32,36}... | collective-permute-start | bytes 365576 | tf_op jit(solution)/shard_map/ppermute | solution.py:28
  8.6 11.0 %collective-permute-start.1 = (f32[14,17,128]{2,1,0:T(8,128)S(1)}, f32[14,17,128]{2,1,0:T(8,128)S(1)}, u32[]{:S(2)}, u32[]{:S(2)}) collective-permute-start(f32[14,17,128]{2,1,0:T(8,128)S(1)} %get-tuple-element.134), channel_id=1, source_target_pairs={{4,0},{8,4},{12,8},{16,12},{20,16},{24,20},{28,24},{32,28},{36,32}... | collective-permute-start | bytes 365576 | tf_op jit(solution)/shard_map/ppermute | solution.py:30
  15.0 49.6 %copy-start.98 = (f32[40]{0:T(128)}, f32[40]{0:T(128)S(1)}, u32[]{:S(2)}) copy-start(f32[40]{0:T(128)S(1)} %compare_convert_fusion) | copy-start | bytes 484
  18.9 34.3 %collective-permute-start.4 = (f32[40,128]{1,0:T(8,128)}, f32[40,128]{1,0:T(8,128)}, u32[]{:S(2)}, u32[]{:S(2)}) collective-permute-start(f32[40,128]{1,0:T(8,128)} %get-tuple-element.126), channel_id=1, source_target_pairs={{4,0},{8,4},{12,8},{16,12},{20,16},{24,20},{28,24},{32,28},{36,32}... | collective-permute-start | bytes 61448 | tf_op jit(solution)/shard_map/ppermute | solution.py:227
  19.6 34.5 %collective-permute-start.5 = (f32[40,128]{1,0:T(8,128)}, f32[40,128]{1,0:T(8,128)}, u32[]{:S(2)}, u32[]{:S(2)}) collective-permute-start(f32[40,128]{1,0:T(8,128)} %get-tuple-element.125), channel_id=1, source_target_pairs={{0,4},{4,8},{8,12},{12,16},{16,20},{20,24},{24,28},{28,32},{32,36}... | collective-permute-start | bytes 61448 | tf_op jit(solution)/shard_map/ppermute | solution.py:228
  24.2 14.5 %collective-permute-start.2 = (f32[14,162,17]{1,0,2:T(8,128)}, f32[14,162,17]{1,0,2:T(8,128)}, u32[]{:S(2)}, u32[]{:S(2)}) collective-permute-start(f32[14,162,17]{1,0,2:T(8,128)} %copy.412), channel_id=1, source_target_pairs={{0,1},{1,2},{2,3},{3,0},{4,5},{5,6},{6,7},{7,4},{8,9},{9,10},{10,1... | collective-permute-start | bytes 462680 | tf_op jit(solution)/shard_map/ppermute | solution.py:28
  28.1 14.8 %collective-permute-start.3 = (f32[14,162,17]{1,0,2:T(8,128)}, f32[14,162,17]{1,0,2:T(8,128)}, u32[]{:S(2)}, u32[]{:S(2)}) collective-permute-start(f32[14,162,17]{1,0,2:T(8,128)} %copy.413), channel_id=1, source_target_pairs={{1,0},{2,1},{3,2},{0,3},{5,4},{6,5},{7,6},{4,7},{9,8},{10,9},{11,1... | collective-permute-start | bytes 462680 | tf_op jit(solution)/shard_map/ppermute | solution.py:30
  35.1 20.1 %collective-permute-start.6 = (f32[40,128]{1,0:T(8,128)}, f32[40,128]{1,0:T(8,128)}, u32[]{:S(2)}, u32[]{:S(2)}) collective-permute-start(f32[40,128]{1,0:T(8,128)} %bitcast.1559), channel_id=1, source_target_pairs={{1,0},{2,1},{3,2},{0,3},{5,4},{6,5},{7,6},{4,7},{9,8},{10,9},{11,1... | collective-permute-start | bytes 61448 | tf_op jit(solution)/shard_map/ppermute | solution.py:229
  38.7 11.2 %copy-start.101 = (f32[162]{0:T(256)}, f32[162]{0:T(256)S(1)}, u32[]{:S(2)}) copy-start(f32[162]{0:T(256)S(1)} %and_convert_fusion) | copy-start | bytes 1948
  38.7 17.5 %collective-permute-start.7 = (f32[40,128]{1,0:T(8,128)}, f32[40,128]{1,0:T(8,128)}, u32[]{:S(2)}, u32[]{:S(2)}) collective-permute-start(f32[40,128]{1,0:T(8,128)} %bitcast.1560), channel_id=1, source_target_pairs={{0,1},{1,2},{2,3},{3,0},{4,5},{5,6},{6,7},{7,4},{8,9},{9,10},{10,1... | collective-permute-start | bytes 61448 | tf_op jit(solution)/shard_map/ppermute | solution.py:230
  49.9 6.3 %copy-start.73 = (f32[40,128,1]{1,0,2:T(8,128)S(1)}, f32[40,128,1]{1,0,2:T(8,128)}, u32[]{:S(2)}) copy-start(f32[40,128,1]{1,0,2:T(8,128)} %copy.417) | copy-start | bytes 61444
  68.7 4.1 collective-permute-start.8
  72.9 5.2 %collective-permute-start.9 = (f32[2,480]{1,0:T(2,128)S(1)}, f32[2,480]{1,0:T(2,128)S(1)}, u32[]{:S(2)}, u32[]{:S(2)}) collective-permute-start(f32[2,480]{1,0:T(2,128)S(1)} %maximum_select_fusion.12), channel_id=1, source_target_pairs={{0,2},{1,3},{2,0},{3,1},{4,6},{5,7},{6,4},{7,5},{8,10},{9,11},{10,... | collective-permute-start | bytes 11528 | tf_op jit(solution)/shard_map/ppermute | solution.py:60
  78.1 1.3 collective-permute-start.10
  79.3 3.8 collective-permute-start.11
  83.2 5.5 %collective-permute-start.12 = (f32[4,4,480]{2,1,0:T(4,128)S(1)}, f32[4,4,480]{2,1,0:T(4,128)S(1)}, u32[]{:S(2)}, u32[]{:S(2)}) collective-permute-start(f32[4,4,480]{2,1,0:T(4,128)S(1)} %maximum_select_fusion.6), channel_id=1, source_target_pairs={{0,16},{4,20},{8,24},{12,28},{16,0},{20,4},{24,8},{28,12},{32,48},... | collective-permute-start | bytes 92168 | tf_op jit(solution)/shard_map/ppermute | solution.py:60
  88.7 4.3 collective-permute-start.13
  93.1 50.7 %collective-permute-start.14 = (f32[16,4,480]{2,1,0:T(4,128)S(1)}, f32[16,4,480]{2,1,0:T(4,128)S(1)}, u32[]{:S(2)}, u32[]{:S(2)}) collective-permute-start(f32[16,4,480]{2,1,0:T(4,128)S(1)} %maximum_select_fusion.2), channel_id=1, source_target_pairs={{0,64},{4,68},{8,72},{12,76},{16,80},{20,84},{24,88},{28,92},{32,9... | collective-permute-start | bytes 368648 | tf_op jit(solution)/shard_map/ppermute | solution.py:60
  163.8 5.9 %copy-start.1 = (f32[1600,128]{1,0:T(8,128)S(1)}, f32[1600,128]{1,0:T(8,128)}, u32[]{:S(2)}) copy-start(f32[1600,128]{1,0:T(8,128)} %copy-done) | copy-start | bytes 2457604
  176.2 7.8 %copy-start.77 = (f32[6]{0:T(128)}, f32[6]{0:T(128)S(1)}, u32[]{:S(2)}) copy-start(f32[6]{0:T(128)S(1)} %get-tuple-element.210) | copy-start | bytes 76
  187.3 7.5 %copy-start.3 = (f32[1600,128]{1,0:T(8,128)S(1)}, f32[1600,128]{1,0:T(8,128)}, u32[]{:S(2)}) copy-start(f32[1600,128]{1,0:T(8,128)} %copy-done) | copy-start | bytes 2457604
  190.0 7.5 %copy-start.82 = (f32[6]{0:T(128)}, f32[6]{0:T(128)S(1)}, u32[]{:S(2)}) copy-start(f32[6]{0:T(128)S(1)} %get-tuple-element.207) | copy-start | bytes 76
  200.9 7.5 %copy-start.4 = (f32[1600,128]{1,0:T(8,128)S(1)}, f32[1600,128]{1,0:T(8,128)}, u32[]{:S(2)}) copy-start(f32[1600,128]{1,0:T(8,128)} %copy-done) | copy-start | bytes 2457604
  203.6 7.9 %copy-start.88 = (f32[6]{0:T(128)}, f32[6]{0:T(128)S(1)}, u32[]{:S(2)}) copy-start(f32[6]{0:T(128)S(1)} %get-tuple-element.205) | copy-start | bytes 76
  215.0 7.6 %copy-start.5 = (f32[1600,128]{1,0:T(8,128)S(1)}, f32[1600,128]{1,0:T(8,128)}, u32[]{:S(2)}) copy-start(f32[1600,128]{1,0:T(8,128)} %copy-done) | copy-start | bytes 2457604
  217.8 7.5 %copy-start.92 = (f32[6]{0:T(128)}, f32[6]{0:T(128)S(1)}, u32[]{:S(2)}) copy-start(f32[6]{0:T(128)S(1)} %get-tuple-element.203) | copy-start | bytes 76
  228.5 7.5 %copy-start.6 = (f32[1600,128]{1,0:T(8,128)S(1)}, f32[1600,128]{1,0:T(8,128)}, u32[]{:S(2)}) copy-start(f32[1600,128]{1,0:T(8,128)} %copy-done) | copy-start | bytes 2457604
  231.2 7.7 %copy-start.96 = (f32[6]{0:T(128)}, f32[6]{0:T(128)S(1)}, u32[]{:S(2)}) copy-start(f32[6]{0:T(128)S(1)} %get-tuple-element.201) | copy-start | bytes 76
  255.4 8.0 %copy-start.20 = (f32[6,2,128,128]{3,2,1,0:T(8,128)}, f32[6,2,128,128]{3,2,1,0:T(8,128)S(1)}, u32[]{:S(2)}) copy-start(f32[6,2,128,128]{3,2,1,0:T(8,128)S(1)} %slice_add_fusion.1) | copy-start | bytes 2359300
  255.4 8.0 %collective-permute-start.15 = (f32[6,2,17,128]{3,2,1,0:T(8,128)S(1)}, f32[6,2,17,128]{3,2,1,0:T(8,128)S(1)}, u32[]{:S(2)}, u32[]{:S(2)}) collective-permute-start(f32[6,2,17,128]{3,2,1,0:T(8,128)S(1)} %get-tuple-element.135), channel_id=1, source_target_pairs={{0,4},{4,8},{8,12},{12,16},{16,20},{20,24},{24,28},{28,32},{32,36}... | collective-permute-start | bytes 313352 | tf_op jit(solution)/shard_map/ppermute | solution.py:28
  255.5 7.9 %collective-permute-start.16 = (f32[6,2,17,128]{3,2,1,0:T(8,128)S(1)}, f32[6,2,17,128]{3,2,1,0:T(8,128)S(1)}, u32[]{:S(2)}, u32[]{:S(2)}) collective-permute-start(f32[6,2,17,128]{3,2,1,0:T(8,128)S(1)} %get-tuple-element.136), channel_id=1, source_target_pairs={{4,0},{8,4},{12,8},{16,12},{20,16},{24,20},{28,24},{32,28},{36,32}... | collective-permute-start | bytes 313352 | tf_op jit(solution)/shard_map/ppermute | solution.py:30
  264.8 16.4 %copy-start.102 = (f32[162]{0:T(256)S(1)}, f32[162]{0:T(256)}, u32[]{:S(2)}) copy-start(f32[162]{0:T(256)} %copy-done.101) | copy-start | bytes 1948
  268.2 6.0 %collective-permute-start.17 = (f32[6,2,162,17]{2,1,3,0:T(2,128)S(1)}, f32[6,2,162,17]{2,1,3,0:T(2,128)}, u32[]{:S(2)}, u32[]{:S(2)}) collective-permute-start(f32[6,2,162,17]{2,1,3,0:T(2,128)S(1)} %copy.473), channel_id=1, source_target_pairs={{0,1},{1,2},{2,3},{3,0},{4,5},{5,6},{6,7},{7,4},{8,9},{9,10},{10,1... | collective-permute-start | bytes 396584 | tf_op jit(solution)/shard_map/ppermute | solution.py:28
  272.6 6.3 %collective-permute-start.18 = (f32[6,2,162,17]{2,1,3,0:T(2,128)}, f32[6,2,162,17]{2,1,3,0:T(2,128)}, u32[]{:S(2)}, u32[]{:S(2)}) collective-permute-start(f32[6,2,162,17]{2,1,3,0:T(2,128)} %copy.474), channel_id=1, source_target_pairs={{1,0},{2,1},{3,2},{0,3},{5,4},{6,5},{7,6},{4,7},{9,8},{10,9},{11,1... | collective-permute-start | bytes 396584 | tf_op jit(solution)/shard_map/ppermute | solution.py:30
  276.4 8.4 %copy-start.57 = (f32[160,160]{1,0:T(8,128)S(1)}, f32[160,160]{1,0:T(8,128)}, u32[]{:S(2)}) copy-start(f32[160,160]{1,0:T(8,128)} %copy-done.56) | copy-start | bytes 307204
  293.7 3.7 collective-permute-start.19
  297.3 5.2 %collective-permute-start.20 = (f32[2,480]{1,0:T(2,128)S(1)}, f32[2,480]{1,0:T(2,128)S(1)}, u32[]{:S(2)}, u32[]{:S(2)}) collective-permute-start(f32[2,480]{1,0:T(2,128)S(1)} %maximum_select_fusion.13), channel_id=1, source_target_pairs={{0,2},{1,3},{2,0},{3,1},{4,6},{5,7},{6,4},{7,5},{8,10},{9,11},{10,... | collective-permute-start | bytes 11528 | tf_op jit(solution)/shard_map/ppermute | solution.py:60
  302.5 1.3 collective-permute-start.21
  303.8 3.8 collective-permute-start.22
  307.6 5.5 %collective-permute-start.23 = (f32[4,4,480]{2,1,0:T(4,128)S(1)}, f32[4,4,480]{2,1,0:T(4,128)S(1)}, u32[]{:S(2)}, u32[]{:S(2)}) collective-permute-start(f32[4,4,480]{2,1,0:T(4,128)S(1)} %maximum_select_fusion.7), channel_id=1, source_target_pairs={{0,16},{4,20},{8,24},{12,28},{16,0},{20,4},{24,8},{28,12},{32,48},... | collective-permute-start | bytes 92168 | tf_op jit(solution)/shard_map/ppermute | solution.py:60
  313.2 4.7 collective-permute-start.24
  317.9 43.0 %copy-start.71 = (f32[16,4,480]{2,1,0:T(4,128)}, f32[16,4,480]{2,1,0:T(4,128)S(1)}, u32[]{:S(2)}) copy-start(f32[16,4,480]{2,1,0:T(4,128)S(1)} %maximum_select_fusion.3) | copy-start | bytes 368644
  317.9 43.0 %collective-permute-start.25 = (f32[16,4,480]{2,1,0:T(4,128)S(1)}, f32[16,4,480]{2,1,0:T(4,128)}, u32[]{:S(2)}, u32[]{:S(2)}) collective-permute-start(f32[16,4,480]{2,1,0:T(4,128)S(1)} %maximum_select_fusion.3), channel_id=1, source_target_pairs={{0,64},{4,68},{8,72},{12,76},{16,80},{20,84},{24,88},{28,92},{32,9... | collective-permute-start | bytes 368648 | tf_op jit(solution)/shard_map/ppermute | solution.py:60
  367.1 18.2 %copy-start.17 = (f32[12,40,128]{2,1,0:T(8,128)}, f32[12,40,128]{2,1,0:T(8,128)S(1)}, u32[]{:S(2)}) copy-start(f32[12,40,128]{2,1,0:T(8,128)S(1)} %copy.478) | copy-start | bytes 737284
  375.6 5.9 %copy-start.7 = (f32[1600,128]{1,0:T(8,128)S(1)}, f32[1600,128]{1,0:T(8,128)}, u32[]{:S(2)}) copy-start(f32[1600,128]{1,0:T(8,128)} %copy-done) | copy-start | bytes 2457604
  387.7 7.5 %copy-start.75 = (f32[6]{0:T(128)}, f32[6]{0:T(128)S(1)}, u32[]{:S(2)}) copy-start(f32[6]{0:T(128)S(1)} %get-tuple-element.196) | copy-start | bytes 76
  398.0 7.3 %copy-start.9 = (f32[1600,128]{1,0:T(8,128)S(1)}, f32[1600,128]{1,0:T(8,128)}, u32[]{:S(2)}) copy-start(f32[1600,128]{1,0:T(8,128)} %copy-done) | copy-start | bytes 2457604
  400.6 7.4 %copy-start.78 = (f32[6]{0:T(128)}, f32[6]{0:T(128)S(1)}, u32[]{:S(2)}) copy-start(f32[6]{0:T(128)S(1)} %get-tuple-element.193) | copy-start | bytes 76
  411.4 7.7 %copy-start.10 = (f32[1600,128]{1,0:T(8,128)S(1)}, f32[1600,128]{1,0:T(8,128)}, u32[]{:S(2)}) copy-start(f32[1600,128]{1,0:T(8,128)} %copy-done) | copy-start | bytes 2457604
  418.6 6.4 %copy-start.28 = (f32[12,40,128]{2,1,0:T(8,128)S(1)}, f32[12,40,128]{2,1,0:T(8,128)}, u32[]{:S(2)}) copy-start(f32[12,40,128]{2,1,0:T(8,128)} %get-tuple-element.50) | copy-start | bytes 737284
  425.0 7.4 %copy-start.11 = (f32[1600,128]{1,0:T(8,128)S(1)}, f32[1600,128]{1,0:T(8,128)}, u32[]{:S(2)}) copy-start(f32[1600,128]{1,0:T(8,128)} %copy-done) | copy-start | bytes 2457604
  436.5 10.9 %copy-start.25 = (f32[12,40,128]{2,1,0:T(8,128)}, f32[12,40,128]{2,1,0:T(8,128)S(1)}, u32[]{:S(2)}) copy-start(f32[12,40,128]{2,1,0:T(8,128)S(1)} %get-tuple-element.38) | copy-start | bytes 737284
  437.8 7.3 %copy-start.12 = (f32[1600,128]{1,0:T(8,128)S(1)}, f32[1600,128]{1,0:T(8,128)}, u32[]{:S(2)}) copy-start(f32[1600,128]{1,0:T(8,128)} %copy-done) | copy-start | bytes 2457604
  444.8 7.3 %copy-start.76 = (f32[6]{0:T(128)S(1)}, f32[6]{0:T(128)}, u32[]{:S(2)}) copy-start(f32[6]{0:T(128)} %copy-done.75) | copy-start | bytes 76
  444.8 7.3 %copy-start.79 = (f32[6]{0:T(128)S(1)}, f32[6]{0:T(128)}, u32[]{:S(2)}) copy-start(f32[6]{0:T(128)} %copy-done.78) | copy-start | bytes 76
  444.8 7.3 %copy-start.81 = (f32[6]{0:T(128)S(1)}, f32[6]{0:T(128)}, u32[]{:S(2)}) copy-start(f32[6]{0:T(128)} %copy-done.80) | copy-start | bytes 76
  444.8 7.3 %copy-start.85 = (f32[6]{0:T(128)S(1)}, f32[6]{0:T(128)}, u32[]{:S(2)}) copy-start(f32[6]{0:T(128)} %copy-done.84) | copy-start | bytes 76
  445.1 7.0 %copy-start.87 = (f32[6]{0:T(128)S(1)}, f32[6]{0:T(128)}, u32[]{:S(2)}) copy-start(f32[6]{0:T(128)} %copy-done.86) | copy-start | bytes 76
  448.1 7.8 %copy-start.16 = (f32[40,128,128]{2,1,0:T(8,128)S(1)}, f32[40,128,128]{2,1,0:T(8,128)}, u32[]{:S(2)}) copy-start(f32[40,128,128]{2,1,0:T(8,128)} %param.8) | copy-start | bytes 7864324
  448.1 7.8 %copy-start.100 = (f32[40]{0:T(128)S(1)}, f32[40]{0:T(128)}, u32[]{:S(2)}) copy-start(f32[40]{0:T(128)} %copy-done.98) | copy-start | bytes 484
  449.5 9.5 %copy-start.21 = (f32[6,2,128,128]{3,2,1,0:T(8,128)S(1)}, f32[6,2,128,128]{3,2,1,0:T(8,128)}, u32[]{:S(2)}) copy-start(f32[6,2,128,128]{3,2,1,0:T(8,128)} %copy-done.20) | copy-start | bytes 2359300
  (66 other events, 128.8 us)
Sparse Core Ops, SparseCore 0:
  60.2 66.8 all-gather.2
